TPU v7x, 32 devices: a whole 2x2x4 slice. The times are simulated.
32 devices in a mesh: space: 16 (over z, y, core), samp: 2 (over x).
Axes of the slice: x: 2, y: 2, z: 4, core: 2. Of those that a mesh axis runs over, the one named last changes fastest.
Arguments:
- snapshots: float32 [4, 512, 32768], P(None, 'samp', 'space'), may hold values from -24 to 24
- space_basis: float32 [256, 32768], P('samp', 'space'), may hold values from -0.03314563 to 0.03314563
- sample_basis: float32 [512, 64], P('samp'), may hold values from -0.26516504 to 0.26516504
Outputs:
- deflated: float32 [4, 512, 32768], P(None, 'samp', 'space')
All inputs are finite; a program needn't handle non-finite values.
Results may differ from a plain program's by a relative error of at most 0.000078.
Values sent between devices are 32-bit elements; how exact they have to be, the bound alone decides.
No kernel may reach another device: no remote copies, remote signals or barrier semaphores. Data moves between devices by JAX's collectives and lax.ppermute only.
A program may use at most 64 MiB of HBM per device.

v0:
```python
import jax
import jax.numpy as jnp
from jax import lax
from jax.sharding import PartitionSpec as P


def shards(snapshots, space_basis, sample_basis):
    highest = lax.Precision.HIGHEST
    snap_count, local_samples, row_count = snapshots.shape
    rank_samples = sample_basis.shape[1]
    full_basis = lax.all_gather(space_basis, "samp", axis=0, tiled=True)
    rank_rows = full_basis.shape[0]
    flattened = snapshots.reshape(snap_count * local_samples, row_count)
    row_terms = lax.psum_scatter(
        lax.dot_general(
            full_basis,
            flattened,
            (((1,), (1,)), ((), ())),
            precision=highest,
            preferred_element_type=jnp.float32,
        ),
        "space",
        scatter_dimension=0,
        tiled=True,
    )
    shaped = row_terms.reshape(row_terms.shape[0], snap_count, local_samples)
    result = jnp.einsum("rts,sq->rtq", shaped, sample_basis, precision=highest)
    core_rows = lax.psum(result.reshape(row_terms.shape[0], snap_count * rank_samples), "samp")
    core_full = lax.all_gather(core_rows, "space", axis=0, tiled=True)
    core_shaped = core_full.reshape(rank_rows, snap_count, rank_samples)
    spread = jnp.einsum("rtq,sq->rts", core_shaped, sample_basis, precision=highest)
    spread = spread.reshape(rank_rows, snap_count * local_samples)
    removed = lax.dot_general(
        spread,
        full_basis,
        (((0,), (0,)), ((), ())),
        precision=highest,
        preferred_element_type=jnp.float32,
    )
    return snapshots - removed.reshape(snap_count, local_samples, row_count)


def solution(mesh):
    return jax.shard_map(
        shards,
        mesh=mesh,
        in_specs=(P(None, "samp", "space"), P("samp", "space"), P("samp", None)),
        out_specs=P(None, "samp", "space"),
        check_vma=False,
    )
```

profile of v0, /device:TPU:0, one launch (start us, length us, event | category | flops | bytes accessed | tf_op | source)
XLA Modules:
  0.0 163.0 jit_solution(13818916659689119292)
XLA Ops:
  6.5 0.0 copy-start
  6.5 0.0 all-gather.2.cloned.1.call-start
  6.5 0.7 all-gather.2.cloned.1.call-update
  7.3 0.0 reduce-scatter.2.cloned.1.call-start
  7.3 37.4 %all-gather.2.cloned.1.call-done = f32[256,2048]{1,0:T(8,128)} async-done(((f32[128,2048]{1,0:T(8,128)}), f32[256,2048]{1,0:T(8,128)}) %all-gather.2.cloned.1.call-update) | async-done | bytes 2097168 | tf_op jit(solution)/shard_map/all_gather | solution.py:11
  44.7 0.0 copy-start.1
  44.7 12.0 %fusion.6 = f32[256,1024]{1,0:T(8,128)} fusion(f32[256,2048]{1,0:T(8,128)} %all-gather.2.cloned.1.call-done, f32[1024,2048]{1,0:T(8,128)} %bitcast.24), kind=kOutput, calls=%fused_computation.8 | convolution fusion | flops 6442450944 | bytes 11534336 | tf_op jit(solution)/shard_map/dot_general | solution.py:15
  56.7 0.0 reduce-scatter.2.cloned.1.call-update
  56.7 57.8 %reduce-scatter.2.cloned.1.call-done = f32[16,1024]{1,0:T(8,128)} async-done(((f32[256,1024]{1,0:T(8,128)}), f32[16,1024]{1,0:T(8,128)}) %reduce-scatter.2.cloned.1.call-update) | async-done | bytes 65552 | tf_op jit(solution)/shard_map/reduce_scatter | solution.py:14
  114.5 0.0 copy-done
  114.5 1.0 fusion.1
  115.6 0.1 reshape.19
  115.7 8.1 %psum.7 = f32[16,256]{1,0:T(8,128)S(1)} all-reduce(f32[16,256]{1,0:T(8,128)S(1)} %reshape.19), channel_id=1, replica_groups=mesh['space'=16,'samp'=2] {'samp'}, use_global_device_ids=true, to_apply=%region_1.0 | all-reduce | flops 4096 | bytes 32768 | tf_op jit(solution)/shard_map/psum | solution.py:28
  123.8 20.0 %all_gather.7 = f32[256,256]{1,0:T(8,128)S(1)} all-gather(f32[16,256]{1,0:T(8,128)S(1)} %psum.7), channel_id=1, replica_groups=mesh['space'=16,'samp'=2] {'space'}, dimensions={0}, use_global_device_ids=true | all-gather | bytes 278528 | tf_op jit(solution)/shard_map/all_gather | solution.py:29
  143.8 0.1 copy.7
  143.9 1.0 convolution_bitcast_fusion
  145.0 0.0 copy-done.1
  145.0 11.2 %convolution_subtract_fusion = f32[4,256,2048]{2,1,0:T(8,128)} fusion(f32[4,256,2048]{2,1,0:T(8,128)} %param.3, f32[4,256,256]{2,1,0:T(8,128)S(1)} %convolution_bitcast_fusion, f32[256,2048]{1,0:T(8,128)S(1)} %copy-done.1), kind=kOutput, calls=%fused_computation | convolution fusion | flops 6444548096 | bytes 19922944 | tf_op jit(solution)/shard_map/dot_general | solution.py:33
  (1 shorter events, 0.0 us)
Async XLA Ops:
  6.5 108.0 %copy-start = (f32[256,64]{0,1:T(8,128)S(1)}, f32[256,64]{0,1:T(8,128)}, u32[]{:S(2)}) copy-start(f32[256,64]{0,1:T(8,128)} %param.5) | copy-start | bytes 196612
  6.5 38.2 %all-gather.2.cloned.1.call-start = ((), (), s32[]{:S(2)}) async-start(), calls=%async_computation.1 | async-start | bytes 3145728 | tf_op jit(solution)/shard_map/all_gather | solution.py:11
  7.3 107.2 %reduce-scatter.2.cloned.1.call-start = ((), (), s32[]{:S(2)}) async-start(), calls=%async_computation.2 | async-start | bytes 1114112 | tf_op jit(solution)/shard_map/reduce_scatter | solution.py:14
  44.7 100.2 %copy-start.1 = (f32[256,2048]{1,0:T(8,128)S(1)}, f32[256,2048]{1,0:T(8,128)}, u32[]{:S(2)}) copy-start(f32[256,2048]{1,0:T(8,128)} %all-gather.2.cloned.1.call-done) | copy-start | bytes 6291460
Sparse Core Ops, SparseCore 0:
  8.9 35.8 all-gather.1
  56.8 57.6 reduce-scatter.1
where the time goes:
time: 163 us
  waiting for transfers between devices  95.9 us (59%)
  blocking collectives  28.1 us (17%)
  matrix products  25.2 us (15%)
  between operations  13.4 us (8%)
    reduce_scatter x1, waiting for transfers between devices, shards(): lax.psum_scatter(lax.dot_general(full_basis, flattened, (((1,), (1,)), ((...  57.8 us
    all_gather x1, waiting for transfers between devices, shards(): full_basis = lax.all_gather(space_basis, 'samp', axis=0, tiled=True)  37.4 us
    all_gather x1, blocking collectives, shards(): core_full = lax.all_gather(core_rows, 'space', axis=0, tiled=True)  20 us
    dot_general x1, matrix products, shards(): lax.dot_general(full_basis, flattened, (((1,), (1,)), ((), ())), precisio...  12 us
    dot_general x1, matrix products, shards(): lax.dot_general(spread, full_basis, (((0,), (0,)), ((), ())), precision=h...  11.2 us
    psum x1, blocking collectives, shards(): lax.psum(result.reshape(row_terms.shape[0], snap_count * rank_samples), '...  8.09 us
  transfers between devices with their start and end apart: 2, of which 2 were waited for; matrix products, arithmetic and copies ran while one was open for 0% of the time, Pallas kernels for 0%

commit v1 on v0

v1 whole, which is shorter than its diff:
```python
import jax
import jax.numpy as jnp
from jax import lax
from jax.sharding import PartitionSpec as P


def swap(value, axis, size, bit):
    return lax.ppermute(value, axis, [(i, i ^ bit) for i in range(size)])


def bits(size, start=1):
    while start < size:
        yield start
        start *= 2


def solution(mesh):
    space, samp = mesh.shape["space"], mesh.shape["samp"]
    highest = lax.Precision.HIGHEST

    def dot(a, b, dims):
        return lax.dot_general(a, b, (dims, ((), ())), precision=highest, preferred_element_type=jnp.float32)

    def over_space(part):
        core = lax.axis_index("space") % 2
        half = part.shape[-2] // 2
        low, high = part[..., :half, :], part[..., half:, :]
        mine = jnp.where(core == 0, low, high)
        total = mine + swap(jnp.where(core == 0, high, low), "space", space, 1)
        for bit in bits(space, 2):
            total = total + swap(total, "space", space, bit)
        return total

    def shards(snapshots, space_basis, sample_basis):
        snaps, samples, columns = snapshots.shape
        rank = sample_basis.shape[1]
        bases = [space_basis]
        for d in range(1, samp):
            bases.append(swap(space_basis, "samp", samp, d))
        mixed = lax.dot_general(
            sample_basis, snapshots, (((0,), (1,)), ((), ())), precision=highest,
            preferred_element_type=jnp.float32)
        mixed = mixed.transpose(1, 0, 2).reshape(snaps * rank, columns)
        own = over_space(dot(mixed, space_basis, ((1,), (1,))))
        rest = over_space(jnp.stack([dot(mixed, b, ((1,), (1,))) for b in bases[1:]]))
        core = jnp.concatenate([own[None], rest])
        for bit in bits(samp):
            got = swap(core, "samp", samp, bit)
            core = core + jnp.stack([got[d ^ bit] for d in range(samp)])
        other = swap(core, "space", space, 1)
        first = lax.axis_index("space") % 2 == 0
        core = jnp.concatenate([jnp.where(first, core, other), jnp.where(first, other, core)], axis=1)
        weight = sum(dot(core[d], bases[d], ((1,), (0,))) for d in range(samp))
        weight = weight.reshape(snaps, rank, columns)
        removed = lax.dot_general(
            sample_basis, weight, (((1,), (1,)), ((), ())), precision=highest,
            preferred_element_type=jnp.float32)
        return snapshots - removed.transpose(1, 0, 2)

    return jax.shard_map(
        shards,
        mesh=mesh,
        in_specs=(P(None, "samp", "space"), P("samp", "space"), P("samp", None)),
        out_specs=P(None, "samp", "space"),
        check_vma=False,
    )
```

time: 163 us -> 82.1 us (0.50)
  waiting for transfers between devices: 95.9 us -> 24 us
  blocking collectives: 28.1 us -> 0 us
  local copies, waits for them, and re-layouts: 0.24 us -> 17.4 us
  starting transfers between devices: 0.04 us -> 15.9 us
  between operations: 13.4 us -> 0.18 us
    reduce_scatter x1 -> x0, waiting for transfers between devices: 57.8 us -> none  [shards(): lax.psum_scatter(lax.dot_general(full_basis, flattened, (((1,), (1,)), ((...]
    all_gather x1 -> x0, waiting for transfers between devices: 37.4 us -> none  [shards(): full_basis = lax.all_gather(space_basis, 'samp', axis=0, tiled=True)]
    ppermute x0 -> x11, waiting for transfers between devices: none -> 24 us  [swap(): return lax.ppermute(value, axis, [(i, i ^ bit) for i in range(size)])]
    all_gather x1 -> x0, blocking collectives: 20 us -> none  [shards(): core_full = lax.all_gather(core_rows, 'space', axis=0, tiled=True)]
    ppermute x0 -> x11, starting transfers between devices: none -> 15.9 us  [swap(): return lax.ppermute(value, axis, [(i, i ^ bit) for i in range(size)])]
    unnamed x4 -> x7, local copies, waits for them, and re-layouts: 0.01 us -> 8.69 us
    sub x0 -> x1, local copies, waits for them, and re-layouts: none -> 8.67 us  [shards(): return snapshots - removed.transpose(1, 0, 2)]
    psum x1 -> x0, blocking collectives: 8.09 us -> none  [shards(): lax.psum(result.reshape(row_terms.shape[0], snap_count * rank_samples), '...]
  transfers between devices with their start and end apart: 2 -> 11, of which waited for: 2 -> 6; matrix products, arithmetic and copies ran while one was open for 0% -> 24% of each run, Pallas kernels for 0% -> 0%
where the time goes in v1:
time: 82.1 us; the launch traced here: 81.7 us
  matrix products  24.2 us (29%)
  waiting for transfers between devices  24 us (29%)
  local copies, waits for them, and re-layouts  17.4 us (21%)
  starting transfers between devices  15.9 us (19%)
    ppermute x11, waiting for transfers between devices, swap(): return lax.ppermute(value, axis, [(i, i ^ bit) for i in range(size)])  24 us
    ppermute x11, starting transfers between devices, swap(): return lax.ppermute(value, axis, [(i, i ^ bit) for i in range(size)])  15.9 us
    dot_general x1, matrix products, shards(): lax.dot_general(sample_basis, weight, (((1,), (1,)), ((), ())), precision...  9.44 us
    unnamed x7, local copies, waits for them, and re-layouts  8.69 us
    sub x1, local copies, waits for them, and re-layouts, shards(): return snapshots - removed.transpose(1, 0, 2)  8.67 us
    dot_general x1, matrix products, shards(): lax.dot_general(sample_basis, snapshots, (((0,), (1,)), ((), ())), precis...  7.54 us
    dot_general x4, matrix products, dot(): lax.dot_general(a, b, (dims, ((), ())), precision=highest, preferred_elem...  7.21 us
  transfers between devices with their start and end apart: 11, of which 6 were waited for; matrix products, arithmetic and copies ran while one was open for 24% of the time, Pallas kernels for 0%

profile of v1, /device:TPU:0, one launch (start us, length us, event | category | flops | bytes accessed | tf_op | source)
XLA Modules:
  0.0 81.7 jit_solution(10213711506462925019)
XLA Ops:
  0.0 0.0 copy-start
  0.0 3.0 %collective-permute-start.4 = (f32[128,2048]{1,0:T(8,128)}, f32[128,2048]{1,0:T(8,128)S(1)}, u32[]{:S(2)}, u32[]{:S(2)}) collective-permute-start(f32[128,2048]{1,0:T(8,128)} %param.4), channel_id=1, source_target_pairs={{0,1},{1,0},{2,3},{3,2},{4,5},{5,4},{6,7},{7,6},{8,9},{9,8},{10,11... | collective-permute-start | bytes 3145736 | tf_op jit(solution)/shard_map/ppermute | solution.py:8
  3.0 0.0 copy-done
  3.0 0.0 copy-start.2
  3.0 7.5 %fusion.8 = f32[64,4,2048]{2,0,1:T(8,128)S(1)} fusion(f32[4,256,2048]{2,1,0:T(8,128)} %param.3, f32[256,64]{0,1:T(8,128)S(1)} %copy-done), kind=kOutput, calls=%fused_computation.14 | convolution fusion | flops 1610612736 | bytes 10551296 | tf_op jit(solution)/shard_map/dot_general | solution.py:40
  10.5 0.0 copy-done.2
  10.5 1.8 %fusion.13 = f32[256,128]{1,0:T(8,128)S(1)} fusion(f32[256,2048]{1,0:T(8,128)S(1)} %bitcast.29, f32[128,2048]{1,0:T(8,128)S(1)} %copy-done.2), kind=kOutput, calls=%fused_computation.26 | convolution fusion | flops 805306368 | bytes 3276800 | tf_op jit(solution)/shard_map/dot_general | solution.py:22
  12.4 0.1 collective-permute-start
  12.4 13.9 %collective-permute-done.4 = f32[128,2048]{1,0:T(8,128)S(1)} collective-permute-done((f32[128,2048]{1,0:T(8,128)}, f32[128,2048]{1,0:T(8,128)S(1)}, u32[]{:S(2)}, u32[]{:S(2)}) %collective-permute-start.4) | collective-permute-done | bytes 1048608 | tf_op jit(solution)/shard_map/ppermute | solution.py:8
  26.3 1.8 %convolution_bitcast_fusion = f32[1,256,128]{2,1,0:T(8,128)S(1)} fusion(f32[256,2048]{1,0:T(8,128)S(1)} %bitcast.30, f32[128,2048]{1,0:T(8,128)S(1)} %collective-permute-done.4), kind=kOutput, calls=%fused_computation.2 | convolution fusion | flops 805306368 | bytes 3276800 | tf_op jit(solution)/shard_map/dot_general | solution.py:22
  28.2 0.1 collective-permute-start.5
  28.2 0.0 collective-permute-done
  28.3 1.8 %collective-permute-start.1 = (f32[128,128]{1,0:T(8,128)S(1)}, f32[128,128]{1,0:T(8,128)S(1)}, u32[]{:S(2)}, u32[]{:S(2)}) collective-permute-start(f32[128,128]{1,0:T(8,128)S(1)} %select_add_fusion.1), channel_id=1, source_target_pairs={{0,4},{2,6},{4,0},{6,2},{8,12},{10,14},{12,8},{14,10},{16,20},{18,... | collective-permute-start | bytes 196616 | tf_op jit(solution)/shard_map/ppermute | solution.py:8
  30.1 0.0 collective-permute-done.5
  30.1 1.2 %collective-permute-start.6 = (f32[1,128,128]{2,1,0:T(8,128)S(1)}, f32[1,128,128]{2,1,0:T(8,128)S(1)}, u32[]{:S(2)}, u32[]{:S(2)}) collective-permute-start(f32[1,128,128]{2,1,0:T(8,128)S(1)} %select_add_fusion), channel_id=1, source_target_pairs={{0,4},{2,6},{4,0},{6,2},{8,12},{10,14},{12,8},{14,10},{16,20},{18,... | collective-permute-start | bytes 196616 | tf_op jit(solution)/shard_map/ppermute | solution.py:8
  31.3 1.5 %collective-permute-done.1 = f32[128,128]{1,0:T(8,128)S(1)} collective-permute-done((f32[128,128]{1,0:T(8,128)S(1)}, f32[128,128]{1,0:T(8,128)S(1)}, u32[]{:S(2)}, u32[]{:S(2)}) %collective-permute-start.1) | collective-permute-done | bytes 65568 | tf_op jit(solution)/shard_map/ppermute | solution.py:8
  32.9 1.9 %collective-permute-start.2 = (f32[128,128]{1,0:T(8,128)S(1)}, f32[128,128]{1,0:T(8,128)S(1)}, u32[]{:S(2)}, u32[]{:S(2)}) collective-permute-start(f32[128,128]{1,0:T(8,128)S(1)} %add.38), channel_id=1, source_target_pairs={{0,8},{2,10},{4,12},{6,14},{8,0},{10,2},{12,4},{14,6},{16,24},{18,... | collective-permute-start | bytes 196616 | tf_op jit(solution)/shard_map/ppermute | solution.py:8
  34.8 0.0 collective-permute-done.6
  34.8 1.3 %collective-permute-start.7 = (f32[1,128,128]{2,1,0:T(8,128)S(1)}, f32[1,128,128]{2,1,0:T(8,128)S(1)}, u32[]{:S(2)}, u32[]{:S(2)}) collective-permute-start(f32[1,128,128]{2,1,0:T(8,128)S(1)} %add.42), channel_id=1, source_target_pairs={{0,8},{2,10},{4,12},{6,14},{8,0},{10,2},{12,4},{14,6},{16,24},{18,... | collective-permute-start | bytes 196616 | tf_op jit(solution)/shard_map/ppermute | solution.py:8
  36.1 1.5 %collective-permute-done.2 = f32[128,128]{1,0:T(8,128)S(1)} collective-permute-done((f32[128,128]{1,0:T(8,128)S(1)}, f32[128,128]{1,0:T(8,128)S(1)}, u32[]{:S(2)}, u32[]{:S(2)}) %collective-permute-start.2) | collective-permute-done | bytes 65568 | tf_op jit(solution)/shard_map/ppermute | solution.py:8
  37.7 3.2 %collective-permute-start.3 = (f32[128,128]{1,0:T(8,128)S(1)}, f32[128,128]{1,0:T(8,128)S(1)}, u32[]{:S(2)}, u32[]{:S(2)}) collective-permute-start(f32[128,128]{1,0:T(8,128)S(1)} %add.39), channel_id=1, source_target_pairs={{0,16},{2,18},{4,20},{6,22},{8,24},{10,26},{12,28},{14,30},{16,0},... | collective-permute-start | bytes 196616 | tf_op jit(solution)/shard_map/ppermute | solution.py:8
  40.8 0.0 collective-permute-done.7
  40.8 1.7 %collective-permute-start.8 = (f32[1,128,128]{2,1,0:T(8,128)S(1)}, f32[1,128,128]{2,1,0:T(8,128)S(1)}, u32[]{:S(2)}, u32[]{:S(2)}) collective-permute-start(f32[1,128,128]{2,1,0:T(8,128)S(1)} %add.43), channel_id=1, source_target_pairs={{0,16},{2,18},{4,20},{6,22},{8,24},{10,26},{12,28},{14,30},{16,0},... | collective-permute-start | bytes 196616 | tf_op jit(solution)/shard_map/ppermute | solution.py:8
  42.5 2.2 %collective-permute-done.3 = f32[128,128]{1,0:T(8,128)S(1)} collective-permute-done((f32[128,128]{1,0:T(8,128)S(1)}, f32[128,128]{1,0:T(8,128)S(1)}, u32[]{:S(2)}, u32[]{:S(2)}) %collective-permute-start.3) | collective-permute-done | bytes 65568 | tf_op jit(solution)/shard_map/ppermute | solution.py:8
  44.7 1.4 %collective-permute-done.8 = f32[1,128,128]{2,1,0:T(8,128)S(1)} collective-permute-done((f32[1,128,128]{2,1,0:T(8,128)S(1)}, f32[1,128,128]{2,1,0:T(8,128)S(1)}, u32[]{:S(2)}, u32[]{:S(2)}) %collective-permute-start.8) | collective-permute-done | bytes 65568 | tf_op jit(solution)/shard_map/ppermute | solution.py:8
  46.1 1.6 %collective-permute-start.9 = (f32[2,128,128]{2,1,0:T(8,128)S(1)}, f32[2,128,128]{2,1,0:T(8,128)S(1)}, u32[]{:S(2)}, u32[]{:S(2)}) collective-permute-start(f32[2,128,128]{2,1,0:T(8,128)S(1)} %pad_maximum_fusion.1), channel_id=1, source_target_pairs={{0,1},{1,0},{2,3},{3,2},{4,5},{5,4},{6,7},{7,6},{8,9},{9,8},{10,11... | collective-permute-start | bytes 393224 | tf_op jit(solution)/shard_map/ppermute | solution.py:8
  47.6 3.5 %collective-permute-done.9 = f32[2,128,128]{2,1,0:T(8,128)S(1)} collective-permute-done((f32[2,128,128]{2,1,0:T(8,128)S(1)}, f32[2,128,128]{2,1,0:T(8,128)S(1)}, u32[]{:S(2)}, u32[]{:S(2)}) %collective-permute-start.9) | collective-permute-done | bytes 131104 | tf_op jit(solution)/shard_map/ppermute | solution.py:8
  51.2 0.1 collective-permute-start.10
  51.2 8.7 %copy.4 = f32[4,256,2048]{1,2,0:T(8,128)} copy(f32[4,256,2048]{2,1,0:T(8,128)} %param.3) | data formatting | bytes 16777216 | tf_op args[0]
  59.9 0.0 collective-permute-done.10
  60.0 0.0 copy-start.1
  60.0 1.8 %fusion.2 = f32[256,2048]{1,0:T(8,128)S(1)} fusion(f32[128,2048]{1,0:T(8,128)S(1)} %copy-done.2, f32[2,128,128]{2,1,0:T(8,128)S(1)} %get-tuple-element.6, f32[2,128,128]{2,1,0:T(8,128)S(1)} %get-tuple-element.5), kind=kOutput, calls=%fused_computation.7 | convolution fusion | flops 805339136 | bytes 3407872 | tf_op jit(solution)/shard_map/dot_general | solution.py:22
  61.8 1.8 %convolution_add_fusion = f32[256,2048]{1,0:T(8,128)S(1)} fusion(f32[256,2048]{1,0:T(8,128)S(1)} %fusion.2, f32[128,2048]{1,0:T(8,128)S(1)} %collective-permute-done.4, f32[2,128,128]{2,1,0:T(8,128)S(1)} %get-tuple-element.5, f32[2,128,128]{2,1,0:T(8,128)S(1)} %get-tuple-element.6), kind=kOutput, calls=%fused_computation.1 | convolution fusion | flops 805863424 | bytes 5505024 | tf_op jit(solution)/shard_map/dot_general | solution.py:22
  63.6 0.0 copy-done.1
  63.6 9.4 %bitcast_subtract_fusion = f32[4,256,2048]{1,2,0:T(8,128)} fusion(f32[4,256,2048]{1,2,0:T(8,128)S(1)} %copy-done.1, f32[4,64,2048]{2,1,0:T(8,128)S(1)} %bitcast.31, f32[256,64]{0,1:T(8,128)S(1)} %copy-done), kind=kOutput, calls=%fused_computation | convolution fusion | flops 1612709888 | bytes 18939904 | tf_op jit(solution)/shard_map/dot_general | solution.py:55
  73.1 8.7 %copy.5 = f32[4,256,2048]{2,1,0:T(8,128)} copy(f32[4,256,2048]{1,2,0:T(8,128)} %bitcast_subtract_fusion) | data formatting | bytes 16777216 | tf_op jit(solution)/shard_map/sub | solution.py:58
  (14 shorter events, 0.2 us)
Async XLA Ops:
  0.0 3.0 %copy-start = (f32[256,64]{0,1:T(8,128)S(1)}, f32[256,64]{0,1:T(8,128)}, u32[]{:S(2)}) copy-start(f32[256,64]{0,1:T(8,128)} %param.5) | copy-start | bytes 196612
  0.0 26.3 %collective-permute-start.4 = (f32[128,2048]{1,0:T(8,128)}, f32[128,2048]{1,0:T(8,128)S(1)}, u32[]{:S(2)}, u32[]{:S(2)}) collective-permute-start(f32[128,2048]{1,0:T(8,128)} %param.4), channel_id=1, source_target_pairs={{0,1},{1,0},{2,3},{3,2},{4,5},{5,4},{6,7},{7,6},{8,9},{9,8},{10,11... | collective-permute-start | bytes 3145736 | tf_op jit(solution)/shard_map/ppermute | solution.py:8
  3.0 7.6 %copy-start.2 = (f32[128,2048]{1,0:T(8,128)S(1)}, f32[128,2048]{1,0:T(8,128)}, u32[]{:S(2)}) copy-start(f32[128,2048]{1,0:T(8,128)} %param.4) | copy-start | bytes 3145732
  12.4 15.9 %collective-permute-start = (f32[128,128]{1,0:T(8,128)S(1)}, f32[128,128]{1,0:T(8,128)S(1)}, u32[]{:S(2)}, u32[]{:S(2)}) collective-permute-start(f32[128,128]{1,0:T(8,128)S(1)} %slice_select_fusion.1), channel_id=1, source_target_pairs={{0,2},{2,0},{4,6},{6,4},{8,10},{10,8},{12,14},{14,12},{16,18},{18,... | collective-permute-start | bytes 196616 | tf_op jit(solution)/shard_map/ppermute | solution.py:8
  28.2 2.0 %collective-permute-start.5 = (f32[1,128,128]{2,1,0:T(8,128)S(1)}, f32[1,128,128]{2,1,0:T(8,128)S(1)}, u32[]{:S(2)}, u32[]{:S(2)}) collective-permute-start(f32[1,128,128]{2,1,0:T(8,128)S(1)} %slice_select_fusion), channel_id=1, source_target_pairs={{0,2},{2,0},{4,6},{6,4},{8,10},{10,8},{12,14},{14,12},{16,18},{18,... | collective-permute-start | bytes 196616 | tf_op jit(solution)/shard_map/ppermute | solution.py:8
  28.3 4.6 %collective-permute-start.1 = (f32[128,128]{1,0:T(8,128)S(1)}, f32[128,128]{1,0:T(8,128)S(1)}, u32[]{:S(2)}, u32[]{:S(2)}) collective-permute-start(f32[128,128]{1,0:T(8,128)S(1)} %select_add_fusion.1), channel_id=1, source_target_pairs={{0,4},{2,6},{4,0},{6,2},{8,12},{10,14},{12,8},{14,10},{16,20},{18,... | collective-permute-start | bytes 196616 | tf_op jit(solution)/shard_map/ppermute | solution.py:8
  30.1 4.7 %collective-permute-start.6 = (f32[1,128,128]{2,1,0:T(8,128)S(1)}, f32[1,128,128]{2,1,0:T(8,128)S(1)}, u32[]{:S(2)}, u32[]{:S(2)}) collective-permute-start(f32[1,128,128]{2,1,0:T(8,128)S(1)} %select_add_fusion), channel_id=1, source_target_pairs={{0,4},{2,6},{4,0},{6,2},{8,12},{10,14},{12,8},{14,10},{16,20},{18,... | collective-permute-start | bytes 196616 | tf_op jit(solution)/shard_map/ppermute | solution.py:8
  32.9 4.8 %collective-permute-start.2 = (f32[128,128]{1,0:T(8,128)S(1)}, f32[128,128]{1,0:T(8,128)S(1)}, u32[]{:S(2)}, u32[]{:S(2)}) collective-permute-start(f32[128,128]{1,0:T(8,128)S(1)} %add.38), channel_id=1, source_target_pairs={{0,8},{2,10},{4,12},{6,14},{8,0},{10,2},{12,4},{14,6},{16,24},{18,... | collective-permute-start | bytes 196616 | tf_op jit(solution)/shard_map/ppermute | solution.py:8
  34.8 6.0 %collective-permute-start.7 = (f32[1,128,128]{2,1,0:T(8,128)S(1)}, f32[1,128,128]{2,1,0:T(8,128)S(1)}, u32[]{:S(2)}, u32[]{:S(2)}) collective-permute-start(f32[1,128,128]{2,1,0:T(8,128)S(1)} %add.42), channel_id=1, source_target_pairs={{0,8},{2,10},{4,12},{6,14},{8,0},{10,2},{12,4},{14,6},{16,24},{18,... | collective-permute-start | bytes 196616 | tf_op jit(solution)/shard_map/ppermute | solution.py:8
  37.7 7.0 %collective-permute-start.3 = (f32[128,128]{1,0:T(8,128)S(1)}, f32[128,128]{1,0:T(8,128)S(1)}, u32[]{:S(2)}, u32[]{:S(2)}) collective-permute-start(f32[128,128]{1,0:T(8,128)S(1)} %add.39), channel_id=1, source_target_pairs={{0,16},{2,18},{4,20},{6,22},{8,24},{10,26},{12,28},{14,30},{16,0},... | collective-permute-start | bytes 196616 | tf_op jit(solution)/shard_map/ppermute | solution.py:8
  40.8 5.2 %collective-permute-start.8 = (f32[1,128,128]{2,1,0:T(8,128)S(1)}, f32[1,128,128]{2,1,0:T(8,128)S(1)}, u32[]{:S(2)}, u32[]{:S(2)}) collective-permute-start(f32[1,128,128]{2,1,0:T(8,128)S(1)} %add.43), channel_id=1, source_target_pairs={{0,16},{2,18},{4,20},{6,22},{8,24},{10,26},{12,28},{14,30},{16,0},... | collective-permute-start | bytes 196616 | tf_op jit(solution)/shard_map/ppermute | solution.py:8
  46.1 5.0 %collective-permute-start.9 = (f32[2,128,128]{2,1,0:T(8,128)S(1)}, f32[2,128,128]{2,1,0:T(8,128)S(1)}, u32[]{:S(2)}, u32[]{:S(2)}) collective-permute-start(f32[2,128,128]{2,1,0:T(8,128)S(1)} %pad_maximum_fusion.1), channel_id=1, source_target_pairs={{0,1},{1,0},{2,3},{3,2},{4,5},{5,4},{6,7},{7,6},{8,9},{9,8},{10,11... | collective-permute-start | bytes 393224 | tf_op jit(solution)/shard_map/ppermute | solution.py:8
  51.2 8.8 %collective-permute-start.10 = (f32[2,128,128]{2,1,0:T(8,128)S(1)}, f32[2,128,128]{2,1,0:T(8,128)S(1)}, u32[]{:S(2)}, u32[]{:S(2)}) collective-permute-start(f32[2,128,128]{2,1,0:T(8,128)S(1)} %maximum_add_fusion), channel_id=1, source_target_pairs={{0,2},{2,0},{4,6},{6,4},{8,10},{10,8},{12,14},{14,12},{16,18},{18,... | collective-permute-start | bytes 393224 | tf_op jit(solution)/shard_map/ppermute | solution.py:8
  60.0 3.7 %copy-start.1 = (f32[4,256,2048]{1,2,0:T(8,128)S(1)}, f32[4,256,2048]{1,2,0:T(8,128)}, u32[]{:S(2)}) copy-start(f32[4,256,2048]{1,2,0:T(8,128)} %copy.4) | copy-start | bytes 25165828

commit v2 on v1

v2 whole, which is shorter than its diff:
```python
import functools

import jax
import jax.numpy as jnp
from jax import lax
from jax.experimental import pallas as pl
from jax.experimental.pallas import tpu as pltpu
from jax.sharding import PartitionSpec as P

MIB = 1 << 20


def swap(value, axis, size, bit):
    return lax.ppermute(value, axis, [(i, i ^ bit) for i in range(size)])


def bits(size, start=1):
    while start < size:
        yield start
        start *= 2


def tile_of(columns):
    for tile in (512, 256, 128):
        if columns % tile == 0:
            return tile
    return columns


def split(value):
    high = value.astype(jnp.bfloat16)
    return high, (value - high.astype(jnp.float32)).astype(jnp.bfloat16)


def mul(a, b):
    return lax.dot_general(a, b, (((1,), (0,)), ((), ())), preferred_element_type=jnp.float32)


def mul_t(a, b):
    return lax.dot_general(a, b, (((1,), (1,)), ((), ())), preferred_element_type=jnp.float32)


def rows_times(y_high, y_low, b):
    rank = b.shape[0]
    high, low = split(b)
    both = mul_t(y_high, jnp.concatenate([high, low], axis=0))
    return both[:, :rank] + both[:, rank:] + mul_t(y_low, high), high, low


def first_kernel(tile, x_hbm, s_ref, b_hbm, x_ref, y_ref, bs_ref, part_ref, b_ref, sems, b_sem):
    snaps, samples, columns = x_ref.shape
    rank = s_ref.shape[0]
    steps = columns // tile
    copies = []
    for j in range(steps):
        cols = pl.ds(j * tile, tile)
        copies.append(pltpu.make_async_copy(x_hbm.at[:, :, cols], x_ref.at[:, :, cols], sems.at[j]))
    b_copy = pltpu.make_async_copy(b_hbm, b_ref, b_sem)
    copies[0].start()
    b_copy.start()
    for copy in copies[1:]:
        copy.start()
    s_high, s_low = split(s_ref[...])
    s_both = jnp.concatenate([s_high, s_low], axis=0)
    for j in range(steps):
        cols = pl.ds(j * tile, tile)
        copies[j].wait()
        if j == 0:
            b_copy.wait()
        for t in range(snaps):
            x_high, x_low = split(x_ref[t, :, cols])
            both = mul(s_both, x_high)
            y = both[:rank] + both[rank:] + mul(s_high, x_low)
            y_high, y_low = split(y)
            y_ref[0, t * rank:(t + 1) * rank, cols] = y_high
            y_ref[1, t * rank:(t + 1) * rank, cols] = y_low
        total, high, low = rows_times(y_ref[0, :, cols], y_ref[1, :, cols], b_ref[:, cols])
        bs_ref[0, :, cols] = high
        bs_ref[1, :, cols] = low
        if j == 0:
            part_ref[...] = total
        else:
            part_ref[...] += total


def second_kernel(tile, parts, *refs):
    b_refs, (y_ref, _), outs = refs[:parts], refs[parts:parts + 2], refs[parts + 2:]
    part_ref, bs_refs = outs[0], outs[1:]
    for d in range(parts):
        for j in range(y_ref.shape[2] // tile):
            cols = pl.ds(j * tile, tile)
            total, high, low = rows_times(y_ref[0, :, cols], y_ref[1, :, cols], b_refs[d][:, cols])
            bs_refs[d][0, :, cols] = high
            bs_refs[d][1, :, cols] = low
            if j == 0:
                part_ref[d] = total
            else:
                part_ref[d] += total


def last_kernel(tile, parts, *refs):
    core_ref, s_ref, x_ref = refs[:3]
    bs_refs, out_hbm, out_ref, sems = refs[3:3 + parts], refs[3 + parts], refs[4 + parts], refs[5 + parts]
    snaps, samples, columns = x_ref.shape
    rank = s_ref.shape[0]
    s_high, s_low = split(s_ref[...].T)
    s_all = jnp.concatenate([s_high, s_low, s_high], axis=1)
    c_high, c_low = split(jnp.concatenate([core_ref[d] for d in range(parts)], axis=1))
    c_both = jnp.concatenate([c_high, c_low], axis=0)
    wide = c_high.shape[0]
    copies = []
    for j in range(columns // tile):
        cols = pl.ds(j * tile, tile)
        b_high = jnp.concatenate([b[0, :, cols] for b in bs_refs], axis=0)
        b_low = jnp.concatenate([b[1, :, cols] for b in bs_refs], axis=0)
        both = mul(c_both, b_high)
        weight = both[:wide] + both[wide:] + mul(c_high, b_low)
        w_high, w_low = split(weight)
        for t in range(snaps):
            high, low = w_high[t * rank:(t + 1) * rank], w_low[t * rank:(t + 1) * rank]
            removed = mul(s_all, jnp.concatenate([high, high, low], axis=0))
            out_ref[t, :, cols] = x_ref[t, :, cols] - removed
        copies.append(pltpu.make_async_copy(out_ref.at[:, :, cols], out_hbm.at[:, :, cols], sems.at[j]))
        copies[-1].start()
    for copy in copies:
        copy.wait()


VMEM = pl.BlockSpec(memory_space=pltpu.VMEM)
ANY = pl.BlockSpec(memory_space=pl.ANY)
HBM = pl.BlockSpec(memory_space=pltpu.HBM)


def on_chip(shape, dtype):
    return pltpu.VMEM(shape, dtype)


def solution(mesh):
    space, samp = mesh.shape["space"], mesh.shape["samp"]

    def over_space(part):
        core = lax.axis_index("space") % 2
        half = part.shape[-2] // 2
        low, high = part[..., :half, :], part[..., half:, :]
        mine = jnp.where(core == 0, low, high)
        total = mine + swap(jnp.where(core == 0, high, low), "space", space, 1)
        for bit in bits(space, 2):
            total = total + swap(total, "space", space, bit)
        return total

    def shards(snapshots, space_basis, sample_basis):
        snaps, samples, columns = snapshots.shape
        rank = sample_basis.shape[1]
        basis_rows = space_basis.shape[0]
        wide = snaps * rank
        tile = tile_of(columns)
        steps = columns // tile
        others = [swap(space_basis, "samp", samp, d) for d in range(1, samp)]
        mixer = sample_basis.T
        flops = 6 * wide * samples * columns
        x_chip, mixed, own_split, own = pl.pallas_call(
            functools.partial(first_kernel, tile),
            out_shape=(
                on_chip(snapshots.shape, jnp.float32),
                on_chip((2, wide, columns), jnp.bfloat16),
                on_chip((2, basis_rows, columns), jnp.bfloat16),
                on_chip((wide, basis_rows), jnp.float32),
            ),
            in_specs=[HBM, VMEM, HBM],
            out_specs=(VMEM,) * 4,
            scratch_shapes=[
                pltpu.VMEM((basis_rows, columns), jnp.float32),
                pltpu.SemaphoreType.DMA((steps,)),
                pltpu.SemaphoreType.DMA,
            ],
            compiler_params=pltpu.CompilerParams(vmem_limit_bytes=48 * MIB),
            cost_estimate=pl.CostEstimate(flops=flops, bytes_accessed=snapshots.size * 4, transcendentals=0),
            name="first",
        )(snapshots, mixer, space_basis)
        own = over_space(own)
        rest, *rest_splits = pl.pallas_call(
            functools.partial(second_kernel, tile, samp - 1),
            out_shape=(
                on_chip((samp - 1, wide, basis_rows), jnp.float32),
                *[on_chip((2, basis_rows, columns), jnp.bfloat16) for _ in others],
            ),
            in_specs=[VMEM] * (len(others) + 1) + [ANY],
            out_specs=(VMEM,) * samp,
            compiler_params=pltpu.CompilerParams(vmem_limit_bytes=16 * MIB),
            cost_estimate=pl.CostEstimate(
                flops=6 * wide * basis_rows * columns * (samp - 1), bytes_accessed=0, transcendentals=0),
            name="second",
        )(*others, mixed, own)
        rest = over_space(rest)
        core = jnp.concatenate([own[None], rest])
        for bit in bits(samp):
            got = swap(core, "samp", samp, bit)
            core = core + jnp.stack([got[d ^ bit] for d in range(samp)])
        other = swap(core, "space", space, 1)
        first = lax.axis_index("space") % 2 == 0
        core = jnp.concatenate([jnp.where(first, core, other), jnp.where(first, other, core)], axis=1)
        return pl.pallas_call(
            functools.partial(last_kernel, tile, samp),
            out_shape=jax.ShapeDtypeStruct(snapshots.shape, jnp.float32),
            in_specs=[VMEM] * (3 + samp),
            out_specs=ANY,
            scratch_shapes=[
                pltpu.VMEM(snapshots.shape, jnp.float32),
                pltpu.SemaphoreType.DMA((steps,)),
            ],
            compiler_params=pltpu.CompilerParams(vmem_limit_bytes=20 * MIB),
            cost_estimate=pl.CostEstimate(flops=2 * flops, bytes_accessed=snapshots.size * 4, transcendentals=0),
            name="last",
        )(core, mixer, x_chip, own_split, *rest_splits)

    return jax.shard_map(
        shards,
        mesh=mesh,
        in_specs=(P(None, "samp", "space"), P("samp", "space"), P("samp", None)),
        out_specs=P(None, "samp", "space"),
        check_vma=False,
    )
```

time: 82.1 us -> 53.2 us (0.65)
  matrix products: 24.2 us -> 0 us
  local copies, waits for them, and re-layouts: 17.4 us -> 0.01 us
  Pallas kernels: 0 us -> 12.2 us
  starting transfers between devices: 15.9 us -> 17.5 us
  waiting for transfers between devices: 24 us -> 23 us
    dot_general x6 -> x0, matrix products: 24.2 us -> none  [the longest x1 9.44 us: shards(): lax.dot_general(sample_basis, weight, (((1,), (1,)), ((), ())), precision...]
    pallas_call x0 -> x3, Pallas kernels: none -> 12.2 us  [the longest x1 7.35 us: shards(): pl.pallas_call(functools.partial(first_kernel, tile), out_shape=(on_chip(...]
    unnamed x7 -> x2, local copies, waits for them, and re-layouts: 8.69 us -> 0.01 us
    sub x1 -> x0, local copies, waits for them, and re-layouts: 8.67 us -> none  [shards(): return snapshots - removed.transpose(1, 0, 2)]
    ppermute x11, starting transfers between devices: 15.9 us -> 17.5 us  [swap(): return lax.ppermute(value, axis, [(i, i ^ bit) for i in range(size)])]
    ppermute x11, waiting for transfers between devices: 24 us -> 23 us  [swap(): return lax.ppermute(value, axis, [(i, i ^ bit) for i in range(size)])]
  transfers between devices with their start and end apart: 11 -> 11, of which waited for: 6 -> 11; matrix products, arithmetic and copies ran while one was open for 24% -> 0% of each run, Pallas kernels for 0% -> 14%
where the time goes in v2:
time: 53.2 us; the launch traced here: 53 us
  waiting for transfers between devices  23 us (43%)
  starting transfers between devices  17.5 us (33%)
  Pallas kernels  12.2 us (23%)
    ppermute x11, waiting for transfers between devices, swap(): return lax.ppermute(value, axis, [(i, i ^ bit) for i in range(size)])  23 us
    ppermute x11, starting transfers between devices, swap(): return lax.ppermute(value, axis, [(i, i ^ bit) for i in range(size)])  17.5 us
    pallas_call x1, Pallas kernels, shards(): pl.pallas_call(functools.partial(first_kernel, tile), out_shape=(on_chip(...  7.35 us
    pallas_call x1, Pallas kernels, shards(): pl.pallas_call(functools.partial(last_kernel, tile, samp), out_shape=jax....  4.11 us
  transfers between devices with their start and end apart: 11, of which 11 were waited for; matrix products, arithmetic and copies ran while one was open for 0% of the time, Pallas kernels for 14%

profile of v2, /device:TPU:0, one launch (start us, length us, event | category | flops | bytes accessed | tf_op | source)
XLA Modules:
  0.0 53.0 jit_solution(11873732425905866025)
XLA Ops:
  0.0 3.0 %collective-permute-start.4 = (f32[128,2048]{1,0:T(8,128)}, f32[128,2048]{1,0:T(8,128)S(1)}, u32[]{:S(2)}, u32[]{:S(2)}) collective-permute-start(f32[128,2048]{1,0:T(8,128)} %b_hbm.1), channel_id=1, source_target_pairs={{0,1},{1,0},{2,3},{3,2},{4,5},{5,4},{6,7},{7,6},{8,9},{9,8},{10,11... | collective-permute-start | bytes 3145736 | tf_op jit(solution)/shard_map/ppermute | solution.py:14
  3.0 0.0 copy-start
  3.0 7.4 %first.1 = (f32[4,256,2048]{2,1,0:T(8,128)S(1)}, bf16[2,256,2048]{2,1,0:T(8,128)(2,1)S(1)}, bf16[2,128,2048]{2,1,0:T(8,128)(2,1)S(1)}, f32[256,128]{1,0:T(8,128)S(1)}) custom-call(f32[4,256,2048]{2,1,0:T(8,128)} %x_hbm.1, f32[64,256]{1,0:T(8,128)} %bitcast.5, f32[128,2048]{1,0:T(8,128)} %b_hbm.1), custom_call_target="tpu_custom_call" | custom-call | flops 805306368 | bytes 8388608 | tf_op jit(solution)/shard_map/first/pallas_call | solution.py:161
  10.3 0.1 collective-permute-start
  10.4 1.2 %collective-permute-done = f32[128,128]{1,0:T(8,128)S(1)} collective-permute-done((f32[128,128]{1,0:T(8,128)S(1)}, f32[128,128]{1,0:T(8,128)S(1)}, u32[]{:S(2)}, u32[]{:S(2)}) %collective-permute-start) | collective-permute-done | bytes 65568 | tf_op jit(solution)/shard_map/ppermute | solution.py:14
  11.7 1.6 %collective-permute-start.1 = (f32[128,128]{1,0:T(8,128)S(1)}, f32[128,128]{1,0:T(8,128)S(1)}, u32[]{:S(2)}, u32[]{:S(2)}) collective-permute-start(f32[128,128]{1,0:T(8,128)S(1)} %select_add_fusion.1), channel_id=1, source_target_pairs={{0,4},{2,6},{4,0},{6,2},{8,12},{10,14},{12,8},{14,10},{16,20},{18,... | collective-permute-start | bytes 196616 | tf_op jit(solution)/shard_map/ppermute | solution.py:14
  13.3 2.7 %collective-permute-done.1 = f32[128,128]{1,0:T(8,128)S(1)} collective-permute-done((f32[128,128]{1,0:T(8,128)S(1)}, f32[128,128]{1,0:T(8,128)S(1)}, u32[]{:S(2)}, u32[]{:S(2)}) %collective-permute-start.1) | collective-permute-done | bytes 65568 | tf_op jit(solution)/shard_map/ppermute | solution.py:14
  16.0 1.6 %collective-permute-start.2 = (f32[128,128]{1,0:T(8,128)S(1)}, f32[128,128]{1,0:T(8,128)S(1)}, u32[]{:S(2)}, u32[]{:S(2)}) collective-permute-start(f32[128,128]{1,0:T(8,128)S(1)} %add.35), channel_id=1, source_target_pairs={{0,8},{2,10},{4,12},{6,14},{8,0},{10,2},{12,4},{14,6},{16,24},{18,... | collective-permute-start | bytes 196616 | tf_op jit(solution)/shard_map/ppermute | solution.py:14
  17.7 2.7 %collective-permute-done.2 = f32[128,128]{1,0:T(8,128)S(1)} collective-permute-done((f32[128,128]{1,0:T(8,128)S(1)}, f32[128,128]{1,0:T(8,128)S(1)}, u32[]{:S(2)}, u32[]{:S(2)}) %collective-permute-start.2) | collective-permute-done | bytes 65568 | tf_op jit(solution)/shard_map/ppermute | solution.py:14
  20.4 2.7 %collective-permute-start.3 = (f32[128,128]{1,0:T(8,128)S(1)}, f32[128,128]{1,0:T(8,128)S(1)}, u32[]{:S(2)}, u32[]{:S(2)}) collective-permute-start(f32[128,128]{1,0:T(8,128)S(1)} %add.36), channel_id=1, source_target_pairs={{0,16},{2,18},{4,20},{6,22},{8,24},{10,26},{12,28},{14,30},{16,0},... | collective-permute-start | bytes 196616 | tf_op jit(solution)/shard_map/ppermute | solution.py:14
  23.0 2.6 %collective-permute-done.3 = f32[128,128]{1,0:T(8,128)S(1)} collective-permute-done((f32[128,128]{1,0:T(8,128)S(1)}, f32[128,128]{1,0:T(8,128)S(1)}, u32[]{:S(2)}, u32[]{:S(2)}) %collective-permute-start.3) | collective-permute-done | bytes 65568 | tf_op jit(solution)/shard_map/ppermute | solution.py:14
  25.6 0.7 %collective-permute-done.4.refs_0_ = f32[128,2048]{1,0:T(8,128)S(1)} collective-permute-done((f32[128,2048]{1,0:T(8,128)}, f32[128,2048]{1,0:T(8,128)S(1)}, u32[]{:S(2)}, u32[]{:S(2)}) %collective-permute-start.4) | collective-permute-done | bytes 1048608 | tf_op jit(solution)/shard_map/ppermute | solution.py:14
  26.3 0.7 %second.1 = (f32[1,256,128]{2,1,0:T(8,128)S(1)}, bf16[2,128,2048]{2,1,0:T(8,128)(2,1)S(1)}) custom-call(f32[128,2048]{1,0:T(8,128)S(1)} %collective-permute-done.4.refs_0_, bf16[2,256,2048]{2,1,0:T(8,128)(2,1)S(1)} %get-tuple-element.12.refs_1_, f32[128,128]{1,0:T(8,128)S(1)} %add.37.refs_2_), custom_call_target="tpu_custom_call" | custom-call | flops 402653184 | tf_op jit(solution)/shard_map/second/pallas_call | solution.py:181
  27.1 0.1 collective-permute-start.5
  27.2 1.2 %collective-permute-done.5 = f32[1,128,128]{2,1,0:T(8,128)S(1)} collective-permute-done((f32[1,128,128]{2,1,0:T(8,128)S(1)}, f32[1,128,128]{2,1,0:T(8,128)S(1)}, u32[]{:S(2)}, u32[]{:S(2)}) %collective-permute-start.5) | collective-permute-done | bytes 65568 | tf_op jit(solution)/shard_map/ppermute | solution.py:14
  28.4 1.8 %collective-permute-start.6 = (f32[1,128,128]{2,1,0:T(8,128)S(1)}, f32[1,128,128]{2,1,0:T(8,128)S(1)}, u32[]{:S(2)}, u32[]{:S(2)}) collective-permute-start(f32[1,128,128]{2,1,0:T(8,128)S(1)} %select_add_fusion), channel_id=1, source_target_pairs={{0,4},{2,6},{4,0},{6,2},{8,12},{10,14},{12,8},{14,10},{16,20},{18,... | collective-permute-start | bytes 196616 | tf_op jit(solution)/shard_map/ppermute | solution.py:14
  30.3 2.5 %collective-permute-done.6 = f32[1,128,128]{2,1,0:T(8,128)S(1)} collective-permute-done((f32[1,128,128]{2,1,0:T(8,128)S(1)}, f32[1,128,128]{2,1,0:T(8,128)S(1)}, u32[]{:S(2)}, u32[]{:S(2)}) %collective-permute-start.6) | collective-permute-done | bytes 65568 | tf_op jit(solution)/shard_map/ppermute | solution.py:14
  32.8 1.9 %collective-permute-start.7 = (f32[1,128,128]{2,1,0:T(8,128)S(1)}, f32[1,128,128]{2,1,0:T(8,128)S(1)}, u32[]{:S(2)}, u32[]{:S(2)}) collective-permute-start(f32[1,128,128]{2,1,0:T(8,128)S(1)} %add.39), channel_id=1, source_target_pairs={{0,8},{2,10},{4,12},{6,14},{8,0},{10,2},{12,4},{14,6},{16,24},{18,... | collective-permute-start | bytes 196616 | tf_op jit(solution)/shard_map/ppermute | solution.py:14
  34.7 2.4 %collective-permute-done.7 = f32[1,128,128]{2,1,0:T(8,128)S(1)} collective-permute-done((f32[1,128,128]{2,1,0:T(8,128)S(1)}, f32[1,128,128]{2,1,0:T(8,128)S(1)}, u32[]{:S(2)}, u32[]{:S(2)}) %collective-permute-start.7) | collective-permute-done | bytes 65568 | tf_op jit(solution)/shard_map/ppermute | solution.py:14
  37.1 2.9 %collective-permute-start.8 = (f32[1,128,128]{2,1,0:T(8,128)S(1)}, f32[1,128,128]{2,1,0:T(8,128)S(1)}, u32[]{:S(2)}, u32[]{:S(2)}) collective-permute-start(f32[1,128,128]{2,1,0:T(8,128)S(1)} %add.40), channel_id=1, source_target_pairs={{0,16},{2,18},{4,20},{6,22},{8,24},{10,26},{12,28},{14,30},{16,0},... | collective-permute-start | bytes 196616 | tf_op jit(solution)/shard_map/ppermute | solution.py:14
  40.0 2.3 %collective-permute-done.8 = f32[1,128,128]{2,1,0:T(8,128)S(1)} collective-permute-done((f32[1,128,128]{2,1,0:T(8,128)S(1)}, f32[1,128,128]{2,1,0:T(8,128)S(1)}, u32[]{:S(2)}, u32[]{:S(2)}) %collective-permute-start.8) | collective-permute-done | bytes 65568 | tf_op jit(solution)/shard_map/ppermute | solution.py:14
  42.4 1.8 %collective-permute-start.9 = (f32[2,128,128]{2,1,0:T(8,128)S(1)}, f32[2,128,128]{2,1,0:T(8,128)S(1)}, u32[]{:S(2)}, u32[]{:S(2)}) collective-permute-start(f32[2,128,128]{2,1,0:T(8,128)S(1)} %pad_maximum_fusion.1), channel_id=1, source_target_pairs={{0,1},{1,0},{2,3},{3,2},{4,5},{5,4},{6,7},{7,6},{8,9},{9,8},{10,11... | collective-permute-start | bytes 393224 | tf_op jit(solution)/shard_map/ppermute | solution.py:14
  44.2 3.2 %collective-permute-done.9 = f32[2,128,128]{2,1,0:T(8,128)S(1)} collective-permute-done((f32[2,128,128]{2,1,0:T(8,128)S(1)}, f32[2,128,128]{2,1,0:T(8,128)S(1)}, u32[]{:S(2)}, u32[]{:S(2)}) %collective-permute-start.9) | collective-permute-done | bytes 131104 | tf_op jit(solution)/shard_map/ppermute | solution.py:14
  47.4 0.1 collective-permute-start.10
  47.5 1.3 %collective-permute-done.10 = f32[2,128,128]{2,1,0:T(8,128)S(1)} collective-permute-done((f32[2,128,128]{2,1,0:T(8,128)S(1)}, f32[2,128,128]{2,1,0:T(8,128)S(1)}, u32[]{:S(2)}, u32[]{:S(2)}) %collective-permute-start.10) | collective-permute-done | bytes 131104 | tf_op jit(solution)/shard_map/ppermute | solution.py:14
  48.9 0.0 copy-done
  48.9 4.1 %last.1 = f32[4,256,2048]{2,1,0:T(8,128)} custom-call(f32[2,256,128]{2,1,0:T(8,128)S(1)} %pad_maximum_fusion.refs_0_, f32[64,256]{1,0:T(8,128)S(1)} %bitcast.6, f32[4,256,2048]{2,1,0:T(8,128)S(1)} %get-tuple-element.14.refs_2_, bf16[2,128,2048]{2,1,0:T(8,128)(2,1)S(1)} %get-tuple-element.15.refs_3_, bf16[2,128,2048]{2,1,0:T(8,128)(2,1)S(1)} %get-tuple-element.16.refs_4_), custom_call_target="tpu_custom_call" | custom-call | flops 1610612736 | bytes 8388608 | tf_op jit(solution)/shard_map/last/pallas_call | solution.py:202
  (15 shorter events, 0.2 us)
Async XLA Ops:
  0.0 26.3 %collective-permute-start.4 = (f32[128,2048]{1,0:T(8,128)}, f32[128,2048]{1,0:T(8,128)S(1)}, u32[]{:S(2)}, u32[]{:S(2)}) collective-permute-start(f32[128,2048]{1,0:T(8,128)} %b_hbm.1), channel_id=1, source_target_pairs={{0,1},{1,0},{2,3},{3,2},{4,5},{5,4},{6,7},{7,6},{8,9},{9,8},{10,11... | collective-permute-start | bytes 3145736 | tf_op jit(solution)/shard_map/ppermute | solution.py:14
  3.0 45.9 %copy-start = (f32[256,64]{0,1:T(8,128)S(1)}, f32[256,64]{0,1:T(8,128)}, u32[]{:S(2)}) copy-start(f32[256,64]{0,1:T(8,128)} %param.5) | copy-start | bytes 196612
  10.3 1.3 %collective-permute-start = (f32[128,128]{1,0:T(8,128)S(1)}, f32[128,128]{1,0:T(8,128)S(1)}, u32[]{:S(2)}, u32[]{:S(2)}) collective-permute-start(f32[128,128]{1,0:T(8,128)S(1)} %slice_select_fusion.1), channel_id=1, source_target_pairs={{0,2},{2,0},{4,6},{6,4},{8,10},{10,8},{12,14},{14,12},{16,18},{18,... | collective-permute-start | bytes 196616 | tf_op jit(solution)/shard_map/ppermute | solution.py:14
  11.7 4.3 %collective-permute-start.1 = (f32[128,128]{1,0:T(8,128)S(1)}, f32[128,128]{1,0:T(8,128)S(1)}, u32[]{:S(2)}, u32[]{:S(2)}) collective-permute-start(f32[128,128]{1,0:T(8,128)S(1)} %select_add_fusion.1), channel_id=1, source_target_pairs={{0,4},{2,6},{4,0},{6,2},{8,12},{10,14},{12,8},{14,10},{16,20},{18,... | collective-permute-start | bytes 196616 | tf_op jit(solution)/shard_map/ppermute | solution.py:14
  16.0 4.3 %collective-permute-start.2 = (f32[128,128]{1,0:T(8,128)S(1)}, f32[128,128]{1,0:T(8,128)S(1)}, u32[]{:S(2)}, u32[]{:S(2)}) collective-permute-start(f32[128,128]{1,0:T(8,128)S(1)} %add.35), channel_id=1, source_target_pairs={{0,8},{2,10},{4,12},{6,14},{8,0},{10,2},{12,4},{14,6},{16,24},{18,... | collective-permute-start | bytes 196616 | tf_op jit(solution)/shard_map/ppermute | solution.py:14
  20.4 5.2 %collective-permute-start.3 = (f32[128,128]{1,0:T(8,128)S(1)}, f32[128,128]{1,0:T(8,128)S(1)}, u32[]{:S(2)}, u32[]{:S(2)}) collective-permute-start(f32[128,128]{1,0:T(8,128)S(1)} %add.36), channel_id=1, source_target_pairs={{0,16},{2,18},{4,20},{6,22},{8,24},{10,26},{12,28},{14,30},{16,0},... | collective-permute-start | bytes 196616 | tf_op jit(solution)/shard_map/ppermute | solution.py:14
  27.1 1.3 %collective-permute-start.5 = (f32[1,128,128]{2,1,0:T(8,128)S(1)}, f32[1,128,128]{2,1,0:T(8,128)S(1)}, u32[]{:S(2)}, u32[]{:S(2)}) collective-permute-start(f32[1,128,128]{2,1,0:T(8,128)S(1)} %slice_select_fusion), channel_id=1, source_target_pairs={{0,2},{2,0},{4,6},{6,4},{8,10},{10,8},{12,14},{14,12},{16,18},{18,... | collective-permute-start | bytes 196616 | tf_op jit(solution)/shard_map/ppermute | solution.py:14
  28.4 4.3 %collective-permute-start.6 = (f32[1,128,128]{2,1,0:T(8,128)S(1)}, f32[1,128,128]{2,1,0:T(8,128)S(1)}, u32[]{:S(2)}, u32[]{:S(2)}) collective-permute-start(f32[1,128,128]{2,1,0:T(8,128)S(1)} %select_add_fusion), channel_id=1, source_target_pairs={{0,4},{2,6},{4,0},{6,2},{8,12},{10,14},{12,8},{14,10},{16,20},{18,... | collective-permute-start | bytes 196616 | tf_op jit(solution)/shard_map/ppermute | solution.py:14
  32.8 4.3 %collective-permute-start.7 = (f32[1,128,128]{2,1,0:T(8,128)S(1)}, f32[1,128,128]{2,1,0:T(8,128)S(1)}, u32[]{:S(2)}, u32[]{:S(2)}) collective-permute-start(f32[1,128,128]{2,1,0:T(8,128)S(1)} %add.39), channel_id=1, source_target_pairs={{0,8},{2,10},{4,12},{6,14},{8,0},{10,2},{12,4},{14,6},{16,24},{18,... | collective-permute-start | bytes 196616 | tf_op jit(solution)/shard_map/ppermute | solution.py:14
  37.1 5.2 %collective-permute-start.8 = (f32[1,128,128]{2,1,0:T(8,128)S(1)}, f32[1,128,128]{2,1,0:T(8,128)S(1)}, u32[]{:S(2)}, u32[]{:S(2)}) collective-permute-start(f32[1,128,128]{2,1,0:T(8,128)S(1)} %add.40), channel_id=1, source_target_pairs={{0,16},{2,18},{4,20},{6,22},{8,24},{10,26},{12,28},{14,30},{16,0},... | collective-permute-start | bytes 196616 | tf_op jit(solution)/shard_map/ppermute | solution.py:14
  42.4 5.0 %collective-permute-start.9 = (f32[2,128,128]{2,1,0:T(8,128)S(1)}, f32[2,128,128]{2,1,0:T(8,128)S(1)}, u32[]{:S(2)}, u32[]{:S(2)}) collective-permute-start(f32[2,128,128]{2,1,0:T(8,128)S(1)} %pad_maximum_fusion.1), channel_id=1, source_target_pairs={{0,1},{1,0},{2,3},{3,2},{4,5},{5,4},{6,7},{7,6},{8,9},{9,8},{10,11... | collective-permute-start | bytes 393224 | tf_op jit(solution)/shard_map/ppermute | solution.py:14
  47.4 1.4 %collective-permute-start.10 = (f32[2,128,128]{2,1,0:T(8,128)S(1)}, f32[2,128,128]{2,1,0:T(8,128)S(1)}, u32[]{:S(2)}, u32[]{:S(2)}) collective-permute-start(f32[2,128,128]{2,1,0:T(8,128)S(1)} %maximum_add_fusion), channel_id=1, source_target_pairs={{0,2},{2,0},{4,6},{6,4},{8,10},{10,8},{12,14},{14,12},{16,18},{18,... | collective-permute-start | bytes 393224 | tf_op jit(solution)/shard_map/ppermute | solution.py:14

commit v3 on v2

--- a/solution.py
+++ b/solution.py
@@ -7,6 +7,7 @@
 from jax.experimental.pallas import tpu as pltpu
 from jax.sharding import PartitionSpec as P
 
+
 MIB = 1 << 20
 
 
@@ -18,6 +19,11 @@
     while start < size:
         yield start
         start *= 2
+
+
+def swap_both(value, space, samp, bit, other):
+    perm = [(i * samp + j, (i ^ bit) * samp + (j ^ other)) for i in range(space) for j in range(samp)]
+    return lax.ppermute(value, ("space", "samp"), perm)
 
 
 def tile_of(columns):
@@ -48,7 +54,7 @@
 
 
 def first_kernel(tile, x_hbm, s_ref, b_hbm, x_ref, y_ref, bs_ref, part_ref, b_ref, sems, b_sem):
-    snaps, samples, columns = x_ref.shape
+    snaps, _, columns = x_ref.shape
     rank = s_ref.shape[0]
     steps = columns // tile
     copies = []
@@ -101,7 +107,7 @@
 def last_kernel(tile, parts, *refs):
     core_ref, s_ref, x_ref = refs[:3]
     bs_refs, out_hbm, out_ref, sems = refs[3:3 + parts], refs[3 + parts], refs[4 + parts], refs[5 + parts]
-    snaps, samples, columns = x_ref.shape
+    snaps, _, columns = x_ref.shape
     rank = s_ref.shape[0]
     s_high, s_low = split(s_ref[...].T)
     s_all = jnp.concatenate([s_high, s_low, s_high], axis=1)
@@ -138,15 +144,45 @@
 def solution(mesh):
     space, samp = mesh.shape["space"], mesh.shape["samp"]
 
-    def over_space(part):
+    left = list(bits(space, 2))
+    groups = []
+    while len(left) > 1:
+        groups.append((left[-1], left[-2] | left[-1], left[-2]))
+        left = left[:-2]
+
+    def halved(part):
         core = lax.axis_index("space") % 2
         half = part.shape[-2] // 2
         low, high = part[..., :half, :], part[..., half:, :]
         mine = jnp.where(core == 0, low, high)
-        total = mine + swap(jnp.where(core == 0, high, low), "space", space, 1)
-        for bit in bits(space, 2):
-            total = total + swap(total, "space", space, bit)
-        return total
+        return mine + swap(jnp.where(core == 0, high, low), "space", space, 1)
+
+    def over_groups(part):
+        for group in groups:
+            got = [swap(part, "space", space, bit) for bit in group]
+            part = part + got[0] + got[1] + got[2]
+        return part
+
+    def over_rest(own, rest):
+        done = [own] + [rest[d] for d in range(samp - 1)]
+        for bit in bits(samp):
+            if bit == 1:
+                got_own = swap(own, "samp", samp, bit)
+                far = [swap_both(rest, space, samp, b, bit) for b in left]
+                got_rest = swap(rest, "samp", samp, bit)
+                near = [swap(rest, "space", space, b) for b in left]
+                got = [got_own]
+                for d in range(1, samp):
+                    value = got_rest[d - 1]
+                    for f in far:
+                        value = value + f[d - 1]
+                    got.append(value)
+                for n in near:
+                    done = [done[0]] + [done[d] + n[d - 1] for d in range(1, samp)]
+            else:
+                got = swap(jnp.stack(done), "samp", samp, bit)
+            done = [done[d] + got[d ^ bit] for d in range(samp)]
+        return jnp.stack(done)
 
     def shards(snapshots, space_basis, sample_basis):
         snaps, samples, columns = snapshots.shape
@@ -177,7 +213,9 @@
             cost_estimate=pl.CostEstimate(flops=flops, bytes_accessed=snapshots.size * 4, transcendentals=0),
             name="first",
         )(snapshots, mixer, space_basis)
-        own = over_space(own)
+        own = over_groups(halved(own))
+        for bit in left:
+            own = own + swap(own, "space", space, bit)
         rest, *rest_splits = pl.pallas_call(
             functools.partial(second_kernel, tile, samp - 1),
             out_shape=(
@@ -191,11 +229,7 @@
                 flops=6 * wide * basis_rows * columns * (samp - 1), bytes_accessed=0, transcendentals=0),
             name="second",
         )(*others, mixed, own)
-        rest = over_space(rest)
-        core = jnp.concatenate([own[None], rest])
-        for bit in bits(samp):
-            got = swap(core, "samp", samp, bit)
-            core = core + jnp.stack([got[d ^ bit] for d in range(samp)])
+        core = over_rest(own, over_groups(halved(rest)))
         other = swap(core, "space", space, 1)
         first = lax.axis_index("space") % 2 == 0
         core = jnp.concatenate([jnp.where(first, core, other), jnp.where(first, other, core)], axis=1)

time: 53.2 us -> 54 us (1.015)
  starting transfers between devices: 17.5 us -> 18.2 us
    ppermute x0 -> x1, starting transfers between devices: none -> 2.51 us  [swap_both(): return lax.ppermute(value, ('space', 'samp'), perm)]
    ppermute x11 -> x14, starting transfers between devices: 17.5 us -> 15.7 us  [swap(): return lax.ppermute(value, axis, [(i, i ^ bit) for i in range(size)])]
    ppermute x0 -> x1, waiting for transfers between devices: none -> 0.55 us  [swap_both(): return lax.ppermute(value, ('space', 'samp'), perm)]
    ppermute x11 -> x14, waiting for transfers between devices: 23 us -> 22.7 us  [swap(): return lax.ppermute(value, axis, [(i, i ^ bit) for i in range(size)])]
  transfers between devices with their start and end apart: 11 -> 15, of which waited for: 11 -> 14; matrix products, arithmetic and copies ran while one was open for 0% -> 0% of each run, Pallas kernels for 14% -> 14%
where the time goes in v3:
time: 54 us; the launch traced here: 53.8 us
  waiting for transfers between devices  23.2 us (43%)
  starting transfers between devices  18.2 us (34%)
  Pallas kernels  12.1 us (22%)
    ppermute x14, waiting for transfers between devices, swap(): return lax.ppermute(value, axis, [(i, i ^ bit) for i in range(size)])  22.7 us
    ppermute x14, starting transfers between devices, swap(): return lax.ppermute(value, axis, [(i, i ^ bit) for i in range(size)])  15.7 us
    pallas_call x1, Pallas kernels, shards(): pl.pallas_call(functools.partial(first_kernel, tile), out_shape=(on_chip(...  7.27 us
    pallas_call x1, Pallas kernels, shards(): pl.pallas_call(functools.partial(last_kernel, tile, samp), out_shape=jax....  4.12 us
    ppermute x1, starting transfers between devices, swap_both(): return lax.ppermute(value, ('space', 'samp'), perm)  2.51 us
  transfers between devices with their start and end apart: 15, of which 14 were waited for; matrix products, arithmetic and copies ran while one was open for 0% of the time, Pallas kernels for 14%

profile of v3, /device:TPU:0, one launch (start us, length us, event | category | flops | bytes accessed | tf_op | source)
XLA Modules:
  0.0 53.8 jit_solution(1766721782448838179)
XLA Ops:
  0.0 0.0 copy-start
  0.0 3.0 %collective-permute-start.5 = (f32[128,2048]{1,0:T(8,128)}, f32[128,2048]{1,0:T(8,128)S(1)}, u32[]{:S(2)}, u32[]{:S(2)}) collective-permute-start(f32[128,2048]{1,0:T(8,128)} %b_hbm.1), channel_id=1, source_target_pairs={{0,1},{1,0},{2,3},{3,2},{4,5},{5,4},{6,7},{7,6},{8,9},{9,8},{10,11... | collective-permute-start | bytes 3145736 | tf_op jit(solution)/shard_map/ppermute | solution.py:15
  3.0 7.3 %first.1 = (f32[4,256,2048]{2,1,0:T(8,128)S(1)}, bf16[2,256,2048]{2,1,0:T(8,128)(2,1)S(1)}, bf16[2,128,2048]{2,1,0:T(8,128)(2,1)S(1)}, f32[256,128]{1,0:T(8,128)S(1)}) custom-call(f32[4,256,2048]{2,1,0:T(8,128)} %x_hbm.1, f32[64,256]{1,0:T(8,128)} %bitcast.13, f32[128,2048]{1,0:T(8,128)} %b_hbm.1), custom_call_target="tpu_custom_call" | custom-call | flops 805306368 | bytes 8388608 | tf_op jit(solution)/shard_map/first/pallas_call | solution.py:197
  10.3 0.1 collective-permute-start
  10.3 1.2 %collective-permute-done = f32[128,128]{1,0:T(8,128)S(1)} collective-permute-done((f32[128,128]{1,0:T(8,128)S(1)}, f32[128,128]{1,0:T(8,128)S(1)}, u32[]{:S(2)}, u32[]{:S(2)}) %collective-permute-start) | collective-permute-done | bytes 65568 | tf_op jit(solution)/shard_map/ppermute | solution.py:15
  11.6 1.6 %collective-permute-start.3 = (f32[128,128]{1,0:T(8,128)S(1)}, f32[128,128]{1,0:T(8,128)S(1)}, u32[]{:S(2)}, u32[]{:S(2)}) collective-permute-start(f32[128,128]{1,0:T(8,128)S(1)} %select_add_fusion.1), channel_id=1, source_target_pairs={{0,8},{2,10},{4,12},{6,14},{8,0},{10,2},{12,4},{14,6},{16,24},{18,... | collective-permute-start | bytes 196616 | tf_op jit(solution)/shard_map/ppermute | solution.py:15
  13.2 2.5 %collective-permute-start.2 = (f32[128,128]{1,0:T(8,128)S(1)}, f32[128,128]{1,0:T(8,128)S(1)}, u32[]{:S(2)}, u32[]{:S(2)}) collective-permute-start(f32[128,128]{1,0:T(8,128)S(1)} %select_add_fusion.1), channel_id=1, source_target_pairs={{0,24},{2,26},{4,28},{6,30},{8,16},{10,18},{12,20},{14,22},{16,8},... | collective-permute-start | bytes 196616 | tf_op jit(solution)/shard_map/ppermute | solution.py:15
  15.7 0.1 collective-permute-start.1
  15.8 0.1 collective-permute-done.3
  15.9 4.0 %collective-permute-done.2 = f32[128,128]{1,0:T(8,128)S(1)} collective-permute-done((f32[128,128]{1,0:T(8,128)S(1)}, f32[128,128]{1,0:T(8,128)S(1)}, u32[]{:S(2)}, u32[]{:S(2)}) %collective-permute-start.2) | collective-permute-done | bytes 65568 | tf_op jit(solution)/shard_map/ppermute | solution.py:15
  19.9 2.4 %collective-permute-done.1 = f32[128,128]{1,0:T(8,128)S(1)} collective-permute-done((f32[128,128]{1,0:T(8,128)S(1)}, f32[128,128]{1,0:T(8,128)S(1)}, u32[]{:S(2)}, u32[]{:S(2)}) %collective-permute-start.1) | collective-permute-done | bytes 65568 | tf_op jit(solution)/shard_map/ppermute | solution.py:15
  22.3 1.6 %collective-permute-start.4 = (f32[128,128]{1,0:T(8,128)S(1)}, f32[128,128]{1,0:T(8,128)S(1)}, u32[]{:S(2)}, u32[]{:S(2)}) collective-permute-start(f32[128,128]{1,0:T(8,128)S(1)} %add_add_fusion.1), channel_id=1, source_target_pairs={{0,4},{2,6},{4,0},{6,2},{8,12},{10,14},{12,8},{14,10},{16,20},{18,... | collective-permute-start | bytes 196616 | tf_op jit(solution)/shard_map/ppermute | solution.py:15
  23.9 2.7 %collective-permute-done.4 = f32[128,128]{1,0:T(8,128)S(1)} collective-permute-done((f32[128,128]{1,0:T(8,128)S(1)}, f32[128,128]{1,0:T(8,128)S(1)}, u32[]{:S(2)}, u32[]{:S(2)}) %collective-permute-start.4) | collective-permute-done | bytes 65568 | tf_op jit(solution)/shard_map/ppermute | solution.py:15
  26.7 0.0 collective-permute-done.5.refs_0_
  26.7 0.7 %second.1 = (f32[1,256,128]{2,1,0:T(8,128)S(1)}, bf16[2,128,2048]{2,1,0:T(8,128)(2,1)S(1)}) custom-call(f32[128,2048]{1,0:T(8,128)S(1)} %collective-permute-done.5.refs_0_, bf16[2,256,2048]{2,1,0:T(8,128)(2,1)S(1)} %get-tuple-element.12.refs_1_, f32[128,128]{1,0:T(8,128)S(1)} %add.56.refs_2_), custom_call_target="tpu_custom_call" | custom-call | flops 402653184 | tf_op jit(solution)/shard_map/second/pallas_call | solution.py:219
  27.4 0.1 collective-permute-start.6
  27.5 1.2 %collective-permute-done.6 = f32[1,128,128]{2,1,0:T(8,128)S(1)} collective-permute-done((f32[1,128,128]{2,1,0:T(8,128)S(1)}, f32[1,128,128]{2,1,0:T(8,128)S(1)}, u32[]{:S(2)}, u32[]{:S(2)}) %collective-permute-start.6) | collective-permute-done | bytes 65568 | tf_op jit(solution)/shard_map/ppermute | solution.py:15
  28.8 1.6 %collective-permute-start.9 = (f32[1,128,128]{2,1,0:T(8,128)S(1)}, f32[1,128,128]{2,1,0:T(8,128)S(1)}, u32[]{:S(2)}, u32[]{:S(2)}) collective-permute-start(f32[1,128,128]{2,1,0:T(8,128)S(1)} %select_add_fusion), channel_id=1, source_target_pairs={{0,8},{2,10},{4,12},{6,14},{8,0},{10,2},{12,4},{14,6},{16,24},{18,... | collective-permute-start | bytes 196616 | tf_op jit(solution)/shard_map/ppermute | solution.py:15
  30.3 2.5 %collective-permute-start.8 = (f32[1,128,128]{2,1,0:T(8,128)S(1)}, f32[1,128,128]{2,1,0:T(8,128)S(1)}, u32[]{:S(2)}, u32[]{:S(2)}) collective-permute-start(f32[1,128,128]{2,1,0:T(8,128)S(1)} %select_add_fusion), channel_id=1, source_target_pairs={{0,24},{2,26},{4,28},{6,30},{8,16},{10,18},{12,20},{14,22},{16,8},... | collective-permute-start | bytes 196616 | tf_op jit(solution)/shard_map/ppermute | solution.py:15
  32.8 0.1 collective-permute-start.7
  32.9 0.2 collective-permute-done.9
  33.1 3.9 %collective-permute-done.8 = f32[1,128,128]{2,1,0:T(8,128)S(1)} collective-permute-done((f32[1,128,128]{2,1,0:T(8,128)S(1)}, f32[1,128,128]{2,1,0:T(8,128)S(1)}, u32[]{:S(2)}, u32[]{:S(2)}) %collective-permute-start.8) | collective-permute-done | bytes 65568 | tf_op jit(solution)/shard_map/ppermute | solution.py:15
  37.0 2.4 %collective-permute-done.7 = f32[1,128,128]{2,1,0:T(8,128)S(1)} collective-permute-done((f32[1,128,128]{2,1,0:T(8,128)S(1)}, f32[1,128,128]{2,1,0:T(8,128)S(1)}, u32[]{:S(2)}, u32[]{:S(2)}) %collective-permute-start.7) | collective-permute-done | bytes 65568 | tf_op jit(solution)/shard_map/ppermute | solution.py:15
  39.4 2.5 %collective-permute-start.11 = (f32[1,128,128]{2,1,0:T(8,128)S(1)}, f32[1,128,128]{2,1,0:T(8,128)S(1)}, u32[]{:S(2)}, u32[]{:S(2)}) collective-permute-start(f32[1,128,128]{2,1,0:T(8,128)S(1)} %add_add_fusion), channel_id=1, source_target_pairs={{0,5},{1,4},{2,7},{3,6},{4,1},{5,0},{6,3},{7,2},{8,13},{9,12},{10,... | collective-permute-start | bytes 196616 | tf_op jit(solution)/shard_map/ppermute | solution.py:26
  41.9 0.5 collective-permute-start.10
  42.4 1.5 %collective-permute-start.13 = (f32[128,128]{1,0:T(8,128)S(1)}, f32[128,128]{1,0:T(8,128)S(1)}, u32[]{:S(2)}, u32[]{:S(2)}) collective-permute-start(f32[128,128]{1,0:T(8,128)S(1)} %add.56.refs_2_), channel_id=1, source_target_pairs={{0,1},{1,0},{2,3},{3,2},{4,5},{5,4},{6,7},{7,6},{8,9},{9,8},{10,11... | collective-permute-start | bytes 196616 | tf_op jit(solution)/shard_map/ppermute | solution.py:15
  43.9 0.5 collective-permute-start.12
  44.4 0.6 %collective-permute-done.11 = f32[1,128,128]{2,1,0:T(8,128)S(1)} collective-permute-done((f32[1,128,128]{2,1,0:T(8,128)S(1)}, f32[1,128,128]{2,1,0:T(8,128)S(1)}, u32[]{:S(2)}, u32[]{:S(2)}) %collective-permute-start.11) | collective-permute-done | bytes 65568 | tf_op jit(solution)/shard_map/ppermute | solution.py:26
  45.0 1.8 %collective-permute-done.10 = f32[1,128,128]{2,1,0:T(8,128)S(1)} collective-permute-done((f32[1,128,128]{2,1,0:T(8,128)S(1)}, f32[1,128,128]{2,1,0:T(8,128)S(1)}, u32[]{:S(2)}, u32[]{:S(2)}) %collective-permute-start.10) | collective-permute-done | bytes 65568 | tf_op jit(solution)/shard_map/ppermute | solution.py:15
  46.8 0.7 %collective-permute-done.13 = f32[128,128]{1,0:T(8,128)S(1)} collective-permute-done((f32[128,128]{1,0:T(8,128)S(1)}, f32[128,128]{1,0:T(8,128)S(1)}, u32[]{:S(2)}, u32[]{:S(2)}) %collective-permute-start.13) | collective-permute-done | bytes 65568 | tf_op jit(solution)/shard_map/ppermute | solution.py:15
  47.5 0.7 %collective-permute-done.12 = f32[1,128,128]{2,1,0:T(8,128)S(1)} collective-permute-done((f32[1,128,128]{2,1,0:T(8,128)S(1)}, f32[1,128,128]{2,1,0:T(8,128)S(1)}, u32[]{:S(2)}, u32[]{:S(2)}) %collective-permute-start.12) | collective-permute-done | bytes 65568 | tf_op jit(solution)/shard_map/ppermute | solution.py:15
  48.2 0.1 collective-permute-start.14
  48.3 1.3 %collective-permute-done.14 = f32[2,128,128]{2,1,0:T(8,128)S(1)} collective-permute-done((f32[2,128,128]{2,1,0:T(8,128)S(1)}, f32[2,128,128]{2,1,0:T(8,128)S(1)}, u32[]{:S(2)}, u32[]{:S(2)}) %collective-permute-start.14) | collective-permute-done | bytes 131104 | tf_op jit(solution)/shard_map/ppermute | solution.py:15
  49.7 0.0 copy-done
  49.7 4.1 %last.1 = f32[4,256,2048]{2,1,0:T(8,128)} custom-call(f32[2,256,128]{2,1,0:T(8,128)S(1)} %pad_maximum_fusion.refs_0_, f32[64,256]{1,0:T(8,128)S(1)} %bitcast.14, f32[4,256,2048]{2,1,0:T(8,128)S(1)} %get-tuple-element.14.refs_2_, bf16[2,128,2048]{2,1,0:T(8,128)(2,1)S(1)} %get-tuple-element.15.refs_3_, bf16[2,128,2048]{2,1,0:T(8,128)(2,1)S(1)} %get-tuple-element.16.refs_4_), custom_call_target="tpu_custom_call" | custom-call | flops 1610612736 | bytes 8388608 | tf_op jit(solution)/shard_map/last/pallas_call | solution.py:236
  (12 shorter events, 0.2 us)
Async XLA Ops:
  0.0 49.7 %copy-start = (f32[256,64]{0,1:T(8,128)S(1)}, f32[256,64]{0,1:T(8,128)}, u32[]{:S(2)}) copy-start(f32[256,64]{0,1:T(8,128)} %param.5) | copy-start | bytes 196612
  0.0 26.7 %collective-permute-start.5 = (f32[128,2048]{1,0:T(8,128)}, f32[128,2048]{1,0:T(8,128)S(1)}, u32[]{:S(2)}, u32[]{:S(2)}) collective-permute-start(f32[128,2048]{1,0:T(8,128)} %b_hbm.1), channel_id=1, source_target_pairs={{0,1},{1,0},{2,3},{3,2},{4,5},{5,4},{6,7},{7,6},{8,9},{9,8},{10,11... | collective-permute-start | bytes 3145736 | tf_op jit(solution)/shard_map/ppermute | solution.py:15
  10.3 1.3 %collective-permute-start = (f32[128,128]{1,0:T(8,128)S(1)}, f32[128,128]{1,0:T(8,128)S(1)}, u32[]{:S(2)}, u32[]{:S(2)}) collective-permute-start(f32[128,128]{1,0:T(8,128)S(1)} %slice_select_fusion.1), channel_id=1, source_target_pairs={{0,2},{2,0},{4,6},{6,4},{8,10},{10,8},{12,14},{14,12},{16,18},{18,... | collective-permute-start | bytes 196616 | tf_op jit(solution)/shard_map/ppermute | solution.py:15
  11.6 4.3 %collective-permute-start.3 = (f32[128,128]{1,0:T(8,128)S(1)}, f32[128,128]{1,0:T(8,128)S(1)}, u32[]{:S(2)}, u32[]{:S(2)}) collective-permute-start(f32[128,128]{1,0:T(8,128)S(1)} %select_add_fusion.1), channel_id=1, source_target_pairs={{0,8},{2,10},{4,12},{6,14},{8,0},{10,2},{12,4},{14,6},{16,24},{18,... | collective-permute-start | bytes 196616 | tf_op jit(solution)/shard_map/ppermute | solution.py:15
  13.2 6.7 %collective-permute-start.2 = (f32[128,128]{1,0:T(8,128)S(1)}, f32[128,128]{1,0:T(8,128)S(1)}, u32[]{:S(2)}, u32[]{:S(2)}) collective-permute-start(f32[128,128]{1,0:T(8,128)S(1)} %select_add_fusion.1), channel_id=1, source_target_pairs={{0,24},{2,26},{4,28},{6,30},{8,16},{10,18},{12,20},{14,22},{16,8},... | collective-permute-start | bytes 196616 | tf_op jit(solution)/shard_map/ppermute | solution.py:15
  15.7 6.6 %collective-permute-start.1 = (f32[128,128]{1,0:T(8,128)S(1)}, f32[128,128]{1,0:T(8,128)S(1)}, u32[]{:S(2)}, u32[]{:S(2)}) collective-permute-start(f32[128,128]{1,0:T(8,128)S(1)} %select_add_fusion.1), channel_id=1, source_target_pairs={{0,16},{2,18},{4,20},{6,22},{8,24},{10,26},{12,28},{14,30},{16,0},... | collective-permute-start | bytes 196616 | tf_op jit(solution)/shard_map/ppermute | solution.py:15
  22.3 4.3 %collective-permute-start.4 = (f32[128,128]{1,0:T(8,128)S(1)}, f32[128,128]{1,0:T(8,128)S(1)}, u32[]{:S(2)}, u32[]{:S(2)}) collective-permute-start(f32[128,128]{1,0:T(8,128)S(1)} %add_add_fusion.1), channel_id=1, source_target_pairs={{0,4},{2,6},{4,0},{6,2},{8,12},{10,14},{12,8},{14,10},{16,20},{18,... | collective-permute-start | bytes 196616 | tf_op jit(solution)/shard_map/ppermute | solution.py:15
  27.4 1.3 %collective-permute-start.6 = (f32[1,128,128]{2,1,0:T(8,128)S(1)}, f32[1,128,128]{2,1,0:T(8,128)S(1)}, u32[]{:S(2)}, u32[]{:S(2)}) collective-permute-start(f32[1,128,128]{2,1,0:T(8,128)S(1)} %slice_select_fusion), channel_id=1, source_target_pairs={{0,2},{2,0},{4,6},{6,4},{8,10},{10,8},{12,14},{14,12},{16,18},{18,... | collective-permute-start | bytes 196616 | tf_op jit(solution)/shard_map/ppermute | solution.py:15
  28.8 4.3 %collective-permute-start.9 = (f32[1,128,128]{2,1,0:T(8,128)S(1)}, f32[1,128,128]{2,1,0:T(8,128)S(1)}, u32[]{:S(2)}, u32[]{:S(2)}) collective-permute-start(f32[1,128,128]{2,1,0:T(8,128)S(1)} %select_add_fusion), channel_id=1, source_target_pairs={{0,8},{2,10},{4,12},{6,14},{8,0},{10,2},{12,4},{14,6},{16,24},{18,... | collective-permute-start | bytes 196616 | tf_op jit(solution)/shard_map/ppermute | solution.py:15
  30.3 6.7 %collective-permute-start.8 = (f32[1,128,128]{2,1,0:T(8,128)S(1)}, f32[1,128,128]{2,1,0:T(8,128)S(1)}, u32[]{:S(2)}, u32[]{:S(2)}) collective-permute-start(f32[1,128,128]{2,1,0:T(8,128)S(1)} %select_add_fusion), channel_id=1, source_target_pairs={{0,24},{2,26},{4,28},{6,30},{8,16},{10,18},{12,20},{14,22},{16,8},... | collective-permute-start | bytes 196616 | tf_op jit(solution)/shard_map/ppermute | solution.py:15
  32.8 6.6 %collective-permute-start.7 = (f32[1,128,128]{2,1,0:T(8,128)S(1)}, f32[1,128,128]{2,1,0:T(8,128)S(1)}, u32[]{:S(2)}, u32[]{:S(2)}) collective-permute-start(f32[1,128,128]{2,1,0:T(8,128)S(1)} %select_add_fusion), channel_id=1, source_target_pairs={{0,16},{2,18},{4,20},{6,22},{8,24},{10,26},{12,28},{14,30},{16,0},... | collective-permute-start | bytes 196616 | tf_op jit(solution)/shard_map/ppermute | solution.py:15
  39.4 5.6 %collective-permute-start.11 = (f32[1,128,128]{2,1,0:T(8,128)S(1)}, f32[1,128,128]{2,1,0:T(8,128)S(1)}, u32[]{:S(2)}, u32[]{:S(2)}) collective-permute-start(f32[1,128,128]{2,1,0:T(8,128)S(1)} %add_add_fusion), channel_id=1, source_target_pairs={{0,5},{1,4},{2,7},{3,6},{4,1},{5,0},{6,3},{7,2},{8,13},{9,12},{10,... | collective-permute-start | bytes 196616 | tf_op jit(solution)/shard_map/ppermute | solution.py:26
  41.9 4.9 %collective-permute-start.10 = (f32[1,128,128]{2,1,0:T(8,128)S(1)}, f32[1,128,128]{2,1,0:T(8,128)S(1)}, u32[]{:S(2)}, u32[]{:S(2)}) collective-permute-start(f32[1,128,128]{2,1,0:T(8,128)S(1)} %add_add_fusion), channel_id=1, source_target_pairs={{0,1},{1,0},{2,3},{3,2},{4,5},{5,4},{6,7},{7,6},{8,9},{9,8},{10,11... | collective-permute-start | bytes 196616 | tf_op jit(solution)/shard_map/ppermute | solution.py:15
  42.4 5.0 %collective-permute-start.13 = (f32[128,128]{1,0:T(8,128)S(1)}, f32[128,128]{1,0:T(8,128)S(1)}, u32[]{:S(2)}, u32[]{:S(2)}) collective-permute-start(f32[128,128]{1,0:T(8,128)S(1)} %add.56.refs_2_), channel_id=1, source_target_pairs={{0,1},{1,0},{2,3},{3,2},{4,5},{5,4},{6,7},{7,6},{8,9},{9,8},{10,11... | collective-permute-start | bytes 196616 | tf_op jit(solution)/shard_map/ppermute | solution.py:15
  43.9 4.3 %collective-permute-start.12 = (f32[1,128,128]{2,1,0:T(8,128)S(1)}, f32[1,128,128]{2,1,0:T(8,128)S(1)}, u32[]{:S(2)}, u32[]{:S(2)}) collective-permute-start(f32[1,128,128]{2,1,0:T(8,128)S(1)} %add_add_fusion), channel_id=1, source_target_pairs={{0,4},{2,6},{4,0},{6,2},{8,12},{10,14},{12,8},{14,10},{16,20},{18,... | collective-permute-start | bytes 196616 | tf_op jit(solution)/shard_map/ppermute | solution.py:15
  48.2 1.4 %collective-permute-start.14 = (f32[2,128,128]{2,1,0:T(8,128)S(1)}, f32[2,128,128]{2,1,0:T(8,128)S(1)}, u32[]{:S(2)}, u32[]{:S(2)}) collective-permute-start(f32[2,128,128]{2,1,0:T(8,128)S(1)} %pad_maximum_fusion.1), channel_id=1, source_target_pairs={{0,2},{2,0},{4,6},{6,4},{8,10},{10,8},{12,14},{14,12},{16,18},{18,... | collective-permute-start | bytes 393224 | tf_op jit(solution)/shard_map/ppermute | solution.py:15

commit v4 on v3

--- a/solution.py
+++ b/solution.py
@@ -9,6 +9,7 @@
 
 
 MIB = 1 << 20
+AHEAD = 2
 
 
 def swap(value, axis, size, bit):
@@ -26,9 +27,9 @@
     return lax.ppermute(value, ("space", "samp"), perm)
 
 
-def tile_of(columns):
+def tile_of(columns, most=512):
     for tile in (512, 256, 128):
-        if columns % tile == 0:
+        if tile <= most and columns % tile == 0:
             return tile
     return columns
 
@@ -53,7 +54,7 @@
     return both[:, :rank] + both[:, rank:] + mul_t(y_low, high), high, low
 
 
-def first_kernel(tile, x_hbm, s_ref, b_hbm, x_ref, y_ref, bs_ref, part_ref, b_ref, sems, b_sem):
+def first_kernel(tile, x_hbm, s_ref, b_hbm, x_ref, y_ref, bs_ref, part_ref, spread_ref, b_ref, sems, b_sem):
     snaps, _, columns = x_ref.shape
     rank = s_ref.shape[0]
     steps = columns // tile
@@ -64,15 +65,19 @@
     b_copy = pltpu.make_async_copy(b_hbm, b_ref, b_sem)
     copies[0].start()
     b_copy.start()
-    for copy in copies[1:]:
+    for copy in copies[1:AHEAD]:
         copy.start()
     s_high, s_low = split(s_ref[...])
     s_both = jnp.concatenate([s_high, s_low], axis=0)
+    t_high, t_low = split(s_ref[...].T)
+    spread_ref[...] = jnp.concatenate([t_high, t_low, t_high], axis=1)
     for j in range(steps):
         cols = pl.ds(j * tile, tile)
         copies[j].wait()
         if j == 0:
             b_copy.wait()
+        if j + AHEAD < steps:
+            copies[j + AHEAD].start()
         for t in range(snaps):
             x_high, x_low = split(x_ref[t, :, cols])
             both = mul(s_both, x_high)
@@ -104,29 +109,38 @@
                 part_ref[d] += total
 
 
-def last_kernel(tile, parts, *refs):
+def last_kernel(tile, parts, mine, *refs):
     core_ref, s_ref, x_ref = refs[:3]
-    bs_refs, out_hbm, out_ref, sems = refs[3:3 + parts], refs[3 + parts], refs[4 + parts], refs[5 + parts]
-    snaps, _, columns = x_ref.shape
-    rank = s_ref.shape[0]
-    s_high, s_low = split(s_ref[...].T)
-    s_all = jnp.concatenate([s_high, s_low, s_high], axis=1)
+    bs_refs = refs[3:3 + parts]
+    out_hbm, out_ref, w_ref, sems = refs[-4:]
+    half, _, columns = out_ref.shape
+    rank = s_ref.shape[1] // 3
+    core = lax.axis_index("space") % 2
+    start = half * (core if mine else 1 - core)
     c_high, c_low = split(jnp.concatenate([core_ref[d] for d in range(parts)], axis=1))
     c_both = jnp.concatenate([c_high, c_low], axis=0)
     wide = c_high.shape[0]
-    copies = []
-    for j in range(columns // tile):
+    steps = columns // tile
+
+    def weigh(j):
         cols = pl.ds(j * tile, tile)
         b_high = jnp.concatenate([b[0, :, cols] for b in bs_refs], axis=0)
         b_low = jnp.concatenate([b[1, :, cols] for b in bs_refs], axis=0)
         both = mul(c_both, b_high)
-        weight = both[:wide] + both[wide:] + mul(c_high, b_low)
-        w_high, w_low = split(weight)
-        for t in range(snaps):
-            high, low = w_high[t * rank:(t + 1) * rank], w_low[t * rank:(t + 1) * rank]
-            removed = mul(s_all, jnp.concatenate([high, high, low], axis=0))
-            out_ref[t, :, cols] = x_ref[t, :, cols] - removed
-        copies.append(pltpu.make_async_copy(out_ref.at[:, :, cols], out_hbm.at[:, :, cols], sems.at[j]))
+        w_ref[0, :, cols], w_ref[1, :, cols] = split(both[:wide] + both[wide:] + mul(c_high, b_low))
+
+    copies = []
+    weigh(0)
+    for j in range(steps):
+        if j + 1 < steps:
+            weigh(j + 1)
+        cols = pl.ds(j * tile, tile)
+        for t in range(half):
+            high, low = w_ref[0, t * rank:(t + 1) * rank, cols], w_ref[1, t * rank:(t + 1) * rank, cols]
+            removed = mul(s_ref[...], jnp.concatenate([high, high, low], axis=0))
+            out_ref[t, :, cols] = x_ref[start + t, :, cols] - removed
+        copies.append(pltpu.make_async_copy(
+            out_ref.at[:, :, cols], out_hbm.at[pl.ds(start, half), :, cols], sems.at[j]))
         copies[-1].start()
     for copy in copies:
         copy.wait()
@@ -194,16 +208,17 @@
         others = [swap(space_basis, "samp", samp, d) for d in range(1, samp)]
         mixer = sample_basis.T
         flops = 6 * wide * samples * columns
-        x_chip, mixed, own_split, own = pl.pallas_call(
+        x_chip, mixed, own_split, own, spreader = pl.pallas_call(
             functools.partial(first_kernel, tile),
             out_shape=(
                 on_chip(snapshots.shape, jnp.float32),
                 on_chip((2, wide, columns), jnp.bfloat16),
                 on_chip((2, basis_rows, columns), jnp.bfloat16),
                 on_chip((wide, basis_rows), jnp.float32),
+                on_chip((samples, 3 * rank), jnp.bfloat16),
             ),
             in_specs=[HBM, VMEM, HBM],
-            out_specs=(VMEM,) * 4,
+            out_specs=(VMEM,) * 5,
             scratch_shapes=[
                 pltpu.VMEM((basis_rows, columns), jnp.float32),
                 pltpu.SemaphoreType.DMA((steps,)),
@@ -231,21 +246,26 @@
         )(*others, mixed, own)
         core = over_rest(own, over_groups(halved(rest)))
         other = swap(core, "space", space, 1)
-        first = lax.axis_index("space") % 2 == 0
-        core = jnp.concatenate([jnp.where(first, core, other), jnp.where(first, other, core)], axis=1)
-        return pl.pallas_call(
-            functools.partial(last_kernel, tile, samp),
-            out_shape=jax.ShapeDtypeStruct(snapshots.shape, jnp.float32),
-            in_specs=[VMEM] * (3 + samp),
-            out_specs=ANY,
-            scratch_shapes=[
-                pltpu.VMEM(snapshots.shape, jnp.float32),
-                pltpu.SemaphoreType.DMA((steps,)),
-            ],
-            compiler_params=pltpu.CompilerParams(vmem_limit_bytes=20 * MIB),
-            cost_estimate=pl.CostEstimate(flops=2 * flops, bytes_accessed=snapshots.size * 4, transcendentals=0),
-            name="last",
-        )(core, mixer, x_chip, own_split, *rest_splits)
+
+        def last(mine, part, *out):
+            fine = tile_of(columns, 256)
+            return pl.pallas_call(
+                functools.partial(last_kernel, fine, samp, mine),
+                out_shape=jax.ShapeDtypeStruct(snapshots.shape, jnp.float32),
+                in_specs=[VMEM] * (3 + samp) + [ANY] * len(out),
+                out_specs=ANY,
+                input_output_aliases={3 + samp: 0} if out else {},
+                scratch_shapes=[
+                    pltpu.VMEM((snaps // 2, samples, columns), jnp.float32),
+                    pltpu.VMEM((2, wide // 2, columns), jnp.bfloat16),
+                    pltpu.SemaphoreType.DMA((columns // fine,)),
+                ],
+                compiler_params=pltpu.CompilerParams(vmem_limit_bytes=20 * MIB),
+                cost_estimate=pl.CostEstimate(flops=flops, bytes_accessed=snapshots.size * 2, transcendentals=0),
+                name="last_mine" if mine else "last_other",
+            )(part, spreader, x_chip, own_split, *rest_splits, *out)
+
+        return last(False, other, last(True, core))
 
     return jax.shard_map(
         shards,

time: 54 us -> 53.6 us (level)
  waiting for transfers between devices: 23.2 us -> 22.6 us
    pallas_call x1, Pallas kernels: 7.27 us -> 6.22 us  [shards(): pl.pallas_call(functools.partial(first_kernel, tile), out_shape=(on_chip(...]
    pallas_call x1 -> x2, Pallas kernels: 4.12 us -> 5.08 us  [last(): pl.pallas_call(functools.partial(last_kernel, fine, samp, mine), out_shap...]
    ppermute x14, waiting for transfers between devices: 22.7 us -> 22.1 us  [swap(): return lax.ppermute(value, axis, [(i, i ^ bit) for i in range(size)])]
  transfers between devices with their start and end apart: 15 -> 15, of which waited for: 14 -> 13; matrix products, arithmetic and copies ran while one was open for 0% -> 0% of each run, Pallas kernels for 14% -> 16%
where the time goes in v4:
time: 53.6 us; the launch traced here: 53.4 us
  waiting for transfers between devices  22.6 us (42%)
  starting transfers between devices  18.5 us (35%)
  Pallas kernels  12 us (22%)
    ppermute x14, waiting for transfers between devices, swap(): return lax.ppermute(value, axis, [(i, i ^ bit) for i in range(size)])  22.1 us
    ppermute x14, starting transfers between devices, swap(): return lax.ppermute(value, axis, [(i, i ^ bit) for i in range(size)])  16 us
    pallas_call x1, Pallas kernels, shards(): pl.pallas_call(functools.partial(first_kernel, tile), out_shape=(on_chip(...  6.22 us
    pallas_call x2, Pallas kernels, last(): pl.pallas_call(functools.partial(last_kernel, fine, samp, mine), out_shap...  5.08 us
    ppermute x1, starting transfers between devices, swap_both(): return lax.ppermute(value, ('space', 'samp'), perm)  2.51 us
  transfers between devices with their start and end apart: 15, of which 13 were waited for; matrix products, arithmetic and copies ran while one was open for 0% of the time, Pallas kernels for 16%

profile of v4, /device:TPU:0, one launch (start us, length us, event | category | flops | bytes accessed | tf_op | source)
XLA Modules:
  0.0 53.4 jit_solution(12096310829220468015)
XLA Ops:
  0.0 3.0 %collective-permute-start.5 = (f32[128,2048]{1,0:T(8,128)}, f32[128,2048]{1,0:T(8,128)S(1)}, u32[]{:S(2)}, u32[]{:S(2)}) collective-permute-start(f32[128,2048]{1,0:T(8,128)} %b_hbm.1), channel_id=1, source_target_pairs={{0,1},{1,0},{2,3},{3,2},{4,5},{5,4},{6,7},{7,6},{8,9},{9,8},{10,11... | collective-permute-start | bytes 3145736 | tf_op jit(solution)/shard_map/ppermute | solution.py:16
  3.0 6.2 %first.1 = (f32[4,256,2048]{2,1,0:T(8,128)S(1)}, bf16[2,256,2048]{2,1,0:T(8,128)(2,1)S(1)}, bf16[2,128,2048]{2,1,0:T(8,128)(2,1)S(1)}, f32[256,128]{1,0:T(8,128)S(1)}, bf16[256,192]{1,0:T(8,128)(2,1)S(1)}) custom-call(f32[4,256,2048]{2,1,0:T(8,128)} %x_hbm.1, f32[64,256]{1,0:T(8,128)} %bitcast.13, f32[128,2048]{1,0:T(8,128)} %b_hbm.1), custom_call_target="tpu_custom_call" | custom-call | flops 805306368 | bytes 8388608 | tf_op jit(solution)/shard_map/first/pallas_call | solution.py:211
  9.2 0.1 collective-permute-start
  9.3 1.2 %collective-permute-done = f32[128,128]{1,0:T(8,128)S(1)} collective-permute-done((f32[128,128]{1,0:T(8,128)S(1)}, f32[128,128]{1,0:T(8,128)S(1)}, u32[]{:S(2)}, u32[]{:S(2)}) %collective-permute-start) | collective-permute-done | bytes 65568 | tf_op jit(solution)/shard_map/ppermute | solution.py:16
  10.6 1.6 %collective-permute-start.3 = (f32[128,128]{1,0:T(8,128)S(1)}, f32[128,128]{1,0:T(8,128)S(1)}, u32[]{:S(2)}, u32[]{:S(2)}) collective-permute-start(f32[128,128]{1,0:T(8,128)S(1)} %select_add_fusion.1), channel_id=1, source_target_pairs={{0,8},{2,10},{4,12},{6,14},{8,0},{10,2},{12,4},{14,6},{16,24},{18,... | collective-permute-start | bytes 196616 | tf_op jit(solution)/shard_map/ppermute | solution.py:16
  12.2 2.5 %collective-permute-start.2 = (f32[128,128]{1,0:T(8,128)S(1)}, f32[128,128]{1,0:T(8,128)S(1)}, u32[]{:S(2)}, u32[]{:S(2)}) collective-permute-start(f32[128,128]{1,0:T(8,128)S(1)} %select_add_fusion.1), channel_id=1, source_target_pairs={{0,24},{2,26},{4,28},{6,30},{8,16},{10,18},{12,20},{14,22},{16,8},... | collective-permute-start | bytes 196616 | tf_op jit(solution)/shard_map/ppermute | solution.py:16
  14.7 0.1 collective-permute-start.1
  14.8 0.1 collective-permute-done.3
  14.9 4.0 %collective-permute-done.2 = f32[128,128]{1,0:T(8,128)S(1)} collective-permute-done((f32[128,128]{1,0:T(8,128)S(1)}, f32[128,128]{1,0:T(8,128)S(1)}, u32[]{:S(2)}, u32[]{:S(2)}) %collective-permute-start.2) | collective-permute-done | bytes 65568 | tf_op jit(solution)/shard_map/ppermute | solution.py:16
  18.9 2.4 %collective-permute-done.1 = f32[128,128]{1,0:T(8,128)S(1)} collective-permute-done((f32[128,128]{1,0:T(8,128)S(1)}, f32[128,128]{1,0:T(8,128)S(1)}, u32[]{:S(2)}, u32[]{:S(2)}) %collective-permute-start.1) | collective-permute-done | bytes 65568 | tf_op jit(solution)/shard_map/ppermute | solution.py:16
  21.3 1.6 %collective-permute-start.4 = (f32[128,128]{1,0:T(8,128)S(1)}, f32[128,128]{1,0:T(8,128)S(1)}, u32[]{:S(2)}, u32[]{:S(2)}) collective-permute-start(f32[128,128]{1,0:T(8,128)S(1)} %add_add_fusion.1), channel_id=1, source_target_pairs={{0,4},{2,6},{4,0},{6,2},{8,12},{10,14},{12,8},{14,10},{16,20},{18,... | collective-permute-start | bytes 196616 | tf_op jit(solution)/shard_map/ppermute | solution.py:16
  22.9 2.7 %collective-permute-done.4 = f32[128,128]{1,0:T(8,128)S(1)} collective-permute-done((f32[128,128]{1,0:T(8,128)S(1)}, f32[128,128]{1,0:T(8,128)S(1)}, u32[]{:S(2)}, u32[]{:S(2)}) %collective-permute-start.4) | collective-permute-done | bytes 65568 | tf_op jit(solution)/shard_map/ppermute | solution.py:16
  25.6 0.7 %collective-permute-done.5.refs_0_ = f32[128,2048]{1,0:T(8,128)S(1)} collective-permute-done((f32[128,2048]{1,0:T(8,128)}, f32[128,2048]{1,0:T(8,128)S(1)}, u32[]{:S(2)}, u32[]{:S(2)}) %collective-permute-start.5) | collective-permute-done | bytes 1048608 | tf_op jit(solution)/shard_map/ppermute | solution.py:16
  26.3 0.7 %second.1 = (f32[1,256,128]{2,1,0:T(8,128)S(1)}, bf16[2,128,2048]{2,1,0:T(8,128)(2,1)S(1)}) custom-call(f32[128,2048]{1,0:T(8,128)S(1)} %collective-permute-done.5.refs_0_, bf16[2,256,2048]{2,1,0:T(8,128)(2,1)S(1)} %get-tuple-element.13.refs_1_, f32[128,128]{1,0:T(8,128)S(1)} %add.55.refs_2_), custom_call_target="tpu_custom_call" | custom-call | flops 402653184 | tf_op jit(solution)/shard_map/second/pallas_call | solution.py:234
  27.1 0.1 collective-permute-start.6
  27.2 1.2 %collective-permute-done.6 = f32[1,128,128]{2,1,0:T(8,128)S(1)} collective-permute-done((f32[1,128,128]{2,1,0:T(8,128)S(1)}, f32[1,128,128]{2,1,0:T(8,128)S(1)}, u32[]{:S(2)}, u32[]{:S(2)}) %collective-permute-start.6) | collective-permute-done | bytes 65568 | tf_op jit(solution)/shard_map/ppermute | solution.py:16
  28.4 1.9 %collective-permute-start.9 = (f32[1,128,128]{2,1,0:T(8,128)S(1)}, f32[1,128,128]{2,1,0:T(8,128)S(1)}, u32[]{:S(2)}, u32[]{:S(2)}) collective-permute-start(f32[1,128,128]{2,1,0:T(8,128)S(1)} %select_add_fusion), channel_id=1, source_target_pairs={{0,8},{2,10},{4,12},{6,14},{8,0},{10,2},{12,4},{14,6},{16,24},{18,... | collective-permute-start | bytes 196616 | tf_op jit(solution)/shard_map/ppermute | solution.py:16
  30.3 2.5 %collective-permute-start.8 = (f32[1,128,128]{2,1,0:T(8,128)S(1)}, f32[1,128,128]{2,1,0:T(8,128)S(1)}, u32[]{:S(2)}, u32[]{:S(2)}) collective-permute-start(f32[1,128,128]{2,1,0:T(8,128)S(1)} %select_add_fusion), channel_id=1, source_target_pairs={{0,24},{2,26},{4,28},{6,30},{8,16},{10,18},{12,20},{14,22},{16,8},... | collective-permute-start | bytes 196616 | tf_op jit(solution)/shard_map/ppermute | solution.py:16
  32.8 0.1 collective-permute-start.7
  32.9 0.0 collective-permute-done.9
  32.9 4.1 %collective-permute-done.8 = f32[1,128,128]{2,1,0:T(8,128)S(1)} collective-permute-done((f32[1,128,128]{2,1,0:T(8,128)S(1)}, f32[1,128,128]{2,1,0:T(8,128)S(1)}, u32[]{:S(2)}, u32[]{:S(2)}) %collective-permute-start.8) | collective-permute-done | bytes 65568 | tf_op jit(solution)/shard_map/ppermute | solution.py:16
  37.0 2.4 %collective-permute-done.7 = f32[1,128,128]{2,1,0:T(8,128)S(1)} collective-permute-done((f32[1,128,128]{2,1,0:T(8,128)S(1)}, f32[1,128,128]{2,1,0:T(8,128)S(1)}, u32[]{:S(2)}, u32[]{:S(2)}) %collective-permute-start.7) | collective-permute-done | bytes 65568 | tf_op jit(solution)/shard_map/ppermute | solution.py:16
  39.4 2.5 %collective-permute-start.11 = (f32[1,128,128]{2,1,0:T(8,128)S(1)}, f32[1,128,128]{2,1,0:T(8,128)S(1)}, u32[]{:S(2)}, u32[]{:S(2)}) collective-permute-start(f32[1,128,128]{2,1,0:T(8,128)S(1)} %add_add_fusion), channel_id=1, source_target_pairs={{0,5},{1,4},{2,7},{3,6},{4,1},{5,0},{6,3},{7,2},{8,13},{9,12},{10,... | collective-permute-start | bytes 196616 | tf_op jit(solution)/shard_map/ppermute | solution.py:27
  41.9 0.5 %collective-permute-start.10 = (f32[1,128,128]{2,1,0:T(8,128)S(1)}, f32[1,128,128]{2,1,0:T(8,128)S(1)}, u32[]{:S(2)}, u32[]{:S(2)}) collective-permute-start(f32[1,128,128]{2,1,0:T(8,128)S(1)} %add_add_fusion), channel_id=1, source_target_pairs={{0,1},{1,0},{2,3},{3,2},{4,5},{5,4},{6,7},{7,6},{8,9},{9,8},{10,11... | collective-permute-start | bytes 196616 | tf_op jit(solution)/shard_map/ppermute | solution.py:16
  42.4 1.5 %collective-permute-start.13 = (f32[128,128]{1,0:T(8,128)S(1)}, f32[128,128]{1,0:T(8,128)S(1)}, u32[]{:S(2)}, u32[]{:S(2)}) collective-permute-start(f32[128,128]{1,0:T(8,128)S(1)} %add.55.refs_2_), channel_id=1, source_target_pairs={{0,1},{1,0},{2,3},{3,2},{4,5},{5,4},{6,7},{7,6},{8,9},{9,8},{10,11... | collective-permute-start | bytes 196616 | tf_op jit(solution)/shard_map/ppermute | solution.py:16
  43.9 0.5 collective-permute-start.12
  44.4 0.5 %collective-permute-done.11 = f32[1,128,128]{2,1,0:T(8,128)S(1)} collective-permute-done((f32[1,128,128]{2,1,0:T(8,128)S(1)}, f32[1,128,128]{2,1,0:T(8,128)S(1)}, u32[]{:S(2)}, u32[]{:S(2)}) %collective-permute-start.11) | collective-permute-done | bytes 65568 | tf_op jit(solution)/shard_map/ppermute | solution.py:27
  45.0 1.8 %collective-permute-done.10 = f32[1,128,128]{2,1,0:T(8,128)S(1)} collective-permute-done((f32[1,128,128]{2,1,0:T(8,128)S(1)}, f32[1,128,128]{2,1,0:T(8,128)S(1)}, u32[]{:S(2)}, u32[]{:S(2)}) %collective-permute-start.10) | collective-permute-done | bytes 65568 | tf_op jit(solution)/shard_map/ppermute | solution.py:16
  46.8 0.7 %collective-permute-done.13 = f32[128,128]{1,0:T(8,128)S(1)} collective-permute-done((f32[128,128]{1,0:T(8,128)S(1)}, f32[128,128]{1,0:T(8,128)S(1)}, u32[]{:S(2)}, u32[]{:S(2)}) %collective-permute-start.13) | collective-permute-done | bytes 65568 | tf_op jit(solution)/shard_map/ppermute | solution.py:16
  47.5 0.7 %collective-permute-done.12 = f32[1,128,128]{2,1,0:T(8,128)S(1)} collective-permute-done((f32[1,128,128]{2,1,0:T(8,128)S(1)}, f32[1,128,128]{2,1,0:T(8,128)S(1)}, u32[]{:S(2)}, u32[]{:S(2)}) %collective-permute-start.12) | collective-permute-done | bytes 65568 | tf_op jit(solution)/shard_map/ppermute | solution.py:16
  48.2 0.1 collective-permute-start.14
  48.3 2.5 %last_mine.1.refs_5_ = f32[4,256,2048]{2,1,0:T(8,128)} custom-call(f32[2,128,128]{2,1,0:T(8,128)S(1)} %pad_maximum_fusion.refs_0_, bf16[256,192]{1,0:T(8,128)(2,1)S(1)} %get-tuple-element.15.refs_1_, f32[4,256,2048]{2,1,0:T(8,128)S(1)} %get-tuple-element.16.refs_2_, bf16[2,128,2048]{2,1,0:T(8,128)(2,1)S(1)} %get-tuple-element.17.refs_3_, ...), custom_call_target="tpu_custom_call" | custom-call | flops 805306368 | bytes 4194304 | tf_op jit(solution)/shard_map/last_mine/pallas_call | solution.py:252
  50.8 0.0 collective-permute-done.14.refs_0_
  50.8 2.5 %last_other.1 = f32[4,256,2048]{2,1,0:T(8,128)} custom-call(f32[2,128,128]{2,1,0:T(8,128)S(1)} %collective-permute-done.14.refs_0_, bf16[256,192]{1,0:T(8,128)(2,1)S(1)} %get-tuple-element.15.refs_1_, f32[4,256,2048]{2,1,0:T(8,128)S(1)} %get-tuple-element.16.refs_2_, ...), custom_call_target="tpu_custom_call", output_to_operand_aliasing={{}: (5, {})} | custom-call | flops 805306368 | bytes 4194304 | tf_op jit(solution)/shard_map/last_other/pallas_call | solution.py:252
  (10 shorter events, 0.1 us)
Async XLA Ops:
  0.0 26.3 %collective-permute-start.5 = (f32[128,2048]{1,0:T(8,128)}, f32[128,2048]{1,0:T(8,128)S(1)}, u32[]{:S(2)}, u32[]{:S(2)}) collective-permute-start(f32[128,2048]{1,0:T(8,128)} %b_hbm.1), channel_id=1, source_target_pairs={{0,1},{1,0},{2,3},{3,2},{4,5},{5,4},{6,7},{7,6},{8,9},{9,8},{10,11... | collective-permute-start | bytes 3145736 | tf_op jit(solution)/shard_map/ppermute | solution.py:16
  9.2 1.3 %collective-permute-start = (f32[128,128]{1,0:T(8,128)S(1)}, f32[128,128]{1,0:T(8,128)S(1)}, u32[]{:S(2)}, u32[]{:S(2)}) collective-permute-start(f32[128,128]{1,0:T(8,128)S(1)} %slice_select_fusion.1), channel_id=1, source_target_pairs={{0,2},{2,0},{4,6},{6,4},{8,10},{10,8},{12,14},{14,12},{16,18},{18,... | collective-permute-start | bytes 196616 | tf_op jit(solution)/shard_map/ppermute | solution.py:16
  10.6 4.3 %collective-permute-start.3 = (f32[128,128]{1,0:T(8,128)S(1)}, f32[128,128]{1,0:T(8,128)S(1)}, u32[]{:S(2)}, u32[]{:S(2)}) collective-permute-start(f32[128,128]{1,0:T(8,128)S(1)} %select_add_fusion.1), channel_id=1, source_target_pairs={{0,8},{2,10},{4,12},{6,14},{8,0},{10,2},{12,4},{14,6},{16,24},{18,... | collective-permute-start | bytes 196616 | tf_op jit(solution)/shard_map/ppermute | solution.py:16
  12.2 6.7 %collective-permute-start.2 = (f32[128,128]{1,0:T(8,128)S(1)}, f32[128,128]{1,0:T(8,128)S(1)}, u32[]{:S(2)}, u32[]{:S(2)}) collective-permute-start(f32[128,128]{1,0:T(8,128)S(1)} %select_add_fusion.1), channel_id=1, source_target_pairs={{0,24},{2,26},{4,28},{6,30},{8,16},{10,18},{12,20},{14,22},{16,8},... | collective-permute-start | bytes 196616 | tf_op jit(solution)/shard_map/ppermute | solution.py:16
  14.7 6.6 %collective-permute-start.1 = (f32[128,128]{1,0:T(8,128)S(1)}, f32[128,128]{1,0:T(8,128)S(1)}, u32[]{:S(2)}, u32[]{:S(2)}) collective-permute-start(f32[128,128]{1,0:T(8,128)S(1)} %select_add_fusion.1), channel_id=1, source_target_pairs={{0,16},{2,18},{4,20},{6,22},{8,24},{10,26},{12,28},{14,30},{16,0},... | collective-permute-start | bytes 196616 | tf_op jit(solution)/shard_map/ppermute | solution.py:16
  21.3 4.3 %collective-permute-start.4 = (f32[128,128]{1,0:T(8,128)S(1)}, f32[128,128]{1,0:T(8,128)S(1)}, u32[]{:S(2)}, u32[]{:S(2)}) collective-permute-start(f32[128,128]{1,0:T(8,128)S(1)} %add_add_fusion.1), channel_id=1, source_target_pairs={{0,4},{2,6},{4,0},{6,2},{8,12},{10,14},{12,8},{14,10},{16,20},{18,... | collective-permute-start | bytes 196616 | tf_op jit(solution)/shard_map/ppermute | solution.py:16
  27.1 1.3 %collective-permute-start.6 = (f32[1,128,128]{2,1,0:T(8,128)S(1)}, f32[1,128,128]{2,1,0:T(8,128)S(1)}, u32[]{:S(2)}, u32[]{:S(2)}) collective-permute-start(f32[1,128,128]{2,1,0:T(8,128)S(1)} %slice_select_fusion), channel_id=1, source_target_pairs={{0,2},{2,0},{4,6},{6,4},{8,10},{10,8},{12,14},{14,12},{16,18},{18,... | collective-permute-start | bytes 196616 | tf_op jit(solution)/shard_map/ppermute | solution.py:16
  28.4 4.5 %collective-permute-start.9 = (f32[1,128,128]{2,1,0:T(8,128)S(1)}, f32[1,128,128]{2,1,0:T(8,128)S(1)}, u32[]{:S(2)}, u32[]{:S(2)}) collective-permute-start(f32[1,128,128]{2,1,0:T(8,128)S(1)} %select_add_fusion), channel_id=1, source_target_pairs={{0,8},{2,10},{4,12},{6,14},{8,0},{10,2},{12,4},{14,6},{16,24},{18,... | collective-permute-start | bytes 196616 | tf_op jit(solution)/shard_map/ppermute | solution.py:16
  30.3 6.7 %collective-permute-start.8 = (f32[1,128,128]{2,1,0:T(8,128)S(1)}, f32[1,128,128]{2,1,0:T(8,128)S(1)}, u32[]{:S(2)}, u32[]{:S(2)}) collective-permute-start(f32[1,128,128]{2,1,0:T(8,128)S(1)} %select_add_fusion), channel_id=1, source_target_pairs={{0,24},{2,26},{4,28},{6,30},{8,16},{10,18},{12,20},{14,22},{16,8},... | collective-permute-start | bytes 196616 | tf_op jit(solution)/shard_map/ppermute | solution.py:16
  32.8 6.6 %collective-permute-start.7 = (f32[1,128,128]{2,1,0:T(8,128)S(1)}, f32[1,128,128]{2,1,0:T(8,128)S(1)}, u32[]{:S(2)}, u32[]{:S(2)}) collective-permute-start(f32[1,128,128]{2,1,0:T(8,128)S(1)} %select_add_fusion), channel_id=1, source_target_pairs={{0,16},{2,18},{4,20},{6,22},{8,24},{10,26},{12,28},{14,30},{16,0},... | collective-permute-start | bytes 196616 | tf_op jit(solution)/shard_map/ppermute | solution.py:16
  39.4 5.6 %collective-permute-start.11 = (f32[1,128,128]{2,1,0:T(8,128)S(1)}, f32[1,128,128]{2,1,0:T(8,128)S(1)}, u32[]{:S(2)}, u32[]{:S(2)}) collective-permute-start(f32[1,128,128]{2,1,0:T(8,128)S(1)} %add_add_fusion), channel_id=1, source_target_pairs={{0,5},{1,4},{2,7},{3,6},{4,1},{5,0},{6,3},{7,2},{8,13},{9,12},{10,... | collective-permute-start | bytes 196616 | tf_op jit(solution)/shard_map/ppermute | solution.py:27
  41.9 4.9 %collective-permute-start.10 = (f32[1,128,128]{2,1,0:T(8,128)S(1)}, f32[1,128,128]{2,1,0:T(8,128)S(1)}, u32[]{:S(2)}, u32[]{:S(2)}) collective-permute-start(f32[1,128,128]{2,1,0:T(8,128)S(1)} %add_add_fusion), channel_id=1, source_target_pairs={{0,1},{1,0},{2,3},{3,2},{4,5},{5,4},{6,7},{7,6},{8,9},{9,8},{10,11... | collective-permute-start | bytes 196616 | tf_op jit(solution)/shard_map/ppermute | solution.py:16
  42.4 5.0 %collective-permute-start.13 = (f32[128,128]{1,0:T(8,128)S(1)}, f32[128,128]{1,0:T(8,128)S(1)}, u32[]{:S(2)}, u32[]{:S(2)}) collective-permute-start(f32[128,128]{1,0:T(8,128)S(1)} %add.55.refs_2_), channel_id=1, source_target_pairs={{0,1},{1,0},{2,3},{3,2},{4,5},{5,4},{6,7},{7,6},{8,9},{9,8},{10,11... | collective-permute-start | bytes 196616 | tf_op jit(solution)/shard_map/ppermute | solution.py:16
  43.9 4.3 %collective-permute-start.12 = (f32[1,128,128]{2,1,0:T(8,128)S(1)}, f32[1,128,128]{2,1,0:T(8,128)S(1)}, u32[]{:S(2)}, u32[]{:S(2)}) collective-permute-start(f32[1,128,128]{2,1,0:T(8,128)S(1)} %add_add_fusion), channel_id=1, source_target_pairs={{0,4},{2,6},{4,0},{6,2},{8,12},{10,14},{12,8},{14,10},{16,20},{18,... | collective-permute-start | bytes 196616 | tf_op jit(solution)/shard_map/ppermute | solution.py:16
  48.2 2.6 %collective-permute-start.14 = (f32[2,128,128]{2,1,0:T(8,128)S(1)}, f32[2,128,128]{2,1,0:T(8,128)S(1)}, u32[]{:S(2)}, u32[]{:S(2)}) collective-permute-start(f32[2,128,128]{2,1,0:T(8,128)S(1)} %pad_maximum_fusion.refs_0_), channel_id=1, source_target_pairs={{0,2},{2,0},{4,6},{6,4},{8,10},{10,8},{12,14},{14,12},{16,18},{18,... | collective-permute-start | bytes 393224 | tf_op jit(solution)/shard_map/ppermute | solution.py:16

commit v5 on v4

--- a/solution.py
+++ b/solution.py
@@ -109,14 +109,22 @@
                 part_ref[d] += total
 
 
-def last_kernel(tile, parts, mine, *refs):
+def last_kernel(tile, kept, parts, mine, *refs):
     core_ref, s_ref, x_ref = refs[:3]
     bs_refs = refs[3:3 + parts]
-    out_hbm, out_ref, w_ref, sems = refs[-4:]
-    half, _, columns = out_ref.shape
+    if mine:
+        out_hbm, kept_ref, out_ref, w_ref, sems = refs[3 + parts:]
+    else:
+        kept_ref, _, out_hbm, out_ref, w_ref, sems, kept_sem = refs[3 + parts:]
+    half, columns = x_ref.shape[0] // 2, x_ref.shape[2]
     rank = s_ref.shape[1] // 3
     core = lax.axis_index("space") % 2
     start = half * (core if mine else 1 - core)
+    whole = columns - kept
+    if not mine:
+        kept_copy = pltpu.make_async_copy(
+            kept_ref, out_hbm.at[pl.ds(half - start, half), :, pl.ds(whole, kept)], kept_sem)
+        kept_copy.start()
     c_high, c_low = split(jnp.concatenate([core_ref[d] for d in range(parts)], axis=1))
     c_both = jnp.concatenate([c_high, c_low], axis=0)
     wide = c_high.shape[0]
@@ -135,15 +143,23 @@
         if j + 1 < steps:
             weigh(j + 1)
         cols = pl.ds(j * tile, tile)
+        keep = mine and j * tile >= whole
         for t in range(half):
             high, low = w_ref[0, t * rank:(t + 1) * rank, cols], w_ref[1, t * rank:(t + 1) * rank, cols]
             removed = mul(s_ref[...], jnp.concatenate([high, high, low], axis=0))
-            out_ref[t, :, cols] = x_ref[start + t, :, cols] - removed
-        copies.append(pltpu.make_async_copy(
-            out_ref.at[:, :, cols], out_hbm.at[pl.ds(start, half), :, cols], sems.at[j]))
-        copies[-1].start()
+            value = x_ref[start + t, :, cols] - removed
+            if keep:
+                kept_ref[t, :, pl.ds(j * tile - whole, tile)] = value
+            else:
+                out_ref[t, :, cols] = value
+        if not keep:
+            copies.append(pltpu.make_async_copy(
+                out_ref.at[:, :, cols], out_hbm.at[pl.ds(start, half), :, cols], sems.at[j]))
+            copies[-1].start()
     for copy in copies:
         copy.wait()
+    if not mine:
+        kept_copy.wait()
 
 
 VMEM = pl.BlockSpec(memory_space=pltpu.VMEM)
@@ -247,25 +263,31 @@
         core = over_rest(own, over_groups(halved(rest)))
         other = swap(core, "space", space, 1)
 
-        def last(mine, part, *out):
-            fine = tile_of(columns, 256)
+        fine = tile_of(columns, 256)
+        kept = columns // fine * 3 // 8 * fine
+
+        def last(mine, part, *before):
+            out = jax.ShapeDtypeStruct(snapshots.shape, jnp.float32)
+            out_columns = columns - kept if mine else columns
+            scratch = [
+                pltpu.VMEM((snaps // 2, samples, out_columns), jnp.float32),
+                pltpu.VMEM((2, wide // 2, columns), jnp.bfloat16),
+                pltpu.SemaphoreType.DMA((out_columns // fine,)),
+            ]
             return pl.pallas_call(
-                functools.partial(last_kernel, fine, samp, mine),
-                out_shape=jax.ShapeDtypeStruct(snapshots.shape, jnp.float32),
-                in_specs=[VMEM] * (3 + samp) + [ANY] * len(out),
-                out_specs=ANY,
-                input_output_aliases={3 + samp: 0} if out else {},
-                scratch_shapes=[
-                    pltpu.VMEM((snaps // 2, samples, columns), jnp.float32),
-                    pltpu.VMEM((2, wide // 2, columns), jnp.bfloat16),
-                    pltpu.SemaphoreType.DMA((columns // fine,)),
-                ],
+                functools.partial(last_kernel, fine, kept, samp, mine),
+                out_shape=(out, on_chip((snaps // 2, samples, kept), jnp.float32)) if mine else out,
+                in_specs=[VMEM] * (3 + samp) + ([] if mine else [VMEM, ANY]),
+                out_specs=(ANY, VMEM) if mine else ANY,
+                input_output_aliases={} if mine else {4 + samp: 0},
+                scratch_shapes=scratch if mine else scratch + [pltpu.SemaphoreType.DMA],
                 compiler_params=pltpu.CompilerParams(vmem_limit_bytes=20 * MIB),
                 cost_estimate=pl.CostEstimate(flops=flops, bytes_accessed=snapshots.size * 2, transcendentals=0),
                 name="last_mine" if mine else "last_other",
-            )(part, spreader, x_chip, own_split, *rest_splits, *out)
-
-        return last(False, other, last(True, core))
+            )(part, spreader, x_chip, own_split, *rest_splits, *before)
+
+        written, on_hold = last(True, core)
+        return last(False, other, on_hold, written)
 
     return jax.shard_map(
         shards,

time: 53.6 us -> 53.2 us (level)
  no operation moved by 1% of the time
where the time goes in v5:
time: 53.2 us; the launch traced here: 53 us
  waiting for transfers between devices  22.6 us (42%)
  starting transfers between devices  18.5 us (35%)
  Pallas kernels  11.6 us (22%)
    ppermute x14, waiting for transfers between devices, swap(): return lax.ppermute(value, axis, [(i, i ^ bit) for i in range(size)])  22.1 us
    ppermute x14, starting transfers between devices, swap(): return lax.ppermute(value, axis, [(i, i ^ bit) for i in range(size)])  16 us
    pallas_call x1, Pallas kernels, shards(): pl.pallas_call(functools.partial(first_kernel, tile), out_shape=(on_chip(...  6.22 us
    pallas_call x2, Pallas kernels, last(): pl.pallas_call(functools.partial(last_kernel, fine, kept, samp, mine), ou...  4.66 us
    ppermute x1, starting transfers between devices, swap_both(): return lax.ppermute(value, ('space', 'samp'), perm)  2.51 us
  transfers between devices with their start and end apart: 15, of which 13 were waited for; matrix products, arithmetic and copies ran while one was open for 0% of the time, Pallas kernels for 16%

profile of v5, /device:TPU:0, one launch (start us, length us, event | category | flops | bytes accessed | tf_op | source)
XLA Modules:
  0.0 53.0 jit_solution(17261173857213080295)
XLA Ops:
  0.0 3.0 %collective-permute-start.5 = (f32[128,2048]{1,0:T(8,128)}, f32[128,2048]{1,0:T(8,128)S(1)}, u32[]{:S(2)}, u32[]{:S(2)}) collective-permute-start(f32[128,2048]{1,0:T(8,128)} %b_hbm.1), channel_id=1, source_target_pairs={{0,1},{1,0},{2,3},{3,2},{4,5},{5,4},{6,7},{7,6},{8,9},{9,8},{10,11... | collective-permute-start | bytes 3145736 | tf_op jit(solution)/shard_map/ppermute | solution.py:16
  3.0 6.2 %first.1 = (f32[4,256,2048]{2,1,0:T(8,128)S(1)}, bf16[2,256,2048]{2,1,0:T(8,128)(2,1)S(1)}, bf16[2,128,2048]{2,1,0:T(8,128)(2,1)S(1)}, f32[256,128]{1,0:T(8,128)S(1)}, bf16[256,192]{1,0:T(8,128)(2,1)S(1)}) custom-call(f32[4,256,2048]{2,1,0:T(8,128)} %x_hbm.1, f32[64,256]{1,0:T(8,128)} %bitcast.13, f32[128,2048]{1,0:T(8,128)} %b_hbm.1), custom_call_target="tpu_custom_call" | custom-call | flops 805306368 | bytes 8388608 | tf_op jit(solution)/shard_map/first/pallas_call | solution.py:227
  9.2 0.1 collective-permute-start
  9.3 1.2 %collective-permute-done = f32[128,128]{1,0:T(8,128)S(1)} collective-permute-done((f32[128,128]{1,0:T(8,128)S(1)}, f32[128,128]{1,0:T(8,128)S(1)}, u32[]{:S(2)}, u32[]{:S(2)}) %collective-permute-start) | collective-permute-done | bytes 65568 | tf_op jit(solution)/shard_map/ppermute | solution.py:16
  10.6 1.6 %collective-permute-start.3 = (f32[128,128]{1,0:T(8,128)S(1)}, f32[128,128]{1,0:T(8,128)S(1)}, u32[]{:S(2)}, u32[]{:S(2)}) collective-permute-start(f32[128,128]{1,0:T(8,128)S(1)} %select_add_fusion.1), channel_id=1, source_target_pairs={{0,8},{2,10},{4,12},{6,14},{8,0},{10,2},{12,4},{14,6},{16,24},{18,... | collective-permute-start | bytes 196616 | tf_op jit(solution)/shard_map/ppermute | solution.py:16
  12.2 2.5 %collective-permute-start.2 = (f32[128,128]{1,0:T(8,128)S(1)}, f32[128,128]{1,0:T(8,128)S(1)}, u32[]{:S(2)}, u32[]{:S(2)}) collective-permute-start(f32[128,128]{1,0:T(8,128)S(1)} %select_add_fusion.1), channel_id=1, source_target_pairs={{0,24},{2,26},{4,28},{6,30},{8,16},{10,18},{12,20},{14,22},{16,8},... | collective-permute-start | bytes 196616 | tf_op jit(solution)/shard_map/ppermute | solution.py:16
  14.7 0.1 collective-permute-start.1
  14.8 0.1 collective-permute-done.3
  14.9 4.0 %collective-permute-done.2 = f32[128,128]{1,0:T(8,128)S(1)} collective-permute-done((f32[128,128]{1,0:T(8,128)S(1)}, f32[128,128]{1,0:T(8,128)S(1)}, u32[]{:S(2)}, u32[]{:S(2)}) %collective-permute-start.2) | collective-permute-done | bytes 65568 | tf_op jit(solution)/shard_map/ppermute | solution.py:16
  18.9 2.4 %collective-permute-done.1 = f32[128,128]{1,0:T(8,128)S(1)} collective-permute-done((f32[128,128]{1,0:T(8,128)S(1)}, f32[128,128]{1,0:T(8,128)S(1)}, u32[]{:S(2)}, u32[]{:S(2)}) %collective-permute-start.1) | collective-permute-done | bytes 65568 | tf_op jit(solution)/shard_map/ppermute | solution.py:16
  21.3 1.6 %collective-permute-start.4 = (f32[128,128]{1,0:T(8,128)S(1)}, f32[128,128]{1,0:T(8,128)S(1)}, u32[]{:S(2)}, u32[]{:S(2)}) collective-permute-start(f32[128,128]{1,0:T(8,128)S(1)} %add_add_fusion.1), channel_id=1, source_target_pairs={{0,4},{2,6},{4,0},{6,2},{8,12},{10,14},{12,8},{14,10},{16,20},{18,... | collective-permute-start | bytes 196616 | tf_op jit(solution)/shard_map/ppermute | solution.py:16
  22.9 2.7 %collective-permute-done.4 = f32[128,128]{1,0:T(8,128)S(1)} collective-permute-done((f32[128,128]{1,0:T(8,128)S(1)}, f32[128,128]{1,0:T(8,128)S(1)}, u32[]{:S(2)}, u32[]{:S(2)}) %collective-permute-start.4) | collective-permute-done | bytes 65568 | tf_op jit(solution)/shard_map/ppermute | solution.py:16
  25.6 0.7 %collective-permute-done.5.refs_0_ = f32[128,2048]{1,0:T(8,128)S(1)} collective-permute-done((f32[128,2048]{1,0:T(8,128)}, f32[128,2048]{1,0:T(8,128)S(1)}, u32[]{:S(2)}, u32[]{:S(2)}) %collective-permute-start.5) | collective-permute-done | bytes 1048608 | tf_op jit(solution)/shard_map/ppermute | solution.py:16
  26.3 0.7 %second.1 = (f32[1,256,128]{2,1,0:T(8,128)S(1)}, bf16[2,128,2048]{2,1,0:T(8,128)(2,1)S(1)}) custom-call(f32[128,2048]{1,0:T(8,128)S(1)} %collective-permute-done.5.refs_0_, bf16[2,256,2048]{2,1,0:T(8,128)(2,1)S(1)} %get-tuple-element.15.refs_1_, f32[128,128]{1,0:T(8,128)S(1)} %add.55.refs_2_), custom_call_target="tpu_custom_call" | custom-call | flops 402653184 | tf_op jit(solution)/shard_map/second/pallas_call | solution.py:250
  27.1 0.1 collective-permute-start.6
  27.2 1.2 %collective-permute-done.6 = f32[1,128,128]{2,1,0:T(8,128)S(1)} collective-permute-done((f32[1,128,128]{2,1,0:T(8,128)S(1)}, f32[1,128,128]{2,1,0:T(8,128)S(1)}, u32[]{:S(2)}, u32[]{:S(2)}) %collective-permute-start.6) | collective-permute-done | bytes 65568 | tf_op jit(solution)/shard_map/ppermute | solution.py:16
  28.4 1.9 %collective-permute-start.9 = (f32[1,128,128]{2,1,0:T(8,128)S(1)}, f32[1,128,128]{2,1,0:T(8,128)S(1)}, u32[]{:S(2)}, u32[]{:S(2)}) collective-permute-start(f32[1,128,128]{2,1,0:T(8,128)S(1)} %select_add_fusion), channel_id=1, source_target_pairs={{0,8},{2,10},{4,12},{6,14},{8,0},{10,2},{12,4},{14,6},{16,24},{18,... | collective-permute-start | bytes 196616 | tf_op jit(solution)/shard_map/ppermute | solution.py:16
  30.3 2.5 %collective-permute-start.8 = (f32[1,128,128]{2,1,0:T(8,128)S(1)}, f32[1,128,128]{2,1,0:T(8,128)S(1)}, u32[]{:S(2)}, u32[]{:S(2)}) collective-permute-start(f32[1,128,128]{2,1,0:T(8,128)S(1)} %select_add_fusion), channel_id=1, source_target_pairs={{0,24},{2,26},{4,28},{6,30},{8,16},{10,18},{12,20},{14,22},{16,8},... | collective-permute-start | bytes 196616 | tf_op jit(solution)/shard_map/ppermute | solution.py:16
  32.8 0.1 collective-permute-start.7
  32.9 0.0 collective-permute-done.9
  32.9 4.1 %collective-permute-done.8 = f32[1,128,128]{2,1,0:T(8,128)S(1)} collective-permute-done((f32[1,128,128]{2,1,0:T(8,128)S(1)}, f32[1,128,128]{2,1,0:T(8,128)S(1)}, u32[]{:S(2)}, u32[]{:S(2)}) %collective-permute-start.8) | collective-permute-done | bytes 65568 | tf_op jit(solution)/shard_map/ppermute | solution.py:16
  37.0 2.4 %collective-permute-done.7 = f32[1,128,128]{2,1,0:T(8,128)S(1)} collective-permute-done((f32[1,128,128]{2,1,0:T(8,128)S(1)}, f32[1,128,128]{2,1,0:T(8,128)S(1)}, u32[]{:S(2)}, u32[]{:S(2)}) %collective-permute-start.7) | collective-permute-done | bytes 65568 | tf_op jit(solution)/shard_map/ppermute | solution.py:16
  39.4 2.5 %collective-permute-start.11 = (f32[1,128,128]{2,1,0:T(8,128)S(1)}, f32[1,128,128]{2,1,0:T(8,128)S(1)}, u32[]{:S(2)}, u32[]{:S(2)}) collective-permute-start(f32[1,128,128]{2,1,0:T(8,128)S(1)} %add_add_fusion), channel_id=1, source_target_pairs={{0,5},{1,4},{2,7},{3,6},{4,1},{5,0},{6,3},{7,2},{8,13},{9,12},{10,... | collective-permute-start | bytes 196616 | tf_op jit(solution)/shard_map/ppermute | solution.py:27
  41.9 0.5 %collective-permute-start.10 = (f32[1,128,128]{2,1,0:T(8,128)S(1)}, f32[1,128,128]{2,1,0:T(8,128)S(1)}, u32[]{:S(2)}, u32[]{:S(2)}) collective-permute-start(f32[1,128,128]{2,1,0:T(8,128)S(1)} %add_add_fusion), channel_id=1, source_target_pairs={{0,1},{1,0},{2,3},{3,2},{4,5},{5,4},{6,7},{7,6},{8,9},{9,8},{10,11... | collective-permute-start | bytes 196616 | tf_op jit(solution)/shard_map/ppermute | solution.py:16
  42.4 1.5 %collective-permute-start.13 = (f32[128,128]{1,0:T(8,128)S(1)}, f32[128,128]{1,0:T(8,128)S(1)}, u32[]{:S(2)}, u32[]{:S(2)}) collective-permute-start(f32[128,128]{1,0:T(8,128)S(1)} %add.55.refs_2_), channel_id=1, source_target_pairs={{0,1},{1,0},{2,3},{3,2},{4,5},{5,4},{6,7},{7,6},{8,9},{9,8},{10,11... | collective-permute-start | bytes 196616 | tf_op jit(solution)/shard_map/ppermute | solution.py:16
  43.9 0.5 collective-permute-start.12
  44.4 0.5 %collective-permute-done.11 = f32[1,128,128]{2,1,0:T(8,128)S(1)} collective-permute-done((f32[1,128,128]{2,1,0:T(8,128)S(1)}, f32[1,128,128]{2,1,0:T(8,128)S(1)}, u32[]{:S(2)}, u32[]{:S(2)}) %collective-permute-start.11) | collective-permute-done | bytes 65568 | tf_op jit(solution)/shard_map/ppermute | solution.py:27
  45.0 1.8 %collective-permute-done.10 = f32[1,128,128]{2,1,0:T(8,128)S(1)} collective-permute-done((f32[1,128,128]{2,1,0:T(8,128)S(1)}, f32[1,128,128]{2,1,0:T(8,128)S(1)}, u32[]{:S(2)}, u32[]{:S(2)}) %collective-permute-start.10) | collective-permute-done | bytes 65568 | tf_op jit(solution)/shard_map/ppermute | solution.py:16
  46.8 0.7 %collective-permute-done.13 = f32[128,128]{1,0:T(8,128)S(1)} collective-permute-done((f32[128,128]{1,0:T(8,128)S(1)}, f32[128,128]{1,0:T(8,128)S(1)}, u32[]{:S(2)}, u32[]{:S(2)}) %collective-permute-start.13) | collective-permute-done | bytes 65568 | tf_op jit(solution)/shard_map/ppermute | solution.py:16
  47.5 0.7 %collective-permute-done.12 = f32[1,128,128]{2,1,0:T(8,128)S(1)} collective-permute-done((f32[1,128,128]{2,1,0:T(8,128)S(1)}, f32[1,128,128]{2,1,0:T(8,128)S(1)}, u32[]{:S(2)}, u32[]{:S(2)}) %collective-permute-start.12) | collective-permute-done | bytes 65568 | tf_op jit(solution)/shard_map/ppermute | solution.py:16
  48.2 0.1 collective-permute-start.14
  48.3 2.0 %last_mine.1 = (f32[4,256,2048]{2,1,0:T(8,128)}, f32[2,256,768]{2,1,0:T(8,128)S(1)}) custom-call(f32[2,128,128]{2,1,0:T(8,128)S(1)} %pad_maximum_fusion.refs_0_, bf16[256,192]{1,0:T(8,128)(2,1)S(1)} %get-tuple-element.17.refs_1_, f32[4,256,2048]{2,1,0:T(8,128)S(1)} %get-tuple-element.18.refs_2_, bf16[2,128,2048]{2,1,0:T(8,128)(2,1)S(1)} %get-tuple-element.19.refs_3_, ...), custom_call_target="tpu_custom_call" | custom-call | flops 805306368 | bytes 4194304 | tf_op jit(solution)/shard_map/last_mine/pallas_call | solution.py:277
  50.3 0.0 collective-permute-done.14.refs_0_
  50.3 2.7 %last_other.1 = f32[4,256,2048]{2,1,0:T(8,128)} custom-call(f32[2,128,128]{2,1,0:T(8,128)S(1)} %collective-permute-done.14.refs_0_, bf16[256,192]{1,0:T(8,128)(2,1)S(1)} %get-tuple-element.17.refs_1_, f32[4,256,2048]{2,1,0:T(8,128)S(1)} %get-tuple-element.18.refs_2_, ...), custom_call_target="tpu_custom_call", output_to_operand_aliasing={{}: (6, {})} | custom-call | flops 805306368 | bytes 4194304 | tf_op jit(solution)/shard_map/last_other/pallas_call | solution.py:277
  (10 shorter events, 0.1 us)
Async XLA Ops:
  0.0 26.3 %collective-permute-start.5 = (f32[128,2048]{1,0:T(8,128)}, f32[128,2048]{1,0:T(8,128)S(1)}, u32[]{:S(2)}, u32[]{:S(2)}) collective-permute-start(f32[128,2048]{1,0:T(8,128)} %b_hbm.1), channel_id=1, source_target_pairs={{0,1},{1,0},{2,3},{3,2},{4,5},{5,4},{6,7},{7,6},{8,9},{9,8},{10,11... | collective-permute-start | bytes 3145736 | tf_op jit(solution)/shard_map/ppermute | solution.py:16
  9.2 1.3 %collective-permute-start = (f32[128,128]{1,0:T(8,128)S(1)}, f32[128,128]{1,0:T(8,128)S(1)}, u32[]{:S(2)}, u32[]{:S(2)}) collective-permute-start(f32[128,128]{1,0:T(8,128)S(1)} %slice_select_fusion.1), channel_id=1, source_target_pairs={{0,2},{2,0},{4,6},{6,4},{8,10},{10,8},{12,14},{14,12},{16,18},{18,... | collective-permute-start | bytes 196616 | tf_op jit(solution)/shard_map/ppermute | solution.py:16
  10.6 4.3 %collective-permute-start.3 = (f32[128,128]{1,0:T(8,128)S(1)}, f32[128,128]{1,0:T(8,128)S(1)}, u32[]{:S(2)}, u32[]{:S(2)}) collective-permute-start(f32[128,128]{1,0:T(8,128)S(1)} %select_add_fusion.1), channel_id=1, source_target_pairs={{0,8},{2,10},{4,12},{6,14},{8,0},{10,2},{12,4},{14,6},{16,24},{18,... | collective-permute-start | bytes 196616 | tf_op jit(solution)/shard_map/ppermute | solution.py:16
  12.2 6.7 %collective-permute-start.2 = (f32[128,128]{1,0:T(8,128)S(1)}, f32[128,128]{1,0:T(8,128)S(1)}, u32[]{:S(2)}, u32[]{:S(2)}) collective-permute-start(f32[128,128]{1,0:T(8,128)S(1)} %select_add_fusion.1), channel_id=1, source_target_pairs={{0,24},{2,26},{4,28},{6,30},{8,16},{10,18},{12,20},{14,22},{16,8},... | collective-permute-start | bytes 196616 | tf_op jit(solution)/shard_map/ppermute | solution.py:16
  14.7 6.6 %collective-permute-start.1 = (f32[128,128]{1,0:T(8,128)S(1)}, f32[128,128]{1,0:T(8,128)S(1)}, u32[]{:S(2)}, u32[]{:S(2)}) collective-permute-start(f32[128,128]{1,0:T(8,128)S(1)} %select_add_fusion.1), channel_id=1, source_target_pairs={{0,16},{2,18},{4,20},{6,22},{8,24},{10,26},{12,28},{14,30},{16,0},... | collective-permute-start | bytes 196616 | tf_op jit(solution)/shard_map/ppermute | solution.py:16
  21.3 4.3 %collective-permute-start.4 = (f32[128,128]{1,0:T(8,128)S(1)}, f32[128,128]{1,0:T(8,128)S(1)}, u32[]{:S(2)}, u32[]{:S(2)}) collective-permute-start(f32[128,128]{1,0:T(8,128)S(1)} %add_add_fusion.1), channel_id=1, source_target_pairs={{0,4},{2,6},{4,0},{6,2},{8,12},{10,14},{12,8},{14,10},{16,20},{18,... | collective-permute-start | bytes 196616 | tf_op jit(solution)/shard_map/ppermute | solution.py:16
  27.1 1.3 %collective-permute-start.6 = (f32[1,128,128]{2,1,0:T(8,128)S(1)}, f32[1,128,128]{2,1,0:T(8,128)S(1)}, u32[]{:S(2)}, u32[]{:S(2)}) collective-permute-start(f32[1,128,128]{2,1,0:T(8,128)S(1)} %slice_select_fusion), channel_id=1, source_target_pairs={{0,2},{2,0},{4,6},{6,4},{8,10},{10,8},{12,14},{14,12},{16,18},{18,... | collective-permute-start | bytes 196616 | tf_op jit(solution)/shard_map/ppermute | solution.py:16
  28.4 4.5 %collective-permute-start.9 = (f32[1,128,128]{2,1,0:T(8,128)S(1)}, f32[1,128,128]{2,1,0:T(8,128)S(1)}, u32[]{:S(2)}, u32[]{:S(2)}) collective-permute-start(f32[1,128,128]{2,1,0:T(8,128)S(1)} %select_add_fusion), channel_id=1, source_target_pairs={{0,8},{2,10},{4,12},{6,14},{8,0},{10,2},{12,4},{14,6},{16,24},{18,... | collective-permute-start | bytes 196616 | tf_op jit(solution)/shard_map/ppermute | solution.py:16
  30.3 6.7 %collective-permute-start.8 = (f32[1,128,128]{2,1,0:T(8,128)S(1)}, f32[1,128,128]{2,1,0:T(8,128)S(1)}, u32[]{:S(2)}, u32[]{:S(2)}) collective-permute-start(f32[1,128,128]{2,1,0:T(8,128)S(1)} %select_add_fusion), channel_id=1, source_target_pairs={{0,24},{2,26},{4,28},{6,30},{8,16},{10,18},{12,20},{14,22},{16,8},... | collective-permute-start | bytes 196616 | tf_op jit(solution)/shard_map/ppermute | solution.py:16
  32.8 6.6 %collective-permute-start.7 = (f32[1,128,128]{2,1,0:T(8,128)S(1)}, f32[1,128,128]{2,1,0:T(8,128)S(1)}, u32[]{:S(2)}, u32[]{:S(2)}) collective-permute-start(f32[1,128,128]{2,1,0:T(8,128)S(1)} %select_add_fusion), channel_id=1, source_target_pairs={{0,16},{2,18},{4,20},{6,22},{8,24},{10,26},{12,28},{14,30},{16,0},... | collective-permute-start | bytes 196616 | tf_op jit(solution)/shard_map/ppermute | solution.py:16
  39.4 5.6 %collective-permute-start.11 = (f32[1,128,128]{2,1,0:T(8,128)S(1)}, f32[1,128,128]{2,1,0:T(8,128)S(1)}, u32[]{:S(2)}, u32[]{:S(2)}) collective-permute-start(f32[1,128,128]{2,1,0:T(8,128)S(1)} %add_add_fusion), channel_id=1, source_target_pairs={{0,5},{1,4},{2,7},{3,6},{4,1},{5,0},{6,3},{7,2},{8,13},{9,12},{10,... | collective-permute-start | bytes 196616 | tf_op jit(solution)/shard_map/ppermute | solution.py:27
  41.9 4.9 %collective-permute-start.10 = (f32[1,128,128]{2,1,0:T(8,128)S(1)}, f32[1,128,128]{2,1,0:T(8,128)S(1)}, u32[]{:S(2)}, u32[]{:S(2)}) collective-permute-start(f32[1,128,128]{2,1,0:T(8,128)S(1)} %add_add_fusion), channel_id=1, source_target_pairs={{0,1},{1,0},{2,3},{3,2},{4,5},{5,4},{6,7},{7,6},{8,9},{9,8},{10,11... | collective-permute-start | bytes 196616 | tf_op jit(solution)/shard_map/ppermute | solution.py:16
  42.4 5.0 %collective-permute-start.13 = (f32[128,128]{1,0:T(8,128)S(1)}, f32[128,128]{1,0:T(8,128)S(1)}, u32[]{:S(2)}, u32[]{:S(2)}) collective-permute-start(f32[128,128]{1,0:T(8,128)S(1)} %add.55.refs_2_), channel_id=1, source_target_pairs={{0,1},{1,0},{2,3},{3,2},{4,5},{5,4},{6,7},{7,6},{8,9},{9,8},{10,11... | collective-permute-start | bytes 196616 | tf_op jit(solution)/shard_map/ppermute | solution.py:16
  43.9 4.3 %collective-permute-start.12 = (f32[1,128,128]{2,1,0:T(8,128)S(1)}, f32[1,128,128]{2,1,0:T(8,128)S(1)}, u32[]{:S(2)}, u32[]{:S(2)}) collective-permute-start(f32[1,128,128]{2,1,0:T(8,128)S(1)} %add_add_fusion), channel_id=1, source_target_pairs={{0,4},{2,6},{4,0},{6,2},{8,12},{10,14},{12,8},{14,10},{16,20},{18,... | collective-permute-start | bytes 196616 | tf_op jit(solution)/shard_map/ppermute | solution.py:16
  48.2 2.1 %collective-permute-start.14 = (f32[2,128,128]{2,1,0:T(8,128)S(1)}, f32[2,128,128]{2,1,0:T(8,128)S(1)}, u32[]{:S(2)}, u32[]{:S(2)}) collective-permute-start(f32[2,128,128]{2,1,0:T(8,128)S(1)} %pad_maximum_fusion.refs_0_), channel_id=1, source_target_pairs={{0,2},{2,0},{4,6},{6,4},{8,10},{10,8},{12,14},{14,12},{16,18},{18,... | collective-permute-start | bytes 393224 | tf_op jit(solution)/shard_map/ppermute | solution.py:16

commit v6 on v5

--- a/solution.py
+++ b/solution.py
@@ -94,15 +94,19 @@
             part_ref[...] += total
 
 
-def second_kernel(tile, parts, *refs):
-    b_refs, (y_ref, _), outs = refs[:parts], refs[parts:parts + 2], refs[parts + 2:]
+def second_kernel(tile, parts, mine, *refs):
+    b_refs, y_ref, outs = refs[:parts], refs[parts], refs[-1 - parts if mine else -1:]
     part_ref, bs_refs = outs[0], outs[1:]
+    half = y_ref.shape[1] // 2
+    core = lax.axis_index("space") % 2
+    rows = pl.ds(pl.multiple_of(half * (core if mine else 1 - core), half), half)
     for d in range(parts):
         for j in range(y_ref.shape[2] // tile):
             cols = pl.ds(j * tile, tile)
-            total, high, low = rows_times(y_ref[0, :, cols], y_ref[1, :, cols], b_refs[d][:, cols])
-            bs_refs[d][0, :, cols] = high
-            bs_refs[d][1, :, cols] = low
+            total, high, low = rows_times(y_ref[0, rows, cols], y_ref[1, rows, cols], b_refs[d][:, cols])
+            if mine:
+                bs_refs[d][0, :, cols] = high
+                bs_refs[d][1, :, cols] = low
             if j == 0:
                 part_ref[d] = total
             else:
@@ -177,8 +181,8 @@
     left = list(bits(space, 2))
     groups = []
     while len(left) > 1:
-        groups.append((left[-1], left[-2] | left[-1], left[-2]))
-        left = left[:-2]
+        groups.append((left[0] | left[1], left[1], left[0]))
+        left = left[2:]
 
     def halved(part):
         core = lax.axis_index("space") % 2
@@ -247,20 +251,27 @@
         own = over_groups(halved(own))
         for bit in left:
             own = own + swap(own, "space", space, bit)
-        rest, *rest_splits = pl.pallas_call(
-            functools.partial(second_kernel, tile, samp - 1),
-            out_shape=(
-                on_chip((samp - 1, wide, basis_rows), jnp.float32),
-                *[on_chip((2, basis_rows, columns), jnp.bfloat16) for _ in others],
-            ),
-            in_specs=[VMEM] * (len(others) + 1) + [ANY],
-            out_specs=(VMEM,) * samp,
-            compiler_params=pltpu.CompilerParams(vmem_limit_bytes=16 * MIB),
-            cost_estimate=pl.CostEstimate(
-                flops=6 * wide * basis_rows * columns * (samp - 1), bytes_accessed=0, transcendentals=0),
-            name="second",
-        )(*others, mixed, own)
-        core = over_rest(own, over_groups(halved(rest)))
+
+        def products(mine, after):
+            return pl.pallas_call(
+                functools.partial(second_kernel, tile, samp - 1, mine),
+                out_shape=(
+                    on_chip((samp - 1, wide // 2, basis_rows), jnp.float32),
+                    *[on_chip((2, basis_rows, columns), jnp.bfloat16) for _ in others if mine],
+                ),
+                in_specs=[VMEM] * (len(others) + 1) + [ANY],
+                out_specs=(VMEM,) * (samp if mine else 1),
+                compiler_params=pltpu.CompilerParams(vmem_limit_bytes=16 * MIB),
+                cost_estimate=pl.CostEstimate(
+                    flops=3 * wide * basis_rows * columns * (samp - 1), bytes_accessed=0, transcendentals=0),
+                name="second_mine" if mine else "second_other",
+            )(*others, mixed, after)
+
+        sent, = products(False, own)
+        got = swap(sent, "space", space, 1)
+        rest, *rest_splits = products(True, own)
+        rest = rest + got
+        core = over_rest(own, over_groups(rest))
         other = swap(core, "space", space, 1)
 
         fine = tile_of(columns, 256)

time: 53.2 us -> 53.2 us (level)
  waiting for transfers between devices: 22.6 us -> 21.8 us
    ppermute x1, starting transfers between devices: 2.51 us -> 3.58 us  [swap_both(): return lax.ppermute(value, ('space', 'samp'), perm)]
    ppermute x14, waiting for transfers between devices: 22.1 us -> 21 us  [swap(): return lax.ppermute(value, axis, [(i, i ^ bit) for i in range(size)])]
    ppermute x14, starting transfers between devices: 16 us -> 15.3 us  [swap(): return lax.ppermute(value, axis, [(i, i ^ bit) for i in range(size)])]
    pallas_call x1 -> x2, Pallas kernels: 0.72 us -> 1.22 us  [products(): pl.pallas_call(functools.partial(second_kernel, tile, samp - 1, mine), ou...]
  transfers between devices with their start and end apart: 15 -> 15, of which waited for: 13 -> 14; matrix products, arithmetic and copies ran while one was open for 0% -> 0% of each run, Pallas kernels for 16% -> 17%
where the time goes in v6:
time: 53.2 us; the launch traced here: 53 us
  waiting for transfers between devices  21.8 us (41%)
  starting transfers between devices  18.9 us (36%)
  Pallas kernels  12.1 us (23%)
    ppermute x14, waiting for transfers between devices, swap(): return lax.ppermute(value, axis, [(i, i ^ bit) for i in range(size)])  21 us
    ppermute x14, starting transfers between devices, swap(): return lax.ppermute(value, axis, [(i, i ^ bit) for i in range(size)])  15.3 us
    pallas_call x1, Pallas kernels, shards(): pl.pallas_call(functools.partial(first_kernel, tile), out_shape=(on_chip(...  6.22 us
    pallas_call x2, Pallas kernels, last(): pl.pallas_call(functools.partial(last_kernel, fine, kept, samp, mine), ou...  4.66 us
    ppermute x1, starting transfers between devices, swap_both(): return lax.ppermute(value, ('space', 'samp'), perm)  3.58 us
    pallas_call x2, Pallas kernels, products(): pl.pallas_call(functools.partial(second_kernel, tile, samp - 1, mine), ou...  1.22 us
  transfers between devices with their start and end apart: 15, of which 14 were waited for; matrix products, arithmetic and copies ran while one was open for 0% of the time, Pallas kernels for 17%

profile of v6, /device:TPU:0, one launch (start us, length us, event | category | flops | bytes accessed | tf_op | source)
XLA Modules:
  0.0 53.0 jit_solution(14957724938026491380)
XLA Ops:
  0.0 3.0 %collective-permute-start.5 = (f32[128,2048]{1,0:T(8,128)}, f32[128,2048]{1,0:T(8,128)S(1)}, u32[]{:S(2)}, u32[]{:S(2)}) collective-permute-start(f32[128,2048]{1,0:T(8,128)} %b_hbm.1), channel_id=1, source_target_pairs={{0,1},{1,0},{2,3},{3,2},{4,5},{5,4},{6,7},{7,6},{8,9},{9,8},{10,11... | collective-permute-start | bytes 3145736 | tf_op jit(solution)/shard_map/ppermute | solution.py:16
  3.0 6.2 %first.1 = (f32[4,256,2048]{2,1,0:T(8,128)S(1)}, bf16[2,256,2048]{2,1,0:T(8,128)(2,1)S(1)}, bf16[2,128,2048]{2,1,0:T(8,128)(2,1)S(1)}, f32[256,128]{1,0:T(8,128)S(1)}, bf16[256,192]{1,0:T(8,128)(2,1)S(1)}) custom-call(f32[4,256,2048]{2,1,0:T(8,128)} %x_hbm.1, f32[64,256]{1,0:T(8,128)} %bitcast.13, f32[128,2048]{1,0:T(8,128)} %b_hbm.1), custom_call_target="tpu_custom_call" | custom-call | flops 805306368 | bytes 8388608 | tf_op jit(solution)/shard_map/first/pallas_call | solution.py:231
  9.2 0.1 collective-permute-start
  9.3 1.2 %collective-permute-done = f32[128,128]{1,0:T(8,128)S(1)} collective-permute-done((f32[128,128]{1,0:T(8,128)S(1)}, f32[128,128]{1,0:T(8,128)S(1)}, u32[]{:S(2)}, u32[]{:S(2)}) %collective-permute-start) | collective-permute-done | bytes 65568 | tf_op jit(solution)/shard_map/ppermute | solution.py:16
  10.6 1.6 %collective-permute-start.3 = (f32[128,128]{1,0:T(8,128)S(1)}, f32[128,128]{1,0:T(8,128)S(1)}, u32[]{:S(2)}, u32[]{:S(2)}) collective-permute-start(f32[128,128]{1,0:T(8,128)S(1)} %select_add_fusion), channel_id=1, source_target_pairs={{0,4},{2,6},{4,0},{6,2},{8,12},{10,14},{12,8},{14,10},{16,20},{18,... | collective-permute-start | bytes 196616 | tf_op jit(solution)/shard_map/ppermute | solution.py:16
  12.1 1.6 %collective-permute-start.2 = (f32[128,128]{1,0:T(8,128)S(1)}, f32[128,128]{1,0:T(8,128)S(1)}, u32[]{:S(2)}, u32[]{:S(2)}) collective-permute-start(f32[128,128]{1,0:T(8,128)S(1)} %select_add_fusion), channel_id=1, source_target_pairs={{0,8},{2,10},{4,12},{6,14},{8,0},{10,2},{12,4},{14,6},{16,24},{18,... | collective-permute-start | bytes 196616 | tf_op jit(solution)/shard_map/ppermute | solution.py:16
  13.7 0.4 collective-permute-start.1
  14.1 0.8 %collective-permute-done.3 = f32[128,128]{1,0:T(8,128)S(1)} collective-permute-done((f32[128,128]{1,0:T(8,128)S(1)}, f32[128,128]{1,0:T(8,128)S(1)}, u32[]{:S(2)}, u32[]{:S(2)}) %collective-permute-start.3) | collective-permute-done | bytes 65568 | tf_op jit(solution)/shard_map/ppermute | solution.py:16
  14.9 2.1 %collective-permute-done.2 = f32[128,128]{1,0:T(8,128)S(1)} collective-permute-done((f32[128,128]{1,0:T(8,128)S(1)}, f32[128,128]{1,0:T(8,128)S(1)}, u32[]{:S(2)}, u32[]{:S(2)}) %collective-permute-start.2) | collective-permute-done | bytes 65568 | tf_op jit(solution)/shard_map/ppermute | solution.py:16
  17.0 1.9 %collective-permute-done.1 = f32[128,128]{1,0:T(8,128)S(1)} collective-permute-done((f32[128,128]{1,0:T(8,128)S(1)}, f32[128,128]{1,0:T(8,128)S(1)}, u32[]{:S(2)}, u32[]{:S(2)}) %collective-permute-start.1) | collective-permute-done | bytes 65568 | tf_op jit(solution)/shard_map/ppermute | solution.py:16
  18.9 2.7 %collective-permute-start.4 = (f32[128,128]{1,0:T(8,128)S(1)}, f32[128,128]{1,0:T(8,128)S(1)}, u32[]{:S(2)}, u32[]{:S(2)}) collective-permute-start(f32[128,128]{1,0:T(8,128)S(1)} %add_add_fusion.1), channel_id=1, source_target_pairs={{0,16},{2,18},{4,20},{6,22},{8,24},{10,26},{12,28},{14,30},{16,0},... | collective-permute-start | bytes 196616 | tf_op jit(solution)/shard_map/ppermute | solution.py:16
  21.6 3.2 %collective-permute-done.4 = f32[128,128]{1,0:T(8,128)S(1)} collective-permute-done((f32[128,128]{1,0:T(8,128)S(1)}, f32[128,128]{1,0:T(8,128)S(1)}, u32[]{:S(2)}, u32[]{:S(2)}) %collective-permute-start.4) | collective-permute-done | bytes 65568 | tf_op jit(solution)/shard_map/ppermute | solution.py:16
  24.7 1.6 %collective-permute-done.5.refs_0_ = f32[128,2048]{1,0:T(8,128)S(1)} collective-permute-done((f32[128,2048]{1,0:T(8,128)}, f32[128,2048]{1,0:T(8,128)S(1)}, u32[]{:S(2)}, u32[]{:S(2)}) %collective-permute-start.5) | collective-permute-done | bytes 1048608 | tf_op jit(solution)/shard_map/ppermute | solution.py:16
  26.3 0.6 %second_other.1 = f32[1,128,128]{2,1,0:T(8,128)S(1)} custom-call(f32[128,2048]{1,0:T(8,128)S(1)} %collective-permute-done.5.refs_0_, bf16[2,256,2048]{2,1,0:T(8,128)(2,1)S(1)} %get-tuple-element.15.refs_1_, f32[128,128]{1,0:T(8,128)S(1)} %add.54.refs_2_), custom_call_target="tpu_custom_call" | custom-call | flops 201326592 | tf_op jit(solution)/shard_map/second_other/pallas_call | solution.py:256
  26.9 0.1 collective-permute-start.6
  27.0 0.6 %second_mine.1 = (f32[1,128,128]{2,1,0:T(8,128)S(1)}, bf16[2,128,2048]{2,1,0:T(8,128)(2,1)S(1)}) custom-call(f32[128,2048]{1,0:T(8,128)S(1)} %collective-permute-done.5.refs_0_, bf16[2,256,2048]{2,1,0:T(8,128)(2,1)S(1)} %get-tuple-element.15.refs_1_, f32[128,128]{1,0:T(8,128)S(1)} %add.54.refs_2_), custom_call_target="tpu_custom_call" | custom-call | flops 201326592 | tf_op jit(solution)/shard_map/second_mine/pallas_call | solution.py:256
  27.6 0.6 %collective-permute-done.6 = f32[1,128,128]{2,1,0:T(8,128)S(1)} collective-permute-done((f32[1,128,128]{2,1,0:T(8,128)S(1)}, f32[1,128,128]{2,1,0:T(8,128)S(1)}, u32[]{:S(2)}, u32[]{:S(2)}) %collective-permute-start.6) | collective-permute-done | bytes 65568 | tf_op jit(solution)/shard_map/ppermute | solution.py:16
  28.3 1.8 %collective-permute-start.9 = (f32[1,128,128]{2,1,0:T(8,128)S(1)}, f32[1,128,128]{2,1,0:T(8,128)S(1)}, u32[]{:S(2)}, u32[]{:S(2)}) collective-permute-start(f32[1,128,128]{2,1,0:T(8,128)S(1)} %add.55), channel_id=1, source_target_pairs={{0,4},{2,6},{4,0},{6,2},{8,12},{10,14},{12,8},{14,10},{16,20},{18,... | collective-permute-start | bytes 196616 | tf_op jit(solution)/shard_map/ppermute | solution.py:16
  30.1 1.6 %collective-permute-start.8 = (f32[1,128,128]{2,1,0:T(8,128)S(1)}, f32[1,128,128]{2,1,0:T(8,128)S(1)}, u32[]{:S(2)}, u32[]{:S(2)}) collective-permute-start(f32[1,128,128]{2,1,0:T(8,128)S(1)} %add.55), channel_id=1, source_target_pairs={{0,8},{2,10},{4,12},{6,14},{8,0},{10,2},{12,4},{14,6},{16,24},{18,... | collective-permute-start | bytes 196616 | tf_op jit(solution)/shard_map/ppermute | solution.py:16
  31.7 0.1 collective-permute-start.7
  31.8 0.8 %collective-permute-done.9 = f32[1,128,128]{2,1,0:T(8,128)S(1)} collective-permute-done((f32[1,128,128]{2,1,0:T(8,128)S(1)}, f32[1,128,128]{2,1,0:T(8,128)S(1)}, u32[]{:S(2)}, u32[]{:S(2)}) %collective-permute-start.9) | collective-permute-done | bytes 65568 | tf_op jit(solution)/shard_map/ppermute | solution.py:16
  32.6 2.3 %collective-permute-done.8 = f32[1,128,128]{2,1,0:T(8,128)S(1)} collective-permute-done((f32[1,128,128]{2,1,0:T(8,128)S(1)}, f32[1,128,128]{2,1,0:T(8,128)S(1)}, u32[]{:S(2)}, u32[]{:S(2)}) %collective-permute-start.8) | collective-permute-done | bytes 65568 | tf_op jit(solution)/shard_map/ppermute | solution.py:16
  34.9 1.9 %collective-permute-done.7 = f32[1,128,128]{2,1,0:T(8,128)S(1)} collective-permute-done((f32[1,128,128]{2,1,0:T(8,128)S(1)}, f32[1,128,128]{2,1,0:T(8,128)S(1)}, u32[]{:S(2)}, u32[]{:S(2)}) %collective-permute-start.7) | collective-permute-done | bytes 65568 | tf_op jit(solution)/shard_map/ppermute | solution.py:16
  36.9 3.6 %collective-permute-start.11 = (f32[1,128,128]{2,1,0:T(8,128)S(1)}, f32[1,128,128]{2,1,0:T(8,128)S(1)}, u32[]{:S(2)}, u32[]{:S(2)}) collective-permute-start(f32[1,128,128]{2,1,0:T(8,128)S(1)} %add_add_fusion), channel_id=1, source_target_pairs={{0,17},{1,16},{2,19},{3,18},{4,21},{5,20},{6,23},{7,22},{8,25},{9,... | collective-permute-start | bytes 196616 | tf_op jit(solution)/shard_map/ppermute | solution.py:27
  40.5 0.5 %collective-permute-start.10 = (f32[1,128,128]{2,1,0:T(8,128)S(1)}, f32[1,128,128]{2,1,0:T(8,128)S(1)}, u32[]{:S(2)}, u32[]{:S(2)}) collective-permute-start(f32[1,128,128]{2,1,0:T(8,128)S(1)} %add_add_fusion), channel_id=1, source_target_pairs={{0,1},{1,0},{2,3},{3,2},{4,5},{5,4},{6,7},{7,6},{8,9},{9,8},{10,11... | collective-permute-start | bytes 196616 | tf_op jit(solution)/shard_map/ppermute | solution.py:16
  41.0 1.5 %collective-permute-start.13 = (f32[128,128]{1,0:T(8,128)S(1)}, f32[128,128]{1,0:T(8,128)S(1)}, u32[]{:S(2)}, u32[]{:S(2)}) collective-permute-start(f32[128,128]{1,0:T(8,128)S(1)} %add.54.refs_2_), channel_id=1, source_target_pairs={{0,1},{1,0},{2,3},{3,2},{4,5},{5,4},{6,7},{7,6},{8,9},{9,8},{10,11... | collective-permute-start | bytes 196616 | tf_op jit(solution)/shard_map/ppermute | solution.py:16
  42.5 0.3 collective-permute-start.12
  42.8 0.8 %collective-permute-done.11 = f32[1,128,128]{2,1,0:T(8,128)S(1)} collective-permute-done((f32[1,128,128]{2,1,0:T(8,128)S(1)}, f32[1,128,128]{2,1,0:T(8,128)S(1)}, u32[]{:S(2)}, u32[]{:S(2)}) %collective-permute-start.11) | collective-permute-done | bytes 65568 | tf_op jit(solution)/shard_map/ppermute | solution.py:27
  43.6 1.1 %collective-permute-done.10 = f32[1,128,128]{2,1,0:T(8,128)S(1)} collective-permute-done((f32[1,128,128]{2,1,0:T(8,128)S(1)}, f32[1,128,128]{2,1,0:T(8,128)S(1)}, u32[]{:S(2)}, u32[]{:S(2)}) %collective-permute-start.10) | collective-permute-done | bytes 65568 | tf_op jit(solution)/shard_map/ppermute | solution.py:16
  44.7 0.7 %collective-permute-done.13 = f32[128,128]{1,0:T(8,128)S(1)} collective-permute-done((f32[128,128]{1,0:T(8,128)S(1)}, f32[128,128]{1,0:T(8,128)S(1)}, u32[]{:S(2)}, u32[]{:S(2)}) %collective-permute-start.13) | collective-permute-done | bytes 65568 | tf_op jit(solution)/shard_map/ppermute | solution.py:16
  45.4 2.8 %collective-permute-done.12 = f32[1,128,128]{2,1,0:T(8,128)S(1)} collective-permute-done((f32[1,128,128]{2,1,0:T(8,128)S(1)}, f32[1,128,128]{2,1,0:T(8,128)S(1)}, u32[]{:S(2)}, u32[]{:S(2)}) %collective-permute-start.12) | collective-permute-done | bytes 65568 | tf_op jit(solution)/shard_map/ppermute | solution.py:16
  48.3 0.1 collective-permute-start.14
  48.4 2.0 %last_mine.1 = (f32[4,256,2048]{2,1,0:T(8,128)}, f32[2,256,768]{2,1,0:T(8,128)S(1)}) custom-call(f32[2,128,128]{2,1,0:T(8,128)S(1)} %pad_maximum_fusion.refs_0_, bf16[256,192]{1,0:T(8,128)(2,1)S(1)} %get-tuple-element.17.refs_1_, f32[4,256,2048]{2,1,0:T(8,128)S(1)} %get-tuple-element.18.refs_2_, bf16[2,128,2048]{2,1,0:T(8,128)(2,1)S(1)} %get-tuple-element.19.refs_3_, ...), custom_call_target="tpu_custom_call" | custom-call | flops 805306368 | bytes 4194304 | tf_op jit(solution)/shard_map/last_mine/pallas_call | solution.py:288
  50.4 0.0 collective-permute-done.14.refs_0_
  50.4 2.7 %last_other.1 = f32[4,256,2048]{2,1,0:T(8,128)} custom-call(f32[2,128,128]{2,1,0:T(8,128)S(1)} %collective-permute-done.14.refs_0_, bf16[256,192]{1,0:T(8,128)(2,1)S(1)} %get-tuple-element.17.refs_1_, f32[4,256,2048]{2,1,0:T(8,128)S(1)} %get-tuple-element.18.refs_2_, ...), custom_call_target="tpu_custom_call", output_to_operand_aliasing={{}: (6, {})} | custom-call | flops 805306368 | bytes 4194304 | tf_op jit(solution)/shard_map/last_other/pallas_call | solution.py:288
  (9 shorter events, 0.1 us)
Async XLA Ops:
  0.0 26.3 %collective-permute-start.5 = (f32[128,2048]{1,0:T(8,128)}, f32[128,2048]{1,0:T(8,128)S(1)}, u32[]{:S(2)}, u32[]{:S(2)}) collective-permute-start(f32[128,2048]{1,0:T(8,128)} %b_hbm.1), channel_id=1, source_target_pairs={{0,1},{1,0},{2,3},{3,2},{4,5},{5,4},{6,7},{7,6},{8,9},{9,8},{10,11... | collective-permute-start | bytes 3145736 | tf_op jit(solution)/shard_map/ppermute | solution.py:16
  9.2 1.3 %collective-permute-start = (f32[128,128]{1,0:T(8,128)S(1)}, f32[128,128]{1,0:T(8,128)S(1)}, u32[]{:S(2)}, u32[]{:S(2)}) collective-permute-start(f32[128,128]{1,0:T(8,128)S(1)} %slice_select_fusion), channel_id=1, source_target_pairs={{0,2},{2,0},{4,6},{6,4},{8,10},{10,8},{12,14},{14,12},{16,18},{18,... | collective-permute-start | bytes 196616 | tf_op jit(solution)/shard_map/ppermute | solution.py:16
  10.6 4.3 %collective-permute-start.3 = (f32[128,128]{1,0:T(8,128)S(1)}, f32[128,128]{1,0:T(8,128)S(1)}, u32[]{:S(2)}, u32[]{:S(2)}) collective-permute-start(f32[128,128]{1,0:T(8,128)S(1)} %select_add_fusion), channel_id=1, source_target_pairs={{0,4},{2,6},{4,0},{6,2},{8,12},{10,14},{12,8},{14,10},{16,20},{18,... | collective-permute-start | bytes 196616 | tf_op jit(solution)/shard_map/ppermute | solution.py:16
  12.1 4.8 %collective-permute-start.2 = (f32[128,128]{1,0:T(8,128)S(1)}, f32[128,128]{1,0:T(8,128)S(1)}, u32[]{:S(2)}, u32[]{:S(2)}) collective-permute-start(f32[128,128]{1,0:T(8,128)S(1)} %select_add_fusion), channel_id=1, source_target_pairs={{0,8},{2,10},{4,12},{6,14},{8,0},{10,2},{12,4},{14,6},{16,24},{18,... | collective-permute-start | bytes 196616 | tf_op jit(solution)/shard_map/ppermute | solution.py:16
  13.7 5.2 %collective-permute-start.1 = (f32[128,128]{1,0:T(8,128)S(1)}, f32[128,128]{1,0:T(8,128)S(1)}, u32[]{:S(2)}, u32[]{:S(2)}) collective-permute-start(f32[128,128]{1,0:T(8,128)S(1)} %select_add_fusion), channel_id=1, source_target_pairs={{0,12},{2,14},{4,8},{6,10},{8,4},{10,6},{12,0},{14,2},{16,28},{18,... | collective-permute-start | bytes 196616 | tf_op jit(solution)/shard_map/ppermute | solution.py:16
  18.9 5.8 %collective-permute-start.4 = (f32[128,128]{1,0:T(8,128)S(1)}, f32[128,128]{1,0:T(8,128)S(1)}, u32[]{:S(2)}, u32[]{:S(2)}) collective-permute-start(f32[128,128]{1,0:T(8,128)S(1)} %add_add_fusion.1), channel_id=1, source_target_pairs={{0,16},{2,18},{4,20},{6,22},{8,24},{10,26},{12,28},{14,30},{16,0},... | collective-permute-start | bytes 196616 | tf_op jit(solution)/shard_map/ppermute | solution.py:16
  26.9 1.3 %collective-permute-start.6 = (f32[1,128,128]{2,1,0:T(8,128)S(1)}, f32[1,128,128]{2,1,0:T(8,128)S(1)}, u32[]{:S(2)}, u32[]{:S(2)}) collective-permute-start(f32[1,128,128]{2,1,0:T(8,128)S(1)} %second_other.1), channel_id=1, source_target_pairs={{0,2},{2,0},{4,6},{6,4},{8,10},{10,8},{12,14},{14,12},{16,18},{18,... | collective-permute-start | bytes 196616 | tf_op jit(solution)/shard_map/ppermute | solution.py:16
  28.3 4.3 %collective-permute-start.9 = (f32[1,128,128]{2,1,0:T(8,128)S(1)}, f32[1,128,128]{2,1,0:T(8,128)S(1)}, u32[]{:S(2)}, u32[]{:S(2)}) collective-permute-start(f32[1,128,128]{2,1,0:T(8,128)S(1)} %add.55), channel_id=1, source_target_pairs={{0,4},{2,6},{4,0},{6,2},{8,12},{10,14},{12,8},{14,10},{16,20},{18,... | collective-permute-start | bytes 196616 | tf_op jit(solution)/shard_map/ppermute | solution.py:16
  30.1 4.8 %collective-permute-start.8 = (f32[1,128,128]{2,1,0:T(8,128)S(1)}, f32[1,128,128]{2,1,0:T(8,128)S(1)}, u32[]{:S(2)}, u32[]{:S(2)}) collective-permute-start(f32[1,128,128]{2,1,0:T(8,128)S(1)} %add.55), channel_id=1, source_target_pairs={{0,8},{2,10},{4,12},{6,14},{8,0},{10,2},{12,4},{14,6},{16,24},{18,... | collective-permute-start | bytes 196616 | tf_op jit(solution)/shard_map/ppermute | solution.py:16
  31.7 5.2 %collective-permute-start.7 = (f32[1,128,128]{2,1,0:T(8,128)S(1)}, f32[1,128,128]{2,1,0:T(8,128)S(1)}, u32[]{:S(2)}, u32[]{:S(2)}) collective-permute-start(f32[1,128,128]{2,1,0:T(8,128)S(1)} %add.55), channel_id=1, source_target_pairs={{0,12},{2,14},{4,8},{6,10},{8,4},{10,6},{12,0},{14,2},{16,28},{18,... | collective-permute-start | bytes 196616 | tf_op jit(solution)/shard_map/ppermute | solution.py:16
  36.9 6.7 %collective-permute-start.11 = (f32[1,128,128]{2,1,0:T(8,128)S(1)}, f32[1,128,128]{2,1,0:T(8,128)S(1)}, u32[]{:S(2)}, u32[]{:S(2)}) collective-permute-start(f32[1,128,128]{2,1,0:T(8,128)S(1)} %add_add_fusion), channel_id=1, source_target_pairs={{0,17},{1,16},{2,19},{3,18},{4,21},{5,20},{6,23},{7,22},{8,25},{9,... | collective-permute-start | bytes 196616 | tf_op jit(solution)/shard_map/ppermute | solution.py:27
  40.5 4.3 %collective-permute-start.10 = (f32[1,128,128]{2,1,0:T(8,128)S(1)}, f32[1,128,128]{2,1,0:T(8,128)S(1)}, u32[]{:S(2)}, u32[]{:S(2)}) collective-permute-start(f32[1,128,128]{2,1,0:T(8,128)S(1)} %add_add_fusion), channel_id=1, source_target_pairs={{0,1},{1,0},{2,3},{3,2},{4,5},{5,4},{6,7},{7,6},{8,9},{9,8},{10,11... | collective-permute-start | bytes 196616 | tf_op jit(solution)/shard_map/ppermute | solution.py:16
  41.0 4.4 %collective-permute-start.13 = (f32[128,128]{1,0:T(8,128)S(1)}, f32[128,128]{1,0:T(8,128)S(1)}, u32[]{:S(2)}, u32[]{:S(2)}) collective-permute-start(f32[128,128]{1,0:T(8,128)S(1)} %add.54.refs_2_), channel_id=1, source_target_pairs={{0,1},{1,0},{2,3},{3,2},{4,5},{5,4},{6,7},{7,6},{8,9},{9,8},{10,11... | collective-permute-start | bytes 196616 | tf_op jit(solution)/shard_map/ppermute | solution.py:16
  42.5 5.8 %collective-permute-start.12 = (f32[1,128,128]{2,1,0:T(8,128)S(1)}, f32[1,128,128]{2,1,0:T(8,128)S(1)}, u32[]{:S(2)}, u32[]{:S(2)}) collective-permute-start(f32[1,128,128]{2,1,0:T(8,128)S(1)} %add_add_fusion), channel_id=1, source_target_pairs={{0,16},{2,18},{4,20},{6,22},{8,24},{10,26},{12,28},{14,30},{16,0},... | collective-permute-start | bytes 196616 | tf_op jit(solution)/shard_map/ppermute | solution.py:16
  48.3 2.1 %collective-permute-start.14 = (f32[2,128,128]{2,1,0:T(8,128)S(1)}, f32[2,128,128]{2,1,0:T(8,128)S(1)}, u32[]{:S(2)}, u32[]{:S(2)}) collective-permute-start(f32[2,128,128]{2,1,0:T(8,128)S(1)} %pad_maximum_fusion.refs_0_), channel_id=1, source_target_pairs={{0,2},{2,0},{4,6},{6,4},{8,10},{10,8},{12,14},{14,12},{16,18},{18,... | collective-permute-start | bytes 393224 | tf_op jit(solution)/shard_map/ppermute | solution.py:16

commit v7 on v6

--- a/solution.py
+++ b/solution.py
@@ -135,7 +135,9 @@
     steps = columns // tile
 
     def weigh(j):
-        cols = pl.ds(j * tile, tile)
+        if j % 2:
+            return
+        cols = pl.ds(j * tile, 2 * tile)
         b_high = jnp.concatenate([b[0, :, cols] for b in bs_refs], axis=0)
         b_low = jnp.concatenate([b[1, :, cols] for b in bs_refs], axis=0)
         both = mul(c_both, b_high)
@@ -144,8 +146,8 @@
     copies = []
     weigh(0)
     for j in range(steps):
-        if j + 1 < steps:
-            weigh(j + 1)
+        if j + 2 < steps:
+            weigh(j + 2)
         cols = pl.ds(j * tile, tile)
         keep = mine and j * tile >= whole
         for t in range(half):
@@ -275,7 +277,7 @@
         other = swap(core, "space", space, 1)
 
         fine = tile_of(columns, 256)
-        kept = columns // fine * 3 // 8 * fine
+        kept = columns - fine
 
         def last(mine, part, *before):
             out = jax.ShapeDtypeStruct(snapshots.shape, jnp.float32)

time: 53.2 us -> 53.2 us (level)
  transfers between devices with their start and end apart: 15 -> 15, of which waited for: 14 -> 14; matrix products, arithmetic and copies ran while one was open for 0% -> 0% of each run, Pallas kernels for 17% -> 15%
where the time goes in v7:
time: 53.2 us; the launch traced here: 53 us
  waiting for transfers between devices  21.9 us (41%)
  starting transfers between devices  18.9 us (36%)
  Pallas kernels  12 us (23%)
    ppermute x14, waiting for transfers between devices, swap(): return lax.ppermute(value, axis, [(i, i ^ bit) for i in range(size)])  21.1 us
    ppermute x14, starting transfers between devices, swap(): return lax.ppermute(value, axis, [(i, i ^ bit) for i in range(size)])  15.3 us
    pallas_call x1, Pallas kernels, shards(): pl.pallas_call(functools.partial(first_kernel, tile), out_shape=(on_chip(...  6.22 us
    pallas_call x2, Pallas kernels, last(): pl.pallas_call(functools.partial(last_kernel, fine, kept, samp, mine), ou...  4.58 us
    ppermute x1, starting transfers between devices, swap_both(): return lax.ppermute(value, ('space', 'samp'), perm)  3.58 us
    pallas_call x2, Pallas kernels, products(): pl.pallas_call(functools.partial(second_kernel, tile, samp - 1, mine), ou...  1.22 us
  transfers between devices with their start and end apart: 15, of which 14 were waited for; matrix products, arithmetic and copies ran while one was open for 0% of the time, Pallas kernels for 15%

profile of v7, /device:TPU:0, one launch (start us, length us, event | category | flops | bytes accessed | tf_op | source)
XLA Modules:
  0.0 53.0 jit_solution(9641685521477394163)
XLA Ops:
  0.0 3.0 %collective-permute-start.5 = (f32[128,2048]{1,0:T(8,128)}, f32[128,2048]{1,0:T(8,128)S(1)}, u32[]{:S(2)}, u32[]{:S(2)}) collective-permute-start(f32[128,2048]{1,0:T(8,128)} %b_hbm.1), channel_id=1, source_target_pairs={{0,1},{1,0},{2,3},{3,2},{4,5},{5,4},{6,7},{7,6},{8,9},{9,8},{10,11... | collective-permute-start | bytes 3145736 | tf_op jit(solution)/shard_map/ppermute | solution.py:16
  3.0 6.2 %first.1 = (f32[4,256,2048]{2,1,0:T(8,128)S(1)}, bf16[2,256,2048]{2,1,0:T(8,128)(2,1)S(1)}, bf16[2,128,2048]{2,1,0:T(8,128)(2,1)S(1)}, f32[256,128]{1,0:T(8,128)S(1)}, bf16[256,192]{1,0:T(8,128)(2,1)S(1)}) custom-call(f32[4,256,2048]{2,1,0:T(8,128)} %x_hbm.1, f32[64,256]{1,0:T(8,128)} %bitcast.13, f32[128,2048]{1,0:T(8,128)} %b_hbm.1), custom_call_target="tpu_custom_call" | custom-call | flops 805306368 | bytes 8388608 | tf_op jit(solution)/shard_map/first/pallas_call | solution.py:233
  9.2 0.1 collective-permute-start
  9.3 1.2 %collective-permute-done = f32[128,128]{1,0:T(8,128)S(1)} collective-permute-done((f32[128,128]{1,0:T(8,128)S(1)}, f32[128,128]{1,0:T(8,128)S(1)}, u32[]{:S(2)}, u32[]{:S(2)}) %collective-permute-start) | collective-permute-done | bytes 65568 | tf_op jit(solution)/shard_map/ppermute | solution.py:16
  10.6 1.6 %collective-permute-start.3 = (f32[128,128]{1,0:T(8,128)S(1)}, f32[128,128]{1,0:T(8,128)S(1)}, u32[]{:S(2)}, u32[]{:S(2)}) collective-permute-start(f32[128,128]{1,0:T(8,128)S(1)} %select_add_fusion), channel_id=1, source_target_pairs={{0,4},{2,6},{4,0},{6,2},{8,12},{10,14},{12,8},{14,10},{16,20},{18,... | collective-permute-start | bytes 196616 | tf_op jit(solution)/shard_map/ppermute | solution.py:16
  12.1 1.6 %collective-permute-start.2 = (f32[128,128]{1,0:T(8,128)S(1)}, f32[128,128]{1,0:T(8,128)S(1)}, u32[]{:S(2)}, u32[]{:S(2)}) collective-permute-start(f32[128,128]{1,0:T(8,128)S(1)} %select_add_fusion), channel_id=1, source_target_pairs={{0,8},{2,10},{4,12},{6,14},{8,0},{10,2},{12,4},{14,6},{16,24},{18,... | collective-permute-start | bytes 196616 | tf_op jit(solution)/shard_map/ppermute | solution.py:16
  13.7 0.4 collective-permute-start.1
  14.1 0.8 %collective-permute-done.3 = f32[128,128]{1,0:T(8,128)S(1)} collective-permute-done((f32[128,128]{1,0:T(8,128)S(1)}, f32[128,128]{1,0:T(8,128)S(1)}, u32[]{:S(2)}, u32[]{:S(2)}) %collective-permute-start.3) | collective-permute-done | bytes 65568 | tf_op jit(solution)/shard_map/ppermute | solution.py:16
  14.9 2.1 %collective-permute-done.2 = f32[128,128]{1,0:T(8,128)S(1)} collective-permute-done((f32[128,128]{1,0:T(8,128)S(1)}, f32[128,128]{1,0:T(8,128)S(1)}, u32[]{:S(2)}, u32[]{:S(2)}) %collective-permute-start.2) | collective-permute-done | bytes 65568 | tf_op jit(solution)/shard_map/ppermute | solution.py:16
  17.0 1.9 %collective-permute-done.1 = f32[128,128]{1,0:T(8,128)S(1)} collective-permute-done((f32[128,128]{1,0:T(8,128)S(1)}, f32[128,128]{1,0:T(8,128)S(1)}, u32[]{:S(2)}, u32[]{:S(2)}) %collective-permute-start.1) | collective-permute-done | bytes 65568 | tf_op jit(solution)/shard_map/ppermute | solution.py:16
  18.9 2.7 %collective-permute-start.4 = (f32[128,128]{1,0:T(8,128)S(1)}, f32[128,128]{1,0:T(8,128)S(1)}, u32[]{:S(2)}, u32[]{:S(2)}) collective-permute-start(f32[128,128]{1,0:T(8,128)S(1)} %add_add_fusion.1), channel_id=1, source_target_pairs={{0,16},{2,18},{4,20},{6,22},{8,24},{10,26},{12,28},{14,30},{16,0},... | collective-permute-start | bytes 196616 | tf_op jit(solution)/shard_map/ppermute | solution.py:16
  21.6 3.2 %collective-permute-done.4 = f32[128,128]{1,0:T(8,128)S(1)} collective-permute-done((f32[128,128]{1,0:T(8,128)S(1)}, f32[128,128]{1,0:T(8,128)S(1)}, u32[]{:S(2)}, u32[]{:S(2)}) %collective-permute-start.4) | collective-permute-done | bytes 65568 | tf_op jit(solution)/shard_map/ppermute | solution.py:16
  24.7 1.6 %collective-permute-done.5.refs_0_ = f32[128,2048]{1,0:T(8,128)S(1)} collective-permute-done((f32[128,2048]{1,0:T(8,128)}, f32[128,2048]{1,0:T(8,128)S(1)}, u32[]{:S(2)}, u32[]{:S(2)}) %collective-permute-start.5) | collective-permute-done | bytes 1048608 | tf_op jit(solution)/shard_map/ppermute | solution.py:16
  26.3 0.6 %second_other.1 = f32[1,128,128]{2,1,0:T(8,128)S(1)} custom-call(f32[128,2048]{1,0:T(8,128)S(1)} %collective-permute-done.5.refs_0_, bf16[2,256,2048]{2,1,0:T(8,128)(2,1)S(1)} %get-tuple-element.15.refs_1_, f32[128,128]{1,0:T(8,128)S(1)} %add.54.refs_2_), custom_call_target="tpu_custom_call" | custom-call | flops 201326592 | tf_op jit(solution)/shard_map/second_other/pallas_call | solution.py:258
  26.9 0.1 collective-permute-start.6
  27.0 0.6 %second_mine.1 = (f32[1,128,128]{2,1,0:T(8,128)S(1)}, bf16[2,128,2048]{2,1,0:T(8,128)(2,1)S(1)}) custom-call(f32[128,2048]{1,0:T(8,128)S(1)} %collective-permute-done.5.refs_0_, bf16[2,256,2048]{2,1,0:T(8,128)(2,1)S(1)} %get-tuple-element.15.refs_1_, f32[128,128]{1,0:T(8,128)S(1)} %add.54.refs_2_), custom_call_target="tpu_custom_call" | custom-call | flops 201326592 | tf_op jit(solution)/shard_map/second_mine/pallas_call | solution.py:258
  27.6 0.6 %collective-permute-done.6 = f32[1,128,128]{2,1,0:T(8,128)S(1)} collective-permute-done((f32[1,128,128]{2,1,0:T(8,128)S(1)}, f32[1,128,128]{2,1,0:T(8,128)S(1)}, u32[]{:S(2)}, u32[]{:S(2)}) %collective-permute-start.6) | collective-permute-done | bytes 65568 | tf_op jit(solution)/shard_map/ppermute | solution.py:16
  28.3 1.8 %collective-permute-start.9 = (f32[1,128,128]{2,1,0:T(8,128)S(1)}, f32[1,128,128]{2,1,0:T(8,128)S(1)}, u32[]{:S(2)}, u32[]{:S(2)}) collective-permute-start(f32[1,128,128]{2,1,0:T(8,128)S(1)} %add.55), channel_id=1, source_target_pairs={{0,4},{2,6},{4,0},{6,2},{8,12},{10,14},{12,8},{14,10},{16,20},{18,... | collective-permute-start | bytes 196616 | tf_op jit(solution)/shard_map/ppermute | solution.py:16
  30.1 1.6 %collective-permute-start.8 = (f32[1,128,128]{2,1,0:T(8,128)S(1)}, f32[1,128,128]{2,1,0:T(8,128)S(1)}, u32[]{:S(2)}, u32[]{:S(2)}) collective-permute-start(f32[1,128,128]{2,1,0:T(8,128)S(1)} %add.55), channel_id=1, source_target_pairs={{0,8},{2,10},{4,12},{6,14},{8,0},{10,2},{12,4},{14,6},{16,24},{18,... | collective-permute-start | bytes 196616 | tf_op jit(solution)/shard_map/ppermute | solution.py:16
  31.7 0.1 collective-permute-start.7
  31.8 0.8 %collective-permute-done.9 = f32[1,128,128]{2,1,0:T(8,128)S(1)} collective-permute-done((f32[1,128,128]{2,1,0:T(8,128)S(1)}, f32[1,128,128]{2,1,0:T(8,128)S(1)}, u32[]{:S(2)}, u32[]{:S(2)}) %collective-permute-start.9) | collective-permute-done | bytes 65568 | tf_op jit(solution)/shard_map/ppermute | solution.py:16
  32.6 2.3 %collective-permute-done.8 = f32[1,128,128]{2,1,0:T(8,128)S(1)} collective-permute-done((f32[1,128,128]{2,1,0:T(8,128)S(1)}, f32[1,128,128]{2,1,0:T(8,128)S(1)}, u32[]{:S(2)}, u32[]{:S(2)}) %collective-permute-start.8) | collective-permute-done | bytes 65568 | tf_op jit(solution)/shard_map/ppermute | solution.py:16
  34.9 1.9 %collective-permute-done.7 = f32[1,128,128]{2,1,0:T(8,128)S(1)} collective-permute-done((f32[1,128,128]{2,1,0:T(8,128)S(1)}, f32[1,128,128]{2,1,0:T(8,128)S(1)}, u32[]{:S(2)}, u32[]{:S(2)}) %collective-permute-start.7) | collective-permute-done | bytes 65568 | tf_op jit(solution)/shard_map/ppermute | solution.py:16
  36.9 3.6 %collective-permute-start.11 = (f32[1,128,128]{2,1,0:T(8,128)S(1)}, f32[1,128,128]{2,1,0:T(8,128)S(1)}, u32[]{:S(2)}, u32[]{:S(2)}) collective-permute-start(f32[1,128,128]{2,1,0:T(8,128)S(1)} %add_add_fusion), channel_id=1, source_target_pairs={{0,17},{1,16},{2,19},{3,18},{4,21},{5,20},{6,23},{7,22},{8,25},{9,... | collective-permute-start | bytes 196616 | tf_op jit(solution)/shard_map/ppermute | solution.py:27
  40.5 0.5 %collective-permute-start.10 = (f32[1,128,128]{2,1,0:T(8,128)S(1)}, f32[1,128,128]{2,1,0:T(8,128)S(1)}, u32[]{:S(2)}, u32[]{:S(2)}) collective-permute-start(f32[1,128,128]{2,1,0:T(8,128)S(1)} %add_add_fusion), channel_id=1, source_target_pairs={{0,1},{1,0},{2,3},{3,2},{4,5},{5,4},{6,7},{7,6},{8,9},{9,8},{10,11... | collective-permute-start | bytes 196616 | tf_op jit(solution)/shard_map/ppermute | solution.py:16
  41.0 1.5 %collective-permute-start.13 = (f32[128,128]{1,0:T(8,128)S(1)}, f32[128,128]{1,0:T(8,128)S(1)}, u32[]{:S(2)}, u32[]{:S(2)}) collective-permute-start(f32[128,128]{1,0:T(8,128)S(1)} %add.54.refs_2_), channel_id=1, source_target_pairs={{0,1},{1,0},{2,3},{3,2},{4,5},{5,4},{6,7},{7,6},{8,9},{9,8},{10,11... | collective-permute-start | bytes 196616 | tf_op jit(solution)/shard_map/ppermute | solution.py:16
  42.5 0.3 collective-permute-start.12
  42.8 0.8 %collective-permute-done.11 = f32[1,128,128]{2,1,0:T(8,128)S(1)} collective-permute-done((f32[1,128,128]{2,1,0:T(8,128)S(1)}, f32[1,128,128]{2,1,0:T(8,128)S(1)}, u32[]{:S(2)}, u32[]{:S(2)}) %collective-permute-start.11) | collective-permute-done | bytes 65568 | tf_op jit(solution)/shard_map/ppermute | solution.py:27
  43.6 1.1 %collective-permute-done.10 = f32[1,128,128]{2,1,0:T(8,128)S(1)} collective-permute-done((f32[1,128,128]{2,1,0:T(8,128)S(1)}, f32[1,128,128]{2,1,0:T(8,128)S(1)}, u32[]{:S(2)}, u32[]{:S(2)}) %collective-permute-start.10) | collective-permute-done | bytes 65568 | tf_op jit(solution)/shard_map/ppermute | solution.py:16
  44.7 0.7 %collective-permute-done.13 = f32[128,128]{1,0:T(8,128)S(1)} collective-permute-done((f32[128,128]{1,0:T(8,128)S(1)}, f32[128,128]{1,0:T(8,128)S(1)}, u32[]{:S(2)}, u32[]{:S(2)}) %collective-permute-start.13) | collective-permute-done | bytes 65568 | tf_op jit(solution)/shard_map/ppermute | solution.py:16
  45.4 2.8 %collective-permute-done.12 = f32[1,128,128]{2,1,0:T(8,128)S(1)} collective-permute-done((f32[1,128,128]{2,1,0:T(8,128)S(1)}, f32[1,128,128]{2,1,0:T(8,128)S(1)}, u32[]{:S(2)}, u32[]{:S(2)}) %collective-permute-start.12) | collective-permute-done | bytes 65568 | tf_op jit(solution)/shard_map/ppermute | solution.py:16
  48.3 0.1 collective-permute-start.14
  48.4 1.3 %last_mine.1 = (f32[4,256,2048]{2,1,0:T(8,128)}, f32[2,256,1792]{2,1,0:T(8,128)S(1)}) custom-call(f32[2,128,128]{2,1,0:T(8,128)S(1)} %pad_maximum_fusion.refs_0_, bf16[256,192]{1,0:T(8,128)(2,1)S(1)} %get-tuple-element.17.refs_1_, f32[4,256,2048]{2,1,0:T(8,128)S(1)} %get-tuple-element.18.refs_2_, bf16[2,128,2048]{2,1,0:T(8,128)(2,1)S(1)} %get-tuple-element.19.refs_3_, ...), custom_call_target="tpu_custom_call" | custom-call | flops 805306368 | bytes 4194304 | tf_op jit(solution)/shard_map/last_mine/pallas_call | solution.py:290
  49.6 0.0 collective-permute-done.14.refs_0_
  49.7 3.3 %last_other.1 = f32[4,256,2048]{2,1,0:T(8,128)} custom-call(f32[2,128,128]{2,1,0:T(8,128)S(1)} %collective-permute-done.14.refs_0_, bf16[256,192]{1,0:T(8,128)(2,1)S(1)} %get-tuple-element.17.refs_1_, f32[4,256,2048]{2,1,0:T(8,128)S(1)} %get-tuple-element.18.refs_2_, ...), custom_call_target="tpu_custom_call", output_to_operand_aliasing={{}: (6, {})} | custom-call | flops 805306368 | bytes 4194304 | tf_op jit(solution)/shard_map/last_other/pallas_call | solution.py:290
  (9 shorter events, 0.1 us)
Async XLA Ops:
  0.0 26.3 %collective-permute-start.5 = (f32[128,2048]{1,0:T(8,128)}, f32[128,2048]{1,0:T(8,128)S(1)}, u32[]{:S(2)}, u32[]{:S(2)}) collective-permute-start(f32[128,2048]{1,0:T(8,128)} %b_hbm.1), channel_id=1, source_target_pairs={{0,1},{1,0},{2,3},{3,2},{4,5},{5,4},{6,7},{7,6},{8,9},{9,8},{10,11... | collective-permute-start | bytes 3145736 | tf_op jit(solution)/shard_map/ppermute | solution.py:16
  9.2 1.3 %collective-permute-start = (f32[128,128]{1,0:T(8,128)S(1)}, f32[128,128]{1,0:T(8,128)S(1)}, u32[]{:S(2)}, u32[]{:S(2)}) collective-permute-start(f32[128,128]{1,0:T(8,128)S(1)} %slice_select_fusion), channel_id=1, source_target_pairs={{0,2},{2,0},{4,6},{6,4},{8,10},{10,8},{12,14},{14,12},{16,18},{18,... | collective-permute-start | bytes 196616 | tf_op jit(solution)/shard_map/ppermute | solution.py:16
  10.6 4.3 %collective-permute-start.3 = (f32[128,128]{1,0:T(8,128)S(1)}, f32[128,128]{1,0:T(8,128)S(1)}, u32[]{:S(2)}, u32[]{:S(2)}) collective-permute-start(f32[128,128]{1,0:T(8,128)S(1)} %select_add_fusion), channel_id=1, source_target_pairs={{0,4},{2,6},{4,0},{6,2},{8,12},{10,14},{12,8},{14,10},{16,20},{18,... | collective-permute-start | bytes 196616 | tf_op jit(solution)/shard_map/ppermute | solution.py:16
  12.1 4.8 %collective-permute-start.2 = (f32[128,128]{1,0:T(8,128)S(1)}, f32[128,128]{1,0:T(8,128)S(1)}, u32[]{:S(2)}, u32[]{:S(2)}) collective-permute-start(f32[128,128]{1,0:T(8,128)S(1)} %select_add_fusion), channel_id=1, source_target_pairs={{0,8},{2,10},{4,12},{6,14},{8,0},{10,2},{12,4},{14,6},{16,24},{18,... | collective-permute-start | bytes 196616 | tf_op jit(solution)/shard_map/ppermute | solution.py:16
  13.7 5.2 %collective-permute-start.1 = (f32[128,128]{1,0:T(8,128)S(1)}, f32[128,128]{1,0:T(8,128)S(1)}, u32[]{:S(2)}, u32[]{:S(2)}) collective-permute-start(f32[128,128]{1,0:T(8,128)S(1)} %select_add_fusion), channel_id=1, source_target_pairs={{0,12},{2,14},{4,8},{6,10},{8,4},{10,6},{12,0},{14,2},{16,28},{18,... | collective-permute-start | bytes 196616 | tf_op jit(solution)/shard_map/ppermute | solution.py:16
  18.9 5.8 %collective-permute-start.4 = (f32[128,128]{1,0:T(8,128)S(1)}, f32[128,128]{1,0:T(8,128)S(1)}, u32[]{:S(2)}, u32[]{:S(2)}) collective-permute-start(f32[128,128]{1,0:T(8,128)S(1)} %add_add_fusion.1), channel_id=1, source_target_pairs={{0,16},{2,18},{4,20},{6,22},{8,24},{10,26},{12,28},{14,30},{16,0},... | collective-permute-start | bytes 196616 | tf_op jit(solution)/shard_map/ppermute | solution.py:16
  26.9 1.3 %collective-permute-start.6 = (f32[1,128,128]{2,1,0:T(8,128)S(1)}, f32[1,128,128]{2,1,0:T(8,128)S(1)}, u32[]{:S(2)}, u32[]{:S(2)}) collective-permute-start(f32[1,128,128]{2,1,0:T(8,128)S(1)} %second_other.1), channel_id=1, source_target_pairs={{0,2},{2,0},{4,6},{6,4},{8,10},{10,8},{12,14},{14,12},{16,18},{18,... | collective-permute-start | bytes 196616 | tf_op jit(solution)/shard_map/ppermute | solution.py:16
  28.3 4.3 %collective-permute-start.9 = (f32[1,128,128]{2,1,0:T(8,128)S(1)}, f32[1,128,128]{2,1,0:T(8,128)S(1)}, u32[]{:S(2)}, u32[]{:S(2)}) collective-permute-start(f32[1,128,128]{2,1,0:T(8,128)S(1)} %add.55), channel_id=1, source_target_pairs={{0,4},{2,6},{4,0},{6,2},{8,12},{10,14},{12,8},{14,10},{16,20},{18,... | collective-permute-start | bytes 196616 | tf_op jit(solution)/shard_map/ppermute | solution.py:16
  30.1 4.8 %collective-permute-start.8 = (f32[1,128,128]{2,1,0:T(8,128)S(1)}, f32[1,128,128]{2,1,0:T(8,128)S(1)}, u32[]{:S(2)}, u32[]{:S(2)}) collective-permute-start(f32[1,128,128]{2,1,0:T(8,128)S(1)} %add.55), channel_id=1, source_target_pairs={{0,8},{2,10},{4,12},{6,14},{8,0},{10,2},{12,4},{14,6},{16,24},{18,... | collective-permute-start | bytes 196616 | tf_op jit(solution)/shard_map/ppermute | solution.py:16
  31.7 5.2 %collective-permute-start.7 = (f32[1,128,128]{2,1,0:T(8,128)S(1)}, f32[1,128,128]{2,1,0:T(8,128)S(1)}, u32[]{:S(2)}, u32[]{:S(2)}) collective-permute-start(f32[1,128,128]{2,1,0:T(8,128)S(1)} %add.55), channel_id=1, source_target_pairs={{0,12},{2,14},{4,8},{6,10},{8,4},{10,6},{12,0},{14,2},{16,28},{18,... | collective-permute-start | bytes 196616 | tf_op jit(solution)/shard_map/ppermute | solution.py:16
  36.9 6.7 %collective-permute-start.11 = (f32[1,128,128]{2,1,0:T(8,128)S(1)}, f32[1,128,128]{2,1,0:T(8,128)S(1)}, u32[]{:S(2)}, u32[]{:S(2)}) collective-permute-start(f32[1,128,128]{2,1,0:T(8,128)S(1)} %add_add_fusion), channel_id=1, source_target_pairs={{0,17},{1,16},{2,19},{3,18},{4,21},{5,20},{6,23},{7,22},{8,25},{9,... | collective-permute-start | bytes 196616 | tf_op jit(solution)/shard_map/ppermute | solution.py:27
  40.5 4.3 %collective-permute-start.10 = (f32[1,128,128]{2,1,0:T(8,128)S(1)}, f32[1,128,128]{2,1,0:T(8,128)S(1)}, u32[]{:S(2)}, u32[]{:S(2)}) collective-permute-start(f32[1,128,128]{2,1,0:T(8,128)S(1)} %add_add_fusion), channel_id=1, source_target_pairs={{0,1},{1,0},{2,3},{3,2},{4,5},{5,4},{6,7},{7,6},{8,9},{9,8},{10,11... | collective-permute-start | bytes 196616 | tf_op jit(solution)/shard_map/ppermute | solution.py:16
  41.0 4.4 %collective-permute-start.13 = (f32[128,128]{1,0:T(8,128)S(1)}, f32[128,128]{1,0:T(8,128)S(1)}, u32[]{:S(2)}, u32[]{:S(2)}) collective-permute-start(f32[128,128]{1,0:T(8,128)S(1)} %add.54.refs_2_), channel_id=1, source_target_pairs={{0,1},{1,0},{2,3},{3,2},{4,5},{5,4},{6,7},{7,6},{8,9},{9,8},{10,11... | collective-permute-start | bytes 196616 | tf_op jit(solution)/shard_map/ppermute | solution.py:16
  42.5 5.8 %collective-permute-start.12 = (f32[1,128,128]{2,1,0:T(8,128)S(1)}, f32[1,128,128]{2,1,0:T(8,128)S(1)}, u32[]{:S(2)}, u32[]{:S(2)}) collective-permute-start(f32[1,128,128]{2,1,0:T(8,128)S(1)} %add_add_fusion), channel_id=1, source_target_pairs={{0,16},{2,18},{4,20},{6,22},{8,24},{10,26},{12,28},{14,30},{16,0},... | collective-permute-start | bytes 196616 | tf_op jit(solution)/shard_map/ppermute | solution.py:16
  48.3 1.4 %collective-permute-start.14 = (f32[2,128,128]{2,1,0:T(8,128)S(1)}, f32[2,128,128]{2,1,0:T(8,128)S(1)}, u32[]{:S(2)}, u32[]{:S(2)}) collective-permute-start(f32[2,128,128]{2,1,0:T(8,128)S(1)} %pad_maximum_fusion.refs_0_), channel_id=1, source_target_pairs={{0,2},{2,0},{4,6},{6,4},{8,10},{10,8},{12,14},{14,12},{16,18},{18,... | collective-permute-start | bytes 393224 | tf_op jit(solution)/shard_map/ppermute | solution.py:16

commit v8 on v7

--- a/solution.py
+++ b/solution.py
@@ -101,16 +101,18 @@
     core = lax.axis_index("space") % 2
     rows = pl.ds(pl.multiple_of(half * (core if mine else 1 - core), half), half)
     for d in range(parts):
+        rank = b_refs[d].shape[0]
         for j in range(y_ref.shape[2] // tile):
             cols = pl.ds(j * tile, tile)
-            total, high, low = rows_times(y_ref[0, rows, cols], y_ref[1, rows, cols], b_refs[d][:, cols])
+            high, low = split(b_refs[d][:, cols])
             if mine:
                 bs_refs[d][0, :, cols] = high
                 bs_refs[d][1, :, cols] = low
-            if j == 0:
-                part_ref[d] = total
-            else:
-                part_ref[d] += total
+            both = mul_t(y_ref[0, rows, cols], jnp.concatenate([high, low], axis=0))
+            cross = mul_t(y_ref[1, rows, cols], high)
+            both_sum = both if j == 0 else both_sum + both
+            cross_sum = cross if j == 0 else cross_sum + cross
+        part_ref[d] = both_sum[:, :rank] + both_sum[:, rank:] + cross_sum
 
 
 def last_kernel(tile, kept, parts, mine, *refs):
@@ -256,7 +258,7 @@
 
         def products(mine, after):
             return pl.pallas_call(
-                functools.partial(second_kernel, tile, samp - 1, mine),
+                functools.partial(second_kernel, tile_of(columns, 256), samp - 1, mine),
                 out_shape=(
                     on_chip((samp - 1, wide // 2, basis_rows), jnp.float32),
                     *[on_chip((2, basis_rows, columns), jnp.bfloat16) for _ in others if mine],

time: 53.2 us -> 53.1 us (level)
  no operation moved by 1% of the time
where the time goes in v8:
time: 53.1 us; the launch traced here: 53 us
  waiting for transfers between devices  21.9 us (41%)
  starting transfers between devices  18.9 us (36%)
  Pallas kernels  12 us (23%)
    ppermute x14, waiting for transfers between devices, swap(): return lax.ppermute(value, axis, [(i, i ^ bit) for i in range(size)])  21.1 us
    ppermute x14, starting transfers between devices, swap(): return lax.ppermute(value, axis, [(i, i ^ bit) for i in range(size)])  15.3 us
    pallas_call x1, Pallas kernels, shards(): pl.pallas_call(functools.partial(first_kernel, tile), out_shape=(on_chip(...  6.22 us
    pallas_call x2, Pallas kernels, last(): pl.pallas_call(functools.partial(last_kernel, fine, kept, samp, mine), ou...  4.58 us
    ppermute x1, starting transfers between devices, swap_both(): return lax.ppermute(value, ('space', 'samp'), perm)  3.58 us
    pallas_call x2, Pallas kernels, products(): pl.pallas_call(functools.partial(second_kernel, tile_of(columns, 256), sa...  1.18 us
  transfers between devices with their start and end apart: 15, of which 14 were waited for; matrix products, arithmetic and copies ran while one was open for 0% of the time, Pallas kernels for 15%

profile of v8, /device:TPU:0, one launch (start us, length us, event | category | flops | bytes accessed | tf_op | source)
XLA Modules:
  0.0 53.0 jit_solution(752653532479735198)
XLA Ops:
  0.0 3.0 %collective-permute-start.5 = (f32[128,2048]{1,0:T(8,128)}, f32[128,2048]{1,0:T(8,128)S(1)}, u32[]{:S(2)}, u32[]{:S(2)}) collective-permute-start(f32[128,2048]{1,0:T(8,128)} %b_hbm.1), channel_id=1, source_target_pairs={{0,1},{1,0},{2,3},{3,2},{4,5},{5,4},{6,7},{7,6},{8,9},{9,8},{10,11... | collective-permute-start | bytes 3145736 | tf_op jit(solution)/shard_map/ppermute | solution.py:16
  3.0 6.2 %first.1 = (f32[4,256,2048]{2,1,0:T(8,128)S(1)}, bf16[2,256,2048]{2,1,0:T(8,128)(2,1)S(1)}, bf16[2,128,2048]{2,1,0:T(8,128)(2,1)S(1)}, f32[256,128]{1,0:T(8,128)S(1)}, bf16[256,192]{1,0:T(8,128)(2,1)S(1)}) custom-call(f32[4,256,2048]{2,1,0:T(8,128)} %x_hbm.1, f32[64,256]{1,0:T(8,128)} %bitcast.13, f32[128,2048]{1,0:T(8,128)} %b_hbm.1), custom_call_target="tpu_custom_call" | custom-call | flops 805306368 | bytes 8388608 | tf_op jit(solution)/shard_map/first/pallas_call | solution.py:235
  9.2 0.1 collective-permute-start
  9.3 1.2 %collective-permute-done = f32[128,128]{1,0:T(8,128)S(1)} collective-permute-done((f32[128,128]{1,0:T(8,128)S(1)}, f32[128,128]{1,0:T(8,128)S(1)}, u32[]{:S(2)}, u32[]{:S(2)}) %collective-permute-start) | collective-permute-done | bytes 65568 | tf_op jit(solution)/shard_map/ppermute | solution.py:16
  10.6 1.6 %collective-permute-start.3 = (f32[128,128]{1,0:T(8,128)S(1)}, f32[128,128]{1,0:T(8,128)S(1)}, u32[]{:S(2)}, u32[]{:S(2)}) collective-permute-start(f32[128,128]{1,0:T(8,128)S(1)} %select_add_fusion), channel_id=1, source_target_pairs={{0,4},{2,6},{4,0},{6,2},{8,12},{10,14},{12,8},{14,10},{16,20},{18,... | collective-permute-start | bytes 196616 | tf_op jit(solution)/shard_map/ppermute | solution.py:16
  12.1 1.6 %collective-permute-start.2 = (f32[128,128]{1,0:T(8,128)S(1)}, f32[128,128]{1,0:T(8,128)S(1)}, u32[]{:S(2)}, u32[]{:S(2)}) collective-permute-start(f32[128,128]{1,0:T(8,128)S(1)} %select_add_fusion), channel_id=1, source_target_pairs={{0,8},{2,10},{4,12},{6,14},{8,0},{10,2},{12,4},{14,6},{16,24},{18,... | collective-permute-start | bytes 196616 | tf_op jit(solution)/shard_map/ppermute | solution.py:16
  13.7 0.4 collective-permute-start.1
  14.1 0.8 %collective-permute-done.3 = f32[128,128]{1,0:T(8,128)S(1)} collective-permute-done((f32[128,128]{1,0:T(8,128)S(1)}, f32[128,128]{1,0:T(8,128)S(1)}, u32[]{:S(2)}, u32[]{:S(2)}) %collective-permute-start.3) | collective-permute-done | bytes 65568 | tf_op jit(solution)/shard_map/ppermute | solution.py:16
  14.9 2.1 %collective-permute-done.2 = f32[128,128]{1,0:T(8,128)S(1)} collective-permute-done((f32[128,128]{1,0:T(8,128)S(1)}, f32[128,128]{1,0:T(8,128)S(1)}, u32[]{:S(2)}, u32[]{:S(2)}) %collective-permute-start.2) | collective-permute-done | bytes 65568 | tf_op jit(solution)/shard_map/ppermute | solution.py:16
  17.0 1.9 %collective-permute-done.1 = f32[128,128]{1,0:T(8,128)S(1)} collective-permute-done((f32[128,128]{1,0:T(8,128)S(1)}, f32[128,128]{1,0:T(8,128)S(1)}, u32[]{:S(2)}, u32[]{:S(2)}) %collective-permute-start.1) | collective-permute-done | bytes 65568 | tf_op jit(solution)/shard_map/ppermute | solution.py:16
  18.9 2.7 %collective-permute-start.4 = (f32[128,128]{1,0:T(8,128)S(1)}, f32[128,128]{1,0:T(8,128)S(1)}, u32[]{:S(2)}, u32[]{:S(2)}) collective-permute-start(f32[128,128]{1,0:T(8,128)S(1)} %add_add_fusion.1), channel_id=1, source_target_pairs={{0,16},{2,18},{4,20},{6,22},{8,24},{10,26},{12,28},{14,30},{16,0},... | collective-permute-start | bytes 196616 | tf_op jit(solution)/shard_map/ppermute | solution.py:16
  21.6 3.2 %collective-permute-done.4 = f32[128,128]{1,0:T(8,128)S(1)} collective-permute-done((f32[128,128]{1,0:T(8,128)S(1)}, f32[128,128]{1,0:T(8,128)S(1)}, u32[]{:S(2)}, u32[]{:S(2)}) %collective-permute-start.4) | collective-permute-done | bytes 65568 | tf_op jit(solution)/shard_map/ppermute | solution.py:16
  24.7 1.6 %collective-permute-done.5.refs_0_ = f32[128,2048]{1,0:T(8,128)S(1)} collective-permute-done((f32[128,2048]{1,0:T(8,128)}, f32[128,2048]{1,0:T(8,128)S(1)}, u32[]{:S(2)}, u32[]{:S(2)}) %collective-permute-start.5) | collective-permute-done | bytes 1048608 | tf_op jit(solution)/shard_map/ppermute | solution.py:16
  26.3 0.6 %second_other.1 = f32[1,128,128]{2,1,0:T(8,128)S(1)} custom-call(f32[128,2048]{1,0:T(8,128)S(1)} %collective-permute-done.5.refs_0_, bf16[2,256,2048]{2,1,0:T(8,128)(2,1)S(1)} %get-tuple-element.15.refs_1_, f32[128,128]{1,0:T(8,128)S(1)} %add.54.refs_2_), custom_call_target="tpu_custom_call" | custom-call | flops 201326592 | tf_op jit(solution)/shard_map/second_other/pallas_call | solution.py:260
  26.9 0.1 collective-permute-start.6
  27.0 0.6 %second_mine.1 = (f32[1,128,128]{2,1,0:T(8,128)S(1)}, bf16[2,128,2048]{2,1,0:T(8,128)(2,1)S(1)}) custom-call(f32[128,2048]{1,0:T(8,128)S(1)} %collective-permute-done.5.refs_0_, bf16[2,256,2048]{2,1,0:T(8,128)(2,1)S(1)} %get-tuple-element.15.refs_1_, f32[128,128]{1,0:T(8,128)S(1)} %add.54.refs_2_), custom_call_target="tpu_custom_call" | custom-call | flops 201326592 | tf_op jit(solution)/shard_map/second_mine/pallas_call | solution.py:260
  27.6 0.6 %collective-permute-done.6 = f32[1,128,128]{2,1,0:T(8,128)S(1)} collective-permute-done((f32[1,128,128]{2,1,0:T(8,128)S(1)}, f32[1,128,128]{2,1,0:T(8,128)S(1)}, u32[]{:S(2)}, u32[]{:S(2)}) %collective-permute-start.6) | collective-permute-done | bytes 65568 | tf_op jit(solution)/shard_map/ppermute | solution.py:16
  28.3 1.8 %collective-permute-start.9 = (f32[1,128,128]{2,1,0:T(8,128)S(1)}, f32[1,128,128]{2,1,0:T(8,128)S(1)}, u32[]{:S(2)}, u32[]{:S(2)}) collective-permute-start(f32[1,128,128]{2,1,0:T(8,128)S(1)} %add.55), channel_id=1, source_target_pairs={{0,4},{2,6},{4,0},{6,2},{8,12},{10,14},{12,8},{14,10},{16,20},{18,... | collective-permute-start | bytes 196616 | tf_op jit(solution)/shard_map/ppermute | solution.py:16
  30.1 1.6 %collective-permute-start.8 = (f32[1,128,128]{2,1,0:T(8,128)S(1)}, f32[1,128,128]{2,1,0:T(8,128)S(1)}, u32[]{:S(2)}, u32[]{:S(2)}) collective-permute-start(f32[1,128,128]{2,1,0:T(8,128)S(1)} %add.55), channel_id=1, source_target_pairs={{0,8},{2,10},{4,12},{6,14},{8,0},{10,2},{12,4},{14,6},{16,24},{18,... | collective-permute-start | bytes 196616 | tf_op jit(solution)/shard_map/ppermute | solution.py:16
  31.7 0.1 collective-permute-start.7
  31.8 0.8 %collective-permute-done.9 = f32[1,128,128]{2,1,0:T(8,128)S(1)} collective-permute-done((f32[1,128,128]{2,1,0:T(8,128)S(1)}, f32[1,128,128]{2,1,0:T(8,128)S(1)}, u32[]{:S(2)}, u32[]{:S(2)}) %collective-permute-start.9) | collective-permute-done | bytes 65568 | tf_op jit(solution)/shard_map/ppermute | solution.py:16
  32.6 2.3 %collective-permute-done.8 = f32[1,128,128]{2,1,0:T(8,128)S(1)} collective-permute-done((f32[1,128,128]{2,1,0:T(8,128)S(1)}, f32[1,128,128]{2,1,0:T(8,128)S(1)}, u32[]{:S(2)}, u32[]{:S(2)}) %collective-permute-start.8) | collective-permute-done | bytes 65568 | tf_op jit(solution)/shard_map/ppermute | solution.py:16
  34.9 1.9 %collective-permute-done.7 = f32[1,128,128]{2,1,0:T(8,128)S(1)} collective-permute-done((f32[1,128,128]{2,1,0:T(8,128)S(1)}, f32[1,128,128]{2,1,0:T(8,128)S(1)}, u32[]{:S(2)}, u32[]{:S(2)}) %collective-permute-start.7) | collective-permute-done | bytes 65568 | tf_op jit(solution)/shard_map/ppermute | solution.py:16
  36.9 3.6 %collective-permute-start.11 = (f32[1,128,128]{2,1,0:T(8,128)S(1)}, f32[1,128,128]{2,1,0:T(8,128)S(1)}, u32[]{:S(2)}, u32[]{:S(2)}) collective-permute-start(f32[1,128,128]{2,1,0:T(8,128)S(1)} %add_add_fusion), channel_id=1, source_target_pairs={{0,17},{1,16},{2,19},{3,18},{4,21},{5,20},{6,23},{7,22},{8,25},{9,... | collective-permute-start | bytes 196616 | tf_op jit(solution)/shard_map/ppermute | solution.py:27
  40.4 0.5 %collective-permute-start.10 = (f32[1,128,128]{2,1,0:T(8,128)S(1)}, f32[1,128,128]{2,1,0:T(8,128)S(1)}, u32[]{:S(2)}, u32[]{:S(2)}) collective-permute-start(f32[1,128,128]{2,1,0:T(8,128)S(1)} %add_add_fusion), channel_id=1, source_target_pairs={{0,1},{1,0},{2,3},{3,2},{4,5},{5,4},{6,7},{7,6},{8,9},{9,8},{10,11... | collective-permute-start | bytes 196616 | tf_op jit(solution)/shard_map/ppermute | solution.py:16
  41.0 1.5 %collective-permute-start.13 = (f32[128,128]{1,0:T(8,128)S(1)}, f32[128,128]{1,0:T(8,128)S(1)}, u32[]{:S(2)}, u32[]{:S(2)}) collective-permute-start(f32[128,128]{1,0:T(8,128)S(1)} %add.54.refs_2_), channel_id=1, source_target_pairs={{0,1},{1,0},{2,3},{3,2},{4,5},{5,4},{6,7},{7,6},{8,9},{9,8},{10,11... | collective-permute-start | bytes 196616 | tf_op jit(solution)/shard_map/ppermute | solution.py:16
  42.5 0.3 collective-permute-start.12
  42.8 0.8 %collective-permute-done.11 = f32[1,128,128]{2,1,0:T(8,128)S(1)} collective-permute-done((f32[1,128,128]{2,1,0:T(8,128)S(1)}, f32[1,128,128]{2,1,0:T(8,128)S(1)}, u32[]{:S(2)}, u32[]{:S(2)}) %collective-permute-start.11) | collective-permute-done | bytes 65568 | tf_op jit(solution)/shard_map/ppermute | solution.py:27
  43.6 1.1 %collective-permute-done.10 = f32[1,128,128]{2,1,0:T(8,128)S(1)} collective-permute-done((f32[1,128,128]{2,1,0:T(8,128)S(1)}, f32[1,128,128]{2,1,0:T(8,128)S(1)}, u32[]{:S(2)}, u32[]{:S(2)}) %collective-permute-start.10) | collective-permute-done | bytes 65568 | tf_op jit(solution)/shard_map/ppermute | solution.py:16
  44.7 0.7 %collective-permute-done.13 = f32[128,128]{1,0:T(8,128)S(1)} collective-permute-done((f32[128,128]{1,0:T(8,128)S(1)}, f32[128,128]{1,0:T(8,128)S(1)}, u32[]{:S(2)}, u32[]{:S(2)}) %collective-permute-start.13) | collective-permute-done | bytes 65568 | tf_op jit(solution)/shard_map/ppermute | solution.py:16
  45.4 2.8 %collective-permute-done.12 = f32[1,128,128]{2,1,0:T(8,128)S(1)} collective-permute-done((f32[1,128,128]{2,1,0:T(8,128)S(1)}, f32[1,128,128]{2,1,0:T(8,128)S(1)}, u32[]{:S(2)}, u32[]{:S(2)}) %collective-permute-start.12) | collective-permute-done | bytes 65568 | tf_op jit(solution)/shard_map/ppermute | solution.py:16
  48.2 0.1 collective-permute-start.14
  48.3 1.3 %last_mine.1 = (f32[4,256,2048]{2,1,0:T(8,128)}, f32[2,256,1792]{2,1,0:T(8,128)S(1)}) custom-call(f32[2,128,128]{2,1,0:T(8,128)S(1)} %pad_maximum_fusion.refs_0_, bf16[256,192]{1,0:T(8,128)(2,1)S(1)} %get-tuple-element.17.refs_1_, f32[4,256,2048]{2,1,0:T(8,128)S(1)} %get-tuple-element.18.refs_2_, bf16[2,128,2048]{2,1,0:T(8,128)(2,1)S(1)} %get-tuple-element.19.refs_3_, ...), custom_call_target="tpu_custom_call" | custom-call | flops 805306368 | bytes 4194304 | tf_op jit(solution)/shard_map/last_mine/pallas_call | solution.py:292
  49.6 0.0 collective-permute-done.14.refs_0_
  49.7 3.3 %last_other.1 = f32[4,256,2048]{2,1,0:T(8,128)} custom-call(f32[2,128,128]{2,1,0:T(8,128)S(1)} %collective-permute-done.14.refs_0_, bf16[256,192]{1,0:T(8,128)(2,1)S(1)} %get-tuple-element.17.refs_1_, f32[4,256,2048]{2,1,0:T(8,128)S(1)} %get-tuple-element.18.refs_2_, ...), custom_call_target="tpu_custom_call", output_to_operand_aliasing={{}: (6, {})} | custom-call | flops 805306368 | bytes 4194304 | tf_op jit(solution)/shard_map/last_other/pallas_call | solution.py:292
  (9 shorter events, 0.1 us)
Async XLA Ops:
  0.0 26.3 %collective-permute-start.5 = (f32[128,2048]{1,0:T(8,128)}, f32[128,2048]{1,0:T(8,128)S(1)}, u32[]{:S(2)}, u32[]{:S(2)}) collective-permute-start(f32[128,2048]{1,0:T(8,128)} %b_hbm.1), channel_id=1, source_target_pairs={{0,1},{1,0},{2,3},{3,2},{4,5},{5,4},{6,7},{7,6},{8,9},{9,8},{10,11... | collective-permute-start | bytes 3145736 | tf_op jit(solution)/shard_map/ppermute | solution.py:16
  9.2 1.3 %collective-permute-start = (f32[128,128]{1,0:T(8,128)S(1)}, f32[128,128]{1,0:T(8,128)S(1)}, u32[]{:S(2)}, u32[]{:S(2)}) collective-permute-start(f32[128,128]{1,0:T(8,128)S(1)} %slice_select_fusion), channel_id=1, source_target_pairs={{0,2},{2,0},{4,6},{6,4},{8,10},{10,8},{12,14},{14,12},{16,18},{18,... | collective-permute-start | bytes 196616 | tf_op jit(solution)/shard_map/ppermute | solution.py:16
  10.6 4.3 %collective-permute-start.3 = (f32[128,128]{1,0:T(8,128)S(1)}, f32[128,128]{1,0:T(8,128)S(1)}, u32[]{:S(2)}, u32[]{:S(2)}) collective-permute-start(f32[128,128]{1,0:T(8,128)S(1)} %select_add_fusion), channel_id=1, source_target_pairs={{0,4},{2,6},{4,0},{6,2},{8,12},{10,14},{12,8},{14,10},{16,20},{18,... | collective-permute-start | bytes 196616 | tf_op jit(solution)/shard_map/ppermute | solution.py:16
  12.1 4.8 %collective-permute-start.2 = (f32[128,128]{1,0:T(8,128)S(1)}, f32[128,128]{1,0:T(8,128)S(1)}, u32[]{:S(2)}, u32[]{:S(2)}) collective-permute-start(f32[128,128]{1,0:T(8,128)S(1)} %select_add_fusion), channel_id=1, source_target_pairs={{0,8},{2,10},{4,12},{6,14},{8,0},{10,2},{12,4},{14,6},{16,24},{18,... | collective-permute-start | bytes 196616 | tf_op jit(solution)/shard_map/ppermute | solution.py:16
  13.7 5.2 %collective-permute-start.1 = (f32[128,128]{1,0:T(8,128)S(1)}, f32[128,128]{1,0:T(8,128)S(1)}, u32[]{:S(2)}, u32[]{:S(2)}) collective-permute-start(f32[128,128]{1,0:T(8,128)S(1)} %select_add_fusion), channel_id=1, source_target_pairs={{0,12},{2,14},{4,8},{6,10},{8,4},{10,6},{12,0},{14,2},{16,28},{18,... | collective-permute-start | bytes 196616 | tf_op jit(solution)/shard_map/ppermute | solution.py:16
  18.9 5.8 %collective-permute-start.4 = (f32[128,128]{1,0:T(8,128)S(1)}, f32[128,128]{1,0:T(8,128)S(1)}, u32[]{:S(2)}, u32[]{:S(2)}) collective-permute-start(f32[128,128]{1,0:T(8,128)S(1)} %add_add_fusion.1), channel_id=1, source_target_pairs={{0,16},{2,18},{4,20},{6,22},{8,24},{10,26},{12,28},{14,30},{16,0},... | collective-permute-start | bytes 196616 | tf_op jit(solution)/shard_map/ppermute | solution.py:16
  26.9 1.3 %collective-permute-start.6 = (f32[1,128,128]{2,1,0:T(8,128)S(1)}, f32[1,128,128]{2,1,0:T(8,128)S(1)}, u32[]{:S(2)}, u32[]{:S(2)}) collective-permute-start(f32[1,128,128]{2,1,0:T(8,128)S(1)} %second_other.1), channel_id=1, source_target_pairs={{0,2},{2,0},{4,6},{6,4},{8,10},{10,8},{12,14},{14,12},{16,18},{18,... | collective-permute-start | bytes 196616 | tf_op jit(solution)/shard_map/ppermute | solution.py:16
  28.3 4.3 %collective-permute-start.9 = (f32[1,128,128]{2,1,0:T(8,128)S(1)}, f32[1,128,128]{2,1,0:T(8,128)S(1)}, u32[]{:S(2)}, u32[]{:S(2)}) collective-permute-start(f32[1,128,128]{2,1,0:T(8,128)S(1)} %add.55), channel_id=1, source_target_pairs={{0,4},{2,6},{4,0},{6,2},{8,12},{10,14},{12,8},{14,10},{16,20},{18,... | collective-permute-start | bytes 196616 | tf_op jit(solution)/shard_map/ppermute | solution.py:16
  30.1 4.8 %collective-permute-start.8 = (f32[1,128,128]{2,1,0:T(8,128)S(1)}, f32[1,128,128]{2,1,0:T(8,128)S(1)}, u32[]{:S(2)}, u32[]{:S(2)}) collective-permute-start(f32[1,128,128]{2,1,0:T(8,128)S(1)} %add.55), channel_id=1, source_target_pairs={{0,8},{2,10},{4,12},{6,14},{8,0},{10,2},{12,4},{14,6},{16,24},{18,... | collective-permute-start | bytes 196616 | tf_op jit(solution)/shard_map/ppermute | solution.py:16
  31.7 5.2 %collective-permute-start.7 = (f32[1,128,128]{2,1,0:T(8,128)S(1)}, f32[1,128,128]{2,1,0:T(8,128)S(1)}, u32[]{:S(2)}, u32[]{:S(2)}) collective-permute-start(f32[1,128,128]{2,1,0:T(8,128)S(1)} %add.55), channel_id=1, source_target_pairs={{0,12},{2,14},{4,8},{6,10},{8,4},{10,6},{12,0},{14,2},{16,28},{18,... | collective-permute-start | bytes 196616 | tf_op jit(solution)/shard_map/ppermute | solution.py:16
  36.9 6.7 %collective-permute-start.11 = (f32[1,128,128]{2,1,0:T(8,128)S(1)}, f32[1,128,128]{2,1,0:T(8,128)S(1)}, u32[]{:S(2)}, u32[]{:S(2)}) collective-permute-start(f32[1,128,128]{2,1,0:T(8,128)S(1)} %add_add_fusion), channel_id=1, source_target_pairs={{0,17},{1,16},{2,19},{3,18},{4,21},{5,20},{6,23},{7,22},{8,25},{9,... | collective-permute-start | bytes 196616 | tf_op jit(solution)/shard_map/ppermute | solution.py:27
  40.4 4.3 %collective-permute-start.10 = (f32[1,128,128]{2,1,0:T(8,128)S(1)}, f32[1,128,128]{2,1,0:T(8,128)S(1)}, u32[]{:S(2)}, u32[]{:S(2)}) collective-permute-start(f32[1,128,128]{2,1,0:T(8,128)S(1)} %add_add_fusion), channel_id=1, source_target_pairs={{0,1},{1,0},{2,3},{3,2},{4,5},{5,4},{6,7},{7,6},{8,9},{9,8},{10,11... | collective-permute-start | bytes 196616 | tf_op jit(solution)/shard_map/ppermute | solution.py:16
  41.0 4.4 %collective-permute-start.13 = (f32[128,128]{1,0:T(8,128)S(1)}, f32[128,128]{1,0:T(8,128)S(1)}, u32[]{:S(2)}, u32[]{:S(2)}) collective-permute-start(f32[128,128]{1,0:T(8,128)S(1)} %add.54.refs_2_), channel_id=1, source_target_pairs={{0,1},{1,0},{2,3},{3,2},{4,5},{5,4},{6,7},{7,6},{8,9},{9,8},{10,11... | collective-permute-start | bytes 196616 | tf_op jit(solution)/shard_map/ppermute | solution.py:16
  42.5 5.8 %collective-permute-start.12 = (f32[1,128,128]{2,1,0:T(8,128)S(1)}, f32[1,128,128]{2,1,0:T(8,128)S(1)}, u32[]{:S(2)}, u32[]{:S(2)}) collective-permute-start(f32[1,128,128]{2,1,0:T(8,128)S(1)} %add_add_fusion), channel_id=1, source_target_pairs={{0,16},{2,18},{4,20},{6,22},{8,24},{10,26},{12,28},{14,30},{16,0},... | collective-permute-start | bytes 196616 | tf_op jit(solution)/shard_map/ppermute | solution.py:16
  48.2 1.4 %collective-permute-start.14 = (f32[2,128,128]{2,1,0:T(8,128)S(1)}, f32[2,128,128]{2,1,0:T(8,128)S(1)}, u32[]{:S(2)}, u32[]{:S(2)}) collective-permute-start(f32[2,128,128]{2,1,0:T(8,128)S(1)} %pad_maximum_fusion.refs_0_), channel_id=1, source_target_pairs={{0,2},{2,0},{4,6},{6,4},{8,10},{10,8},{12,14},{14,12},{16,18},{18,... | collective-permute-start | bytes 393224 | tf_op jit(solution)/shard_map/ppermute | solution.py:16
